TPU v7x, 32 devices: a whole 2x2x4 slice. The times are simulated.
32 devices in a mesh: seq: 8 (over y, x, core), head: 4 (over z).
Axes of the slice: x: 2, y: 2, z: 4, core: 2. Of those that a mesh axis runs over, the one named last changes fastest.
Arguments:
- hidden: bfloat16 [8192, 1536], P('seq'), may hold values from -6 to 6
- in_gain: bfloat16 [1536], replicated, may hold values from 0.5 to 1.5
- proj_gate: bfloat16 [1536, 3072], P(None, 'head'), may hold values from -0.15625 to 0.15625
- proj_input: bfloat16 [1536, 3072], P(None, 'head'), may hold values from -0.15625 to 0.15625
- proj_states: bfloat16 [1536, 256], P('head'), may hold values from -0.15625 to 0.15625
- proj_step: bfloat16 [1536, 48], P(None, 'head'), may hold values from -0.15625 to 0.15625
- conv_input: bfloat16 [4, 3072], P(None, 'head'), may hold values from -3 to 3
- conv_input_bias: bfloat16 [3072], P('head'), may hold values from -3 to 3
- conv_states: bfloat16 [4, 256], replicated, may hold values from -3 to 3
- conv_states_bias: bfloat16 [256], replicated, may hold values from -3 to 3
- step_bias: float32 [48], P('head'), may hold values from -4.5 to -3.5
- decay_log: float32 [48], P('head'), may hold values from -6.3 to 1.4, as said below
- skip_gain: float32 [48], P('head'), may hold values from 0.5 to 1.5
- gate_gain: bfloat16 [3072], P('head'), may hold values from 0.5 to 1.5
- proj_output: bfloat16 [3072, 1536], P('head'), may hold values from -0.109375 to 0.109375
- cotangent: bfloat16 [8192, 1536], P('seq'), may hold values from -6 to 6
Outputs:
- result: float32 [8192, 1536], P('seq')
- grad_hidden: float32 [8192, 1536], P('seq')
- grad_in_gain: float32 [1536], replicated
- grad_proj_gate: float32 [1536, 3072], P('seq', 'head')
- grad_proj_input: float32 [1536, 3072], P('seq', 'head')
- grad_proj_states: float32 [1536, 256], P('head', 'seq')
- grad_proj_step: float32 [1536, 48], P('seq', 'head')
- grad_conv_input: float32 [4, 3072], P(None, 'head')
- grad_conv_input_bias: float32 [3072], P('head')
- grad_conv_states: float32 [4, 256], replicated
- grad_conv_states_bias: float32 [256], replicated
- grad_step_bias: float32 [48], P('head')
- grad_decay_log: float32 [48], P('head')
- grad_skip_gain: float32 [48], P('head')
- grad_gate_gain: float32 [3072], P('head')
- grad_proj_output: float32 [3072, 1536], P('head', 'seq')
Inputs may be any that keep to these rules, and one draw needn't show every extreme that they name: `decay_log`: one value a head.
All inputs are finite; a program needn't handle non-finite values.
Results may differ from a plain program's by a relative error of at most 0.00185.
The roundings to bfloat16 on the way count: a program that leaves them out, or rounds other values in their place, can miss the bound.
Values may be sent and summed in bfloat16 or wider, within the bound.
A program may use at most 128 MiB of HBM per device.

v0:
```python
import jax
import jax.numpy as jnp
from jax import lax
from jax.sharding import PartitionSpec as P

DI = 3072
BLOCK = 256
SEQS = 1


EPS = 1e-05
HIGH = lax.Precision.HIGHEST


def shifted(block, axis, distance):
    devices = range(lax.axis_size(axis))
    route = [(i - distance, i) for i in devices if i - distance in devices]
    return lax.ppermute(block, axis, route)


def entering(shard, axis, combine, identity, reverse):
    size, mine = (lax.axis_size(axis), lax.axis_index(axis))
    everything = jax.tree.map(lambda part: lax.all_gather(part, axis), shard)
    start = jax.tree.map(
        lambda part, zero: jnp.broadcast_to(jnp.asarray(zero, part.dtype), part.shape),
        shard,
        identity,
    )

    def lap(k, before):
        at = size - 1 - k if reverse else k
        reached = at > mine if reverse else at < mine
        new = combine(before, jax.tree.map(lambda part: part[at], everything))
        return jax.tree.map(lambda a, b: jnp.where(reached, a, b), new, before)

    return lax.fori_loop(0, size, lap, start)


def matmul_low(left, right):
    return jnp.dot(left, right, preferred_element_type=jnp.float32)


def times_transposed(left, right):
    return lax.dot_general(
        left, right, (((1,), (1,)), ((), ())), preferred_element_type=jnp.float32
    )


def transposed_times(left, right):
    return lax.dot_general(
        left, right, (((0,), (0,)), ((), ())), preferred_element_type=jnp.float32
    )


def conv_valid(extended, kernel, bias):
    width = kernel.shape[0]
    count = extended.shape[0] - width + 1
    summed = bias[None, :] + jnp.zeros((count, extended.shape[1]), jnp.float32)
    for offset in range(width):
        summed = summed + kernel[offset][None, :] * extended[offset : offset + count]
    return jax.nn.silu(summed)


def ssd_block(carry_state, block_x, block_step, block_b, block_c, decay_rate):
    length = block_x.shape[0]
    log_sums = jnp.cumsum(block_step * decay_rate[None, :], axis=0)
    row_ids = lax.broadcasted_iota(jnp.int32, (length, length), 0)
    col_ids = lax.broadcasted_iota(jnp.int32, (length, length), 1)
    causal = (row_ids >= col_ids)[None, :, :]
    log_gaps = log_sums.T[:, :, None] - log_sums.T[:, None, :]
    weights = jnp.where(causal, jnp.exp(jnp.where(causal, log_gaps, 0.0)), 0.0)
    scores = jnp.einsum("tn,sn->ts", block_c, block_b, precision=HIGH)
    mixing = scores[None, :, :] * weights * block_step.T[:, None, :]
    intra_out = jnp.einsum("hts,shp->thp", mixing, block_x, precision=HIGH)
    carried = jnp.exp(log_sums)[:, :, None] * jnp.einsum(
        "tn,hpn->thp", block_c, carry_state, precision=HIGH
    )
    to_end = jnp.exp(log_sums[-1][None, :] - log_sums) * block_step
    new_state = jnp.exp(log_sums[-1])[:, None, None] * carry_state + jnp.einsum(
        "sh,shp,sn->hpn", to_end, block_x, block_b, precision=HIGH
    )
    return (new_state, intra_out + carried, log_sums)


def ssd_device(input_conv, step_pre, step_bias, decay_log, skip_gain, bmat, cmat):
    tokens = input_conv.shape[0]
    heads = step_pre.shape[1]
    head_dim = input_conv.shape[1] // heads
    state_size = bmat.shape[1]
    block_count = tokens // BLOCK
    step_size = jax.nn.softplus(step_pre + step_bias[None, :])
    decay_rate = -jnp.exp(decay_log)
    input_heads = input_conv.reshape(tokens, heads, head_dim)

    def advance(carry, pieces):
        new_state, block_out, log_sums = ssd_block(
            carry[0], pieces[0], pieces[1], pieces[2], pieces[3], decay_rate
        )
        return (
            (new_state, carry[1] + log_sums[-1]),
            (block_out, jnp.exp(log_sums + carry[1][None, :])),
        )

    start_carry = (
        jnp.zeros((heads, head_dim, state_size), jnp.float32),
        jnp.zeros((heads,), jnp.float32),
    )
    pieces = (
        input_heads.reshape(block_count, BLOCK, heads, head_dim),
        step_size.reshape(block_count, BLOCK, heads),
        bmat.reshape(block_count, BLOCK, state_size),
        cmat.reshape(block_count, BLOCK, state_size),
    )
    (final_state, total_log), (block_out, decay_tok) = lax.scan(
        jax.checkpoint(advance), start_carry, pieces
    )
    local_out = block_out.reshape(tokens, heads, head_dim) + skip_gain[None, :, None] * input_heads
    return (local_out, jnp.exp(total_log), final_state, decay_tok.reshape(tokens, heads))


def ssd_full(input_conv, step_pre, step_bias, decay_log, skip_gain, states_conv, incoming):
    state_size = incoming.shape[2]
    cmat = states_conv[:, state_size:]
    local_out, dev_decay, dev_state, decay_tok = ssd_device(
        input_conv, step_pre, step_bias, decay_log, skip_gain, states_conv[:, :state_size], cmat
    )
    joined = local_out + decay_tok[:, :, None] * jnp.einsum(
        "tn,hpn->thp", cmat, incoming, precision=HIGH
    )
    return (joined.reshape(joined.shape[0], -1), dev_decay, dev_state)


def on_device(
    hidden,
    in_gain,
    proj_gate,
    proj_input,
    proj_states,
    proj_step,
    conv_input,
    conv_input_bias,
    conv_states,
    conv_states_bias,
    step_bias,
    decay_log,
    skip_gain,
    gate_gain,
    proj_output,
    cotangent,
):
    seg_count = lax.axis_size("seq") // SEQS
    seg_index = lax.axis_index("seq") % seg_count
    is_first = seg_index == 0
    is_last = seg_index == seg_count - 1
    tokens = hidden.shape[0]
    width = hidden.shape[1]
    row_width = proj_states.shape[0]
    heads = proj_step.shape[1]
    inner = proj_gate.shape[1]
    state_size = conv_states.shape[1] // 2
    head_dim = inner // heads
    edge = conv_input.shape[0] - 1
    row_start = lax.axis_index("head") * row_width
    resid = hidden.astype(jnp.float32)
    gain_full = in_gain.astype(jnp.float32)
    inv_rms = lax.rsqrt(jnp.mean(resid * resid, axis=-1, keepdims=True) + EPS)
    normed = (resid * inv_rms * gain_full[None, :]).astype(jnp.bfloat16)
    gate_pre = matmul_low(normed, proj_gate)
    input_pre = matmul_low(normed, proj_input)
    step_pre = matmul_low(normed, proj_step)
    normed_rows = lax.dynamic_slice_in_dim(normed, row_start, row_width, 1)
    states_pre = lax.psum(matmul_low(normed_rows, proj_states), "head")
    keep_first = jnp.where(is_first, 0.0, 1.0)
    halo_input, halo_states = shifted(
        (input_pre[tokens - edge :], states_pre[tokens - edge :]), "seq", 1
    )
    input_ext = jnp.concatenate([halo_input * keep_first, input_pre], axis=0)
    states_ext = jnp.concatenate([halo_states * keep_first, states_pre], axis=0)
    kernel_input = conv_input.astype(jnp.float32)
    bias_input = conv_input_bias.astype(jnp.float32)
    kernel_states = conv_states.astype(jnp.float32)
    bias_states = conv_states_bias.astype(jnp.float32)
    input_conv = conv_valid(input_ext, kernel_input, bias_input)
    states_conv = conv_valid(states_ext, kernel_states, bias_states)
    cmat = states_conv[:, state_size:]
    local_out, dev_decay, dev_state, decay_tok = ssd_device(
        input_conv, step_pre, step_bias, decay_log, skip_gain, states_conv[:, :state_size], cmat
    )
    send_decay = jnp.where(is_last, 0.0, dev_decay)
    send_state = jnp.where(is_last, 0.0, dev_state)
    identity = (jnp.ones((heads,), jnp.float32), jnp.zeros_like(dev_state))

    def compose(earlier, later):
        return (earlier[0] * later[0], earlier[1] * later[0][:, None, None] + later[1])

    prefix_decay, incoming = entering((send_decay, send_state), "seq", compose, identity, False)
    joined = local_out + decay_tok[:, :, None] * jnp.einsum(
        "tn,hpn->thp", cmat, incoming, precision=HIGH
    )
    ssd_out = joined.reshape(tokens, inner)
    gate_silu = jax.nn.silu(gate_pre)
    gated = ssd_out * gate_silu
    square_sum = lax.psum(jnp.sum(gated * gated, axis=-1), "head")
    gate_inv = lax.rsqrt(square_sum / DI + EPS)[:, None]
    gain_gate = gate_gain.astype(jnp.float32)
    ynorm = (gated * gate_inv * gain_gate[None, :]).astype(jnp.bfloat16)
    branch = lax.psum(matmul_low(ynorm, proj_output), "head")
    result = resid + branch
    grad_ynorm = times_transposed(cotangent, proj_output)
    local_proj_output = transposed_times(ynorm, cotangent)
    local_gate_gain = jnp.sum(grad_ynorm * gated * gate_inv, axis=0)
    scaled = grad_ynorm * gain_gate[None, :]
    cross = lax.psum(jnp.sum(scaled * gated, axis=-1), "head")
    grad_gated = gate_inv * scaled - gated * gate_inv**3 * cross[:, None] / DI
    grad_ssd = grad_gated * gate_silu
    sigmoid_gate = jax.nn.sigmoid(gate_pre)
    grad_gate_pre = (
        grad_gated * ssd_out * sigmoid_gate * (1.0 + gate_pre * (1.0 - sigmoid_gate))
    ).astype(jnp.bfloat16)
    grad_heads = grad_ssd.reshape(tokens, heads, head_dim)
    direct_grad = jnp.einsum("th,thp,tn->hpn", decay_tok, grad_heads, cmat, precision=HIGH)
    back_decay = jnp.where(is_first, 0.0, dev_decay)
    back_grad = jnp.where(is_first, 0.0, direct_grad)

    def compose_back(earlier, later):
        return (earlier[0] * later[0], later[1] + later[0][:, None, None] * earlier[1])

    later_decay, later_grad = entering((back_decay, back_grad), "seq", compose_back, identity, True)
    grad_dev_decay = jnp.sum(later_grad * incoming, axis=(1, 2))
    ssd_value, ssd_pull = jax.vjp(
        ssd_full, input_conv, step_pre, step_bias, decay_log, skip_gain, states_conv, incoming
    )
    (
        grad_input_conv,
        grad_step_pre,
        grad_step_bias,
        grad_decay_log,
        grad_skip_gain,
        partial_states,
        unused_incoming,
    ) = ssd_pull((grad_ssd, grad_dev_decay, later_grad))
    grad_states_conv = lax.psum(partial_states, "head")
    conv_value, pull_input = jax.vjp(conv_valid, input_ext, kernel_input, bias_input)
    grad_input_ext, grad_conv_input, grad_conv_input_bias = pull_input(grad_input_conv)
    conv_value, pull_states = jax.vjp(conv_valid, states_ext, kernel_states, bias_states)
    grad_states_ext, grad_conv_states, grad_conv_states_bias = pull_states(grad_states_conv)
    back_input, back_states = shifted((grad_input_ext[:edge], grad_states_ext[:edge]), "seq", -1)
    keep_last = jnp.where(is_last, 0.0, 1.0)
    grad_input_b = jnp.concatenate(
        [grad_input_ext[edge:tokens], grad_input_ext[tokens:] + back_input * keep_last], axis=0
    ).astype(jnp.bfloat16)
    grad_states_b = jnp.concatenate(
        [grad_states_ext[edge:tokens], grad_states_ext[tokens:] + back_states * keep_last], axis=0
    ).astype(jnp.bfloat16)
    grad_step_b = grad_step_pre.astype(jnp.bfloat16)
    grad_normed = (
        times_transposed(grad_gate_pre, proj_gate)
        + times_transposed(grad_input_b, proj_input)
        + times_transposed(grad_step_b, proj_step)
    )
    grad_rows = times_transposed(grad_states_b, proj_states)
    grad_normed = lax.dynamic_update_slice_in_dim(
        grad_normed,
        lax.dynamic_slice_in_dim(grad_normed, row_start, row_width, 1) + grad_rows,
        row_start,
        1,
    )
    grad_normed = lax.psum(grad_normed, "head")
    local_in_gain = jnp.sum(grad_normed * resid * inv_rms, axis=0)
    weighted = grad_normed * gain_full[None, :]
    grad_hidden = (
        cotangent.astype(jnp.float32)
        + inv_rms * weighted
        - resid * inv_rms**3 * jnp.sum(weighted * resid, axis=-1, keepdims=True) / width
    )
    grad_proj_gate, grad_proj_input, grad_proj_step = (
        lax.psum_scatter(
            transposed_times(normed, grad_gate_pre), "seq", scatter_dimension=0, tiled=True
        ),
        lax.psum_scatter(
            transposed_times(normed, grad_input_b), "seq", scatter_dimension=0, tiled=True
        ),
        lax.psum_scatter(
            transposed_times(normed, grad_step_b), "seq", scatter_dimension=0, tiled=True
        ),
    )
    grad_proj_output, grad_proj_states = (
        lax.psum_scatter(local_proj_output, "seq", scatter_dimension=1, tiled=True),
        lax.psum_scatter(
            transposed_times(normed_rows, grad_states_b), "seq", scatter_dimension=1, tiled=True
        ),
    )
    (
        grad_in_gain,
        grad_conv_input,
        grad_conv_input_bias,
        grad_conv_states,
        grad_conv_states_bias,
        grad_step_bias,
        grad_decay_log,
        grad_skip_gain,
        grad_gate_gain,
    ) = lax.psum(
        (
            local_in_gain,
            grad_conv_input,
            grad_conv_input_bias,
            grad_conv_states,
            grad_conv_states_bias,
            grad_step_bias,
            grad_decay_log,
            grad_skip_gain,
            local_gate_gain,
        ),
        "seq",
    )
    return (
        result,
        grad_hidden,
        grad_in_gain,
        grad_proj_gate,
        grad_proj_input,
        grad_proj_states,
        grad_proj_step,
        grad_conv_input,
        grad_conv_input_bias,
        grad_conv_states,
        grad_conv_states_bias,
        grad_step_bias,
        grad_decay_log,
        grad_skip_gain,
        grad_gate_gain,
        grad_proj_output,
    )


def solution(mesh):
    in_specs = (
        P("seq", None),
        P(),
        P(None, "head"),
        P(None, "head"),
        P("head", None),
        P(None, "head"),
        P(None, "head"),
        P("head"),
        P(),
        P(),
        P("head"),
        P("head"),
        P("head"),
        P("head"),
        P("head", None),
        P("seq", None),
    )
    out_specs = (
        P("seq", None),
        P("seq", None),
        P(),
        P("seq", "head"),
        P("seq", "head"),
        P("head", "seq"),
        P("seq", "head"),
        P(None, "head"),
        P("head"),
        P(),
        P(),
        P("head"),
        P("head"),
        P("head"),
        P("head"),
        P("head", "seq"),
    )
    return jax.shard_map(
        on_device, mesh=mesh, in_specs=in_specs, out_specs=out_specs, check_vma=False
    )
```

profile of v0, /device:TPU:0, one launch (start us, length us, event | category | flops | bytes accessed | tf_op | source)
XLA Modules:
  0.0 1433.5 jit_solution(3858136629010609230)
XLA Ops:
  16.6 5.4 fusion.177
  27.6 43.6 %all-reduce.30.cloned.1.call-done = f32[1024,256]{1,0:T(8,128)} async-done(((f32[1024,256]{1,0:T(8,128)}), f32[1024,256]{1,0:T(8,128)}) %all-reduce.30.cloned.1.call-update) | async-done | bytes 1048592 | tf_op jit(solution)/shard_map/psum | solution.py:172
  74.3 8.3 fusion.117
  82.6 3.5 copy.165
  86.1 5.1 reshape_reshape.3
  91.3 4.2 copy.167
  102.1 139.4 %while.93 = (s32[]{:T(128)}, f32[12,64,128]{2,1,0:T(8,128)S(1)}, f32[12]{0:T(128)}, f32[4,256,12,64]{1,0,3,2:T(4,128)}, f32[4,256,12]{1,0,2:T(4,128)}, /*index=5...) while((s32[]{:T(128)}, f32[12,64,128]{2,1,0:T(8,128)S(1)}, ...), condition=%wide.region_5.6_spmd.clone, body=%wide.region_2.5_spmd.clone.sunk | while | flops 1314009088 | bytes 9859188 | solution.py:114
  108.9 5.0 fusion.271
  118.6 17.9 %dynamic_update_slice.82 = f32[4,256,12,64]{1,0,3,2:T(4,128)} dynamic-update-slice(f32[4,256,12,64]{1,0,3,2:T(4,128)} %get-tuple-element.1649, f32[1,256,12,64]{1,0,3,2:T(1,128)S(1)} %copy.279, s32[]{:T(128)S(6)} %copy.313, s32[]{:T(128)} %constant.220.clone.1..sunk, s32[]{:T(128)} %constant.220.clone.1..sunk, s32[]{:T(128)} %constant.220.clone.1..sunk) | dynamic-update-slice | bytes 1572868 | tf_op jit(solution)/shard_map/while/body/jit(dynamic_update_index_in_dim)/dynamic_update_slice | solution.py:114
  143.9 5.0 fusion.271
  153.6 17.9 %dynamic_update_slice.82 = f32[4,256,12,64]{1,0,3,2:T(4,128)} dynamic-update-slice(f32[4,256,12,64]{1,0,3,2:T(4,128)} %get-tuple-element.1649, f32[1,256,12,64]{1,0,3,2:T(1,128)S(1)} %copy.279, s32[]{:T(128)S(6)} %copy.313, s32[]{:T(128)} %constant.220.clone.1..sunk, s32[]{:T(128)} %constant.220.clone.1..sunk, s32[]{:T(128)} %constant.220.clone.1..sunk) | dynamic-update-slice | bytes 1572868 | tf_op jit(solution)/shard_map/while/body/jit(dynamic_update_index_in_dim)/dynamic_update_slice | solution.py:114
  178.9 5.0 fusion.271
  188.6 17.9 %dynamic_update_slice.82 = f32[4,256,12,64]{1,0,3,2:T(4,128)} dynamic-update-slice(f32[4,256,12,64]{1,0,3,2:T(4,128)} %get-tuple-element.1649, f32[1,256,12,64]{1,0,3,2:T(1,128)S(1)} %copy.279, s32[]{:T(128)S(6)} %copy.313, s32[]{:T(128)} %constant.220.clone.1..sunk, s32[]{:T(128)} %constant.220.clone.1..sunk, s32[]{:T(128)} %constant.220.clone.1..sunk) | dynamic-update-slice | bytes 1572868 | tf_op jit(solution)/shard_map/while/body/jit(dynamic_update_index_in_dim)/dynamic_update_slice | solution.py:114
  213.9 5.0 fusion.271
  223.6 17.9 %dynamic_update_slice.82 = f32[4,256,12,64]{1,0,3,2:T(4,128)} dynamic-update-slice(f32[4,256,12,64]{1,0,3,2:T(4,128)} %get-tuple-element.1649, f32[1,256,12,64]{1,0,3,2:T(1,128)S(1)} %copy.279, s32[]{:T(128)S(6)} %copy.313, s32[]{:T(128)} %constant.220.clone.1..sunk, s32[]{:T(128)} %constant.220.clone.1..sunk, s32[]{:T(128)} %constant.220.clone.1..sunk) | dynamic-update-slice | bytes 1572868 | tf_op jit(solution)/shard_map/while/body/jit(dynamic_update_index_in_dim)/dynamic_update_slice | solution.py:114
  248.4 14.1 all-reduce.24
  264.7 5.2 reshape.393
  269.9 4.4 all-gather.7.cloned.1.call-done
  274.3 9.2 while.94
  283.6 3.9 fusion.143
  287.5 5.9 multiply_add_fusion
  293.4 3.5 copy.171
  296.9 8.4 multiply_reduce_fusion.12
  305.3 11.7 psum.106
  317.0 8.6 multiply_reduce_fusion.4
  325.6 8.9 psum.108
  334.5 9.2 multiply_reduce_fusion.5
  343.7 3.6 copy.173
  347.3 5.4 fusion.127
  353.3 62.0 %while.96 = (s32[]{:T(128)}, f32[12,64,128]{2,1,0:T(8,128)S(1)}, f32[12]{0:T(128)}, f32[4,256,12]{1,0,2:T(4,128)}, f32[4,12,64,128]{3,2,1,0:T(8,128)}, /*index=5...) while((s32[]{:T(128)}, f32[12,64,128]{2,1,0:T(8,128)S(1)}, ...), condition=%wide.region_19.20_spmd.clone, body=%wide.region_16.19_spmd.clone.sunk | while | flops 302985280 | bytes 2817692 | solution.py:114
  416.8 5.2 reshape.397
  422.0 3.6 multiply_reduce_fusion.10
  426.3 6.1 fusion.178
  432.4 4.7 fusion.165
  437.1 14.5 %while.95 = (s32[]{:T(128)}, f32[12,64,128]{2,1,0:T(8,128)S(1)}, s32[]{:T(128)}, f32[8,12,64,128]{3,2,1,0:T(8,128)}, f32[8,12]{1,0:T(8,128)}, /*index=5*/s32[]{:T(128)}, s32[]{:T(128)}, s32[]{:T(128)}, s32[]{:T(128)}) while((s32[]{:T(128)}, f32[12,64,128]{2,1,0:T(8,128)S(1)}, s32[]{:T(128)}, f32[8,12,64,128]{3,2,1,0:T(8,128)}, ...), condition=%wide.region_14.15_spmd.clone, body=%wide.region_13.14_spmd.clone.sunk | while | flops 393224 | bytes 1179967 | solution.py:36
  457.0 234.2 %while.97 = (s32[]{:T(128)}, f32[12]{0:T(128)}, f32[12,64,128]{2,1,0:T(8,128)S(1)}, f32[12]{0:T(128)}, f32[4,256,12,64]{1,0,3,2:T(4,128)}, /*index=5*/f32[4,256,...) while((s32[]{:T(128)}, f32[12]{0:T(128)}, ...), condition=%wide.region_35.36_spmd.clone, body=%wide.region_21.35_spmd.clone.sunk | while | flops 3038722048 | bytes 25370376 | solution.py:114
  471.2 5.6 fusion.298
  479.8 2.9 fusion.304
  497.3 17.8 %dynamic_update_slice.89 = f32[4,256,12,64]{1,0,3,2:T(4,128)} dynamic-update-slice(f32[4,256,12,64]{1,0,3,2:T(4,128)} %get-tuple-element.1784, f32[1,256,12,64]{1,0,3,2:T(1,128)S(1)} %copy.296, s32[]{:T(128)S(6)} %sub.296, s32[]{:T(128)} %constant.220.clone.1..sunk.4, s32[]{:T(128)} %constant.220.clone.1..sunk.4, s32[]{:T(128)} %constant.220.clone.1..sunk.4) | dynamic-update-slice | bytes 1572868 | tf_op jit(solution)/shard_map/transpose(jvp())/while/body/jit(dynamic_update_index_in_dim)/dynamic_update_slice | solution.py:114
  529.2 5.6 fusion.298
  555.8 17.8 %dynamic_update_slice.89 = f32[4,256,12,64]{1,0,3,2:T(4,128)} dynamic-update-slice(f32[4,256,12,64]{1,0,3,2:T(4,128)} %get-tuple-element.1784, f32[1,256,12,64]{1,0,3,2:T(1,128)S(1)} %copy.296, s32[]{:T(128)S(6)} %sub.296, s32[]{:T(128)} %constant.220.clone.1..sunk.4, s32[]{:T(128)} %constant.220.clone.1..sunk.4, s32[]{:T(128)} %constant.220.clone.1..sunk.4) | dynamic-update-slice | bytes 1572868 | tf_op jit(solution)/shard_map/transpose(jvp())/while/body/jit(dynamic_update_index_in_dim)/dynamic_update_slice | solution.py:114
  587.7 5.6 fusion.298
  614.4 17.8 %dynamic_update_slice.89 = f32[4,256,12,64]{1,0,3,2:T(4,128)} dynamic-update-slice(f32[4,256,12,64]{1,0,3,2:T(4,128)} %get-tuple-element.1784, f32[1,256,12,64]{1,0,3,2:T(1,128)S(1)} %copy.296, s32[]{:T(128)S(6)} %sub.296, s32[]{:T(128)} %constant.220.clone.1..sunk.4, s32[]{:T(128)} %constant.220.clone.1..sunk.4, s32[]{:T(128)} %constant.220.clone.1..sunk.4) | dynamic-update-slice | bytes 1572868 | tf_op jit(solution)/shard_map/transpose(jvp())/while/body/jit(dynamic_update_index_in_dim)/dynamic_update_slice | solution.py:114
  646.3 5.6 fusion.298
  672.9 17.8 %dynamic_update_slice.89 = f32[4,256,12,64]{1,0,3,2:T(4,128)} dynamic-update-slice(f32[4,256,12,64]{1,0,3,2:T(4,128)} %get-tuple-element.1784, f32[1,256,12,64]{1,0,3,2:T(1,128)S(1)} %copy.296, s32[]{:T(128)S(6)} %sub.296, s32[]{:T(128)} %constant.220.clone.1..sunk.4, s32[]{:T(128)} %constant.220.clone.1..sunk.4, s32[]{:T(128)} %constant.220.clone.1..sunk.4) | dynamic-update-slice | bytes 1572868 | tf_op jit(solution)/shard_map/transpose(jvp())/while/body/jit(dynamic_update_index_in_dim)/dynamic_update_slice | solution.py:114
  691.2 7.1 fusion.124
  699.5 4.3 copy.249
  703.8 3.5 copy.182
  707.3 9.1 multiply_reduce_fusion.8
  726.1 5.8 pad_add_fusion
  738.4 3.7 add_add_fusion
  742.2 8.0 all-reduce.32.cloned.1.call-done
  755.7 3.0 add_dynamic-update-slice_fusion
  760.2 6.7 fusion.179
  767.7 7.8 fusion.164
  778.3 6.7 fusion.135
  789.0 427.6 %all-reduce.34.cloned.1.call-done = (f32[1024,1536]{1,0:T(8,128)}, f32[1024,1536]{1,0:T(8,128)}) async-done(((f32[1024,1536]{1,0:T(8,128)}, f32[1024,1536]{1,0:T(8,128)}), (f32[1024,1536]{1,0:T(8,128)}, f32[1024,1536]{1,0:T(8,128)})) %all-reduce.34.cloned.1.call-update) | async-done | bytes 12582928 | tf_op jit(solution)/shard_map/psum | solution.py:207
  1216.6 4.8 fusion.107
  1221.5 24.9 %all-reduce.23 = (f32[1536]{0:T(1024)}, f32[4,768]{1,0:T(4,128)}, f32[768]{0:T(1024)}, f32[4,256]{1,0:T(4,128)}, f32[256]{0:T(256)}, /*index=5*/f32[12]{0:T(128)}, f32[12]{0:T(128)}, f32[12]{0:T(128)}, f32[768]{0:T(1024)}) all-reduce(f32[1536]{0:T(1024)S(1)} %get-tuple-element.1071, ...), channel_id=1, replica_groups=mesh['seq'=8,'head'=4] {'seq'}, use_global_device_ids=true, to_apply=%region_40.41 | all-reduce | flops 7460 | bytes 59680 | tf_op jit(solution)/shard_map/psum | solution.py:303
  1246.4 11.9 fusion.104
  1258.3 15.0 %reduce-scatter.8.cloned.1.call-done = f32[192,768]{1,0:T(8,128)} async-done(((f32[1536,768]{1,0:T(8,128)}), f32[192,768]{1,0:T(8,128)}) %reduce-scatter.8.cloned.1.call-update) | async-done | bytes 589840 | tf_op jit(solution)/shard_map/reduce_scatter | solution.py:277
  1273.4 57.8 %reduce-scatter.14.cloned.1.call-done = f32[768,192]{0,1:T(8,128)} async-done(((f32[768,1536]{0,1:T(8,128)}), f32[768,192]{0,1:T(8,128)}) %reduce-scatter.14.cloned.1.call-update) | async-done | bytes 589840 | tf_op jit(solution)/shard_map/reduce_scatter | solution.py:288
  1331.2 37.6 %reduce-scatter.12.cloned.1.call-done = f32[384,32]{0,1:T(8,128)} async-done(((f32[384,256]{0,1:T(8,128)}), f32[384,32]{0,1:T(8,128)}) %reduce-scatter.12.cloned.1.call-update) | async-done | bytes 49168 | tf_op jit(solution)/shard_map/reduce_scatter | solution.py:289
  1368.8 57.7 %reduce-scatter.10.cloned.1.call-done = f32[192,768]{1,0:T(8,128)} async-done(((f32[1536,768]{1,0:T(8,128)}), f32[192,768]{1,0:T(8,128)}) %reduce-scatter.10.cloned.1.call-update) | async-done | bytes 589840 | tf_op jit(solution)/shard_map/reduce_scatter | solution.py:280
  (704 shorter events, 340.9 us)
Async XLA Ops:
  7.2 289.7 %copy-start = (bf16[1536,768]{1,0:T(8,128)(2,1)S(1)}, bf16[1536,768]{1,0:T(8,128)(2,1)}, u32[]{:S(2)}) copy-start(bf16[1536,768]{1,0:T(8,128)(2,1)} %param.28) | copy-start | bytes 7077892
  7.2 64.0 %all-reduce.30.cloned.1.call-start = ((), (), s32[]{:S(2)}) async-start(), calls=%async_computation.5 | async-start | bytes 2097152 | tf_op jit(solution)/shard_map/psum | solution.py:172
  16.5 8.1 copy-start.68
  16.5 8.1 copy-start.77
  16.5 8.7 copy-start.67
  16.5 8.7 copy-start.27
  16.5 8.7 copy-start.73
  16.5 257.8 %all-gather.7.cloned.1.call-start = ((), (), s32[]{:S(2)}) async-start(), calls=%async_computation.11 | async-start | bytes 3538944 | tf_op jit(solution)/shard_map/all_gather | solution.py:23
  16.6 8.6 copy-start.3
  22.0 5.6 collective-permute-start
  25.2 70.3 %copy-start.59 = (f32[1,256]{1,0:T(1,128)}, f32[1,256]{1,0:T(1,128)S(1)}, u32[]{:S(2)}) copy-start(f32[1,256]{1,0:T(1,128)S(1)} %get-tuple-element.1250) | copy-start | bytes 3076
  25.2 70.3 %copy-start.61 = (f32[1,256]{1,0:T(1,128)}, f32[1,256]{1,0:T(1,128)S(1)}, u32[]{:S(2)}) copy-start(f32[1,256]{1,0:T(1,128)S(1)} %get-tuple-element.1251) | copy-start | bytes 3076
  25.2 70.3 %copy-start.63 = (f32[1,256]{1,0:T(1,128)}, f32[1,256]{1,0:T(1,128)S(1)}, u32[]{:S(2)}) copy-start(f32[1,256]{1,0:T(1,128)S(1)} %get-tuple-element.1252) | copy-start | bytes 3076
  25.2 70.3 %copy-start.65 = (f32[1,256]{1,0:T(1,128)}, f32[1,256]{1,0:T(1,128)S(1)}, u32[]{:S(2)}) copy-start(f32[1,256]{1,0:T(1,128)S(1)} %get-tuple-element.1253) | copy-start | bytes 3076
  26.8 55.7 %copy-start.38 = (f32[768]{0:T(1024)}, f32[768]{0:T(1024)S(1)}, u32[]{:S(2)}) copy-start(f32[768]{0:T(1024)S(1)} %get-tuple-element.1085) | copy-start | bytes 9220
  26.8 55.7 %copy-start.40 = (f32[768]{0:T(1024)}, f32[768]{0:T(1024)S(1)}, u32[]{:S(2)}) copy-start(f32[768]{0:T(1024)S(1)} %get-tuple-element.1086) | copy-start | bytes 9220
  26.8 55.7 %copy-start.42 = (f32[768]{0:T(1024)}, f32[768]{0:T(1024)S(1)}, u32[]{:S(2)}) copy-start(f32[768]{0:T(1024)S(1)} %get-tuple-element.1087) | copy-start | bytes 9220
  26.8 55.7 %copy-start.44 = (f32[768]{0:T(1024)}, f32[768]{0:T(1024)S(1)}, u32[]{:S(2)}) copy-start(f32[768]{0:T(1024)S(1)} %get-tuple-element.1088) | copy-start | bytes 9220
  27.6 55.0 %copy-start.32 = (f32[3,768]{1,0:T(4,128)}, f32[3,768]{1,0:T(4,128)S(1)}, u32[]{:S(2)}) copy-start(f32[3,768]{1,0:T(4,128)S(1)} %broadcast_multiply_fusion.8) | copy-start | bytes 27652
  71.9 23.5 %collective-permute-start.1 = (f32[3,256]{1,0:T(4,128)S(1)}, f32[3,256]{1,0:T(4,128)S(1)}, u32[]{:S(2)}, u32[]{:S(2)}) collective-permute-start(f32[3,256]{1,0:T(4,128)S(1)} %slice.210), channel_id=1, source_target_pairs={{0,4},{4,8},{8,12},{12,16},{16,20},{20,24},{24,28},{1,5},{5,9},{9,... | collective-permute-start | bytes 9224 | tf_op jit(solution)/shard_map/ppermute | solution.py:18
  95.5 6.6 copy-start.46
  242.3 194.9 %all-gather.9.cloned.1.call-start = ((), (), s32[]{:S(2)}) async-start(), calls=%async_computation.12 | async-start | bytes 3538944 | tf_op jit(solution)/shard_map/all_gather | solution.py:23
  243.1 91.4 %copy-start.53 = (f32[768]{0:T(1024)}, f32[768]{0:T(1024)S(1)}, u32[]{:S(2)}) copy-start(f32[768]{0:T(1024)S(1)} %convert_element_type.45) | copy-start | bytes 9220
  317.0 17.5 %copy-start.49 = (f32[1024]{0:T(1024)}, f32[1024]{0:T(1024)S(1)}, u32[]{:S(2)}) copy-start(f32[1024]{0:T(1024)S(1)} %get-tuple-element.1249) | copy-start | bytes 12292
  352.7 397.5 %all-reduce.32.cloned.1.call-start = ((), (), s32[]{:S(2)}) async-start(), calls=%async_computation.6 | async-start | bytes 2097152 | tf_op jit(solution)/shard_map/psum | solution.py:242
  426.3 6.1 copy-start.16
  426.3 6.1 copy-start.50
  426.3 6.1 copy-start.54
  426.3 6.1 copy-start.74
  437.1 14.7 %copy-start.58 = (f32[12]{0:T(128)S(1)}, f32[12]{0:T(128)}, u32[]{:S(2)}) copy-start(f32[12]{0:T(128)} %get-tuple-element.704) | copy-start | bytes 148
  457.8 19.8 %copy-start.36 = (f32[12]{0:T(128)}, f32[12]{0:T(128)S(1)}, u32[]{:S(2)}) copy-start(f32[12]{0:T(128)S(1)} %fusion.296) | copy-start | bytes 148 | tf_op jit(solution)/shard_map/transpose(jvp())/while
  469.5 8.2 copy-start.25
  515.8 19.8 %copy-start.36 = (f32[12]{0:T(128)}, f32[12]{0:T(128)S(1)}, u32[]{:S(2)}) copy-start(f32[12]{0:T(128)S(1)} %fusion.296) | copy-start | bytes 148 | tf_op jit(solution)/shard_map/transpose(jvp())/while
  527.5 8.2 copy-start.25
  574.3 19.8 %copy-start.36 = (f32[12]{0:T(128)}, f32[12]{0:T(128)S(1)}, u32[]{:S(2)}) copy-start(f32[12]{0:T(128)S(1)} %fusion.296) | copy-start | bytes 148 | tf_op jit(solution)/shard_map/transpose(jvp())/while
  586.0 8.2 copy-start.25
  632.9 19.8 %copy-start.36 = (f32[12]{0:T(128)}, f32[12]{0:T(128)S(1)}, u32[]{:S(2)}) copy-start(f32[12]{0:T(128)S(1)} %fusion.296) | copy-start | bytes 148 | tf_op jit(solution)/shard_map/transpose(jvp())/while
  644.6 8.2 copy-start.25
  691.2 7.2 copy-start.17
  699.4 88.0 %reduce-scatter.16.cloned.1.call-start = ((), (), s32[]{:S(2)}) async-start(), calls=%async_computation.13 | async-start | bytes 884736
  707.3 9.2 copy-start.39
  707.3 9.2 copy-start.41
  707.3 9.2 copy-start.43
  707.3 9.2 copy-start.45
  717.6 6.4 copy-start.24
  717.6 6.6 copy-start.4
  722.8 11.0 collective-permute-start.2
  733.5 483.1 %all-reduce.34.cloned.1.call-start = ((), (), s32[]{:S(2)}) async-start(), calls=%async_computation.14 | async-start | bytes 25165824 | tf_op jit(solution)/shard_map/psum | solution.py:207
  738.4 11.8 copy-start.14
  738.4 11.8 copy-start.15
  738.4 11.8 copy-start.47
  742.2 10.1 copy-start.60
  742.2 10.1 copy-start.62
  742.2 10.1 copy-start.64
  742.2 10.2 copy-start.66
  752.7 3.1 collective-permute-start.3
  758.8 514.6 %reduce-scatter.8.cloned.1.call-start = ((), (), s32[]{:S(2)}) async-start(), calls=%async_computation.7 | async-start | bytes 5308416 | tf_op jit(solution)/shard_map/reduce_scatter | solution.py:277
  767.0 564.2 %reduce-scatter.14.cloned.1.call-start = ((), (), s32[]{:S(2)}) async-start(), calls=%async_computation.10 | async-start | bytes 5308416 | tf_op jit(solution)/shard_map/reduce_scatter | solution.py:288
  775.5 593.3 %reduce-scatter.12.cloned.1.call-start = ((), (), s32[]{:S(2)}) async-start(), calls=%async_computation.9 | async-start | bytes 442368 | tf_op jit(solution)/shard_map/reduce_scatter | solution.py:289
  778.0 648.4 %reduce-scatter.10.cloned.1.call-start = ((), (), s32[]{:S(2)}) async-start(), calls=%async_computation.8 | async-start | bytes 5308416 | tf_op jit(solution)/shard_map/reduce_scatter | solution.py:280
  785.0 431.6 %copy-start.30 = (f32[1536]{0:T(1024)S(1)}, f32[1536]{0:T(1024)}, u32[]{:S(2)}) copy-start(f32[1536]{0:T(1024)} %copy-done.29) | copy-start | bytes 18436
  785.0 431.6 %copy-start.35 = (f32[1024]{0:T(1024)S(1)}, f32[1024]{0:T(1024)}, u32[]{:S(2)}) copy-start(f32[1024]{0:T(1024)} %copy-done.34) | copy-start | bytes 12292
  1216.6 29.8 %copy-start.56 = (f32[1024]{0:T(1024)S(1)}, f32[1024]{0:T(1024)}, u32[]{:S(2)}) copy-start(f32[1024]{0:T(1024)} %get-tuple-element.1246) | copy-start | bytes 12292
  1246.4 180.0 %copy-start.1 = (bf16[1536,768]{1,0:T(8,128)(2,1)S(1)}, bf16[1536,768]{1,0:T(8,128)(2,1)}, u32[]{:S(2)}) copy-start(bf16[1536,768]{1,0:T(8,128)(2,1)} %param.28) | copy-start | bytes 7077892
  (44 other events, 115.6 us)
Sparse Core Ops, SparseCore 0:
  16.6 54.6 all-reduce.29
  242.4 31.9 all-gather.6
  352.8 30.9 all-gather.8
  699.5 50.6 all-reduce.31
  753.2 34.1 reduce-scatter.15
  790.4 426.1 all-reduce.33
  1220.6 52.6 reduce-scatter.7
  1277.4 53.7 reduce-scatter.13
  1334.8 33.8 reduce-scatter.11
  1372.6 53.7 reduce-scatter.9
where the time goes:
time: 1450 us; the launch traced here: 1430 us
  waiting for transfers between devices  654 us (45%)
  local copies, waits for them, and re-layouts  315 us (22%)
  matrix products  205 us (14%)
  other arithmetic  173 us (12%)
  blocking collectives  59.6 us (4%)
  between operations  16.2 us (1%)
    psum x1, waiting for transfers between devices, on_device(): branch = lax.psum(matmul_low(ynorm, proj_output), 'head')  428 us
    dynamic_update_slice x44, local copies, waits for them, and re-layouts, ssd_device(): lax.scan(jax.checkpoint(advance), start_carry, pieces)  172 us
    reduce_scatter x1, waiting for transfers between devices, on_device(): lax.psum_scatter(local_proj_output, 'seq', scatter_dimension=1, tiled=True)  57.8 us
    reduce_scatter x1, waiting for transfers between devices, on_device(): lax.psum_scatter(transposed_times(normed, grad_input_b), 'seq', scatter_d...  57.7 us
    dot_general x12, matrix products, ssd_block(): intra_out = jnp.einsum('hts,shp->thp', mixing, block_x, precision=HIGH)  54.1 us
    psum x1, waiting for transfers between devices, on_device(): states_pre = lax.psum(matmul_low(normed_rows, proj_states), 'head')  43.6 us
    reduce_scatter x1, waiting for transfers between devices, on_device(): lax.psum_scatter(transposed_times(normed_rows, grad_states_b), 'seq', sca...  37.6 us
    another operation x62, other arithmetic  36.9 us
  transfers between devices with their start and end apart: 14, of which 10 were waited for; matrix products, arithmetic and copies ran while one was open for 14% of the time, Pallas kernels for 0%

commit v1 on v0

v1 whole, which is shorter than its diff:
```python
import functools

import jax
import jax.numpy as jnp
import numpy as np
from jax import lax
from jax.experimental import pallas as pl
from jax.experimental.pallas import tpu as pltpu
from jax.sharding import PartitionSpec as P


DI = 3072
EPS = 1e-05
Q = 128
LANES = 128
HALO = 8
TAPS = 4

F32 = jnp.float32
BF16 = jnp.bfloat16
NN = (((1,), (0,)), ((), ()))
NT = (((1,), (1,)), ((), ()))
TN = (((0,), (0,)), ((), ()))
VMEM_LIMIT = 60 * 1024 * 1024
MESH_ID = pl.DeviceIdType.MESH


def dg(left, right, dims):
    return lax.dot_general(left, right, dims, preferred_element_type=F32)


def split(value):
    high = value.astype(BF16)
    return high, (value - high.astype(F32)).astype(BF16)


def dot3(left, right, dims):
    (lh, ll), (rh, rl) = split(left), split(right)
    return dg(lh, rh, dims) + (dg(lh, rl, dims) + dg(ll, rh, dims))


def spread(heads, onehot):
    high, low = split(heads)
    return dg(high, onehot, NN) + dg(low, onehot, NN)


def gather(wide, onehot):
    high, low = split(wide)
    return dg(high, onehot, NT) + dg(low, onehot, NT)


def sigmoid(value):
    return 1.0 / (1.0 + jnp.exp(-value))


def silu(value):
    return value * sigmoid(value)


def shifted(block, axis, distance):
    devices = range(lax.axis_size(axis))
    route = [(i - distance, i) for i in devices if i - distance in devices]
    return lax.ppermute(block, axis, route)


def call(kernel, grid, ins, outs, scratch=(), flops=0, collective=None):
    in_specs = [spec for _, spec in ins]
    size = sum(a.size * a.dtype.itemsize for a, _ in ins) + sum(
        s.size * s.dtype.itemsize for s, _ in outs
    )
    return pl.pallas_call(
        kernel,
        grid=grid,
        in_specs=in_specs,
        out_specs=[spec for _, spec in outs],
        out_shape=[shape for shape, _ in outs],
        scratch_shapes=list(scratch),
        cost_estimate=pl.CostEstimate(flops=flops, bytes_accessed=size, transcendentals=0),
        compiler_params=pltpu.CompilerParams(vmem_limit_bytes=VMEM_LIMIT)
        if collective is None
        else pltpu.CompilerParams(
            vmem_limit_bytes=VMEM_LIMIT, collective_id=collective, has_side_effects=True
        ),
    )(*[a for a, _ in ins])


def sds(shape, dtype=F32):
    return jax.ShapeDtypeStruct(shape, dtype)


def rows(width, reverse=None):
    if reverse is None:
        return pl.BlockSpec((Q, width), lambda c: (c, 0))
    return pl.BlockSpec((Q, width), lambda c: (reverse - 1 - c, 0))


def whole(shape):
    return pl.BlockSpec(shape, lambda c: (0,) * len(shape))


def before(width):
    return pl.BlockSpec((HALO, width), lambda c: (jnp.maximum(c * (Q // HALO) - 1, 0), 0))


def triangle(lower):
    a = lax.broadcasted_iota(jnp.int32, (Q, Q), 0)
    b = lax.broadcasted_iota(jnp.int32, (Q, Q), 1)
    return a >= b if lower else a <= b


def tri_sum(lower, value):
    mask = triangle(lower).astype(BF16)
    high = value.astype(BF16)
    rest = value - high.astype(F32)
    mid = rest.astype(BF16)
    low = (rest - mid.astype(F32)).astype(BF16)
    return dg(mask, high, NN) + (dg(mask, mid, NN) + dg(mask, low, NN))


def conv_act(pre_ref, prev_ref, halo_ref, params, at, ext_ref):
    first = pl.program_id(0) == 0
    size = ext_ref.shape[1]
    ext_ref[:HALO, :] = jnp.where(first, halo_ref[...], prev_ref[...])
    ext_ref[HALO:, :] = pre_ref[...]
    taps = TAPS
    total = params[at + taps : at + taps + 1, :size] + params[at + taps - 1 : at + taps, :size] * pre_ref[...]
    for k in range(taps - 1):
        start = HALO - taps + 1 + k
        total = total + params[at + k : at + k + 1, :size] * ext_ref[start : start + Q, :]
    return total


def states_kernel(
    n, pre, pre_prev, pre_halo, normed, normed_halo, step_w, vec, taps_in, taps_st, onehot, *refs
):
    pieces, refs = refs[:n], refs[n:]
    act_o, sact_o, spre_o, shalo_o, spre_step_o, step_o, cum_o, cumt_o, sin_o, dev_o, total_o = refs[:11]
    before_o, params = refs[11:13]
    ext, sext, state, total, full = refs[13:]
    c = pl.program_id(0)
    me = lax.axis_index("head")
    state_size = bmat_width(sact_o)
    inner = pre.shape[1]
    two = 2 * state_size
    hot = onehot[...]

    def line(first, size):
        return jnp.concatenate([vec[r : r + 1, :] for r in range(first, first + size // LANES)], axis=1)

    @pl.when(c == 0)
    def _():
        state[...] = jnp.zeros_like(state)
        total[...] = jnp.zeros_like(total)
        height = pieces[0].shape[0]
        for k in range(n):
            full[pl.ds(pl.multiple_of(((me + n - k) % n) * height, height), height), :] = pieces[k][...]
        params[...] = jnp.zeros_like(params)
        per = inner // LANES
        params[0:TAPS, :] = taps_in[...].astype(F32)
        params[4:5, :] = line(3, inner)
        params[5:6, :] = line(3 + per, inner)
        params[6:7, :] = spread(jnp.broadcast_to(vec[2:3, :], (HALO, LANES)), hot)[:1]
        params[7:8, :LANES] = -jnp.exp(vec[0:1, :])
        params[7:8, LANES : 2 * LANES] = vec[1:2, :]
        params[8 : 8 + TAPS, :two] = taps_st[...].astype(F32)
        params[12:13, :two] = line(3 + 2 * per, two)
        first = dg(normed_halo[...], full[...], NN)
        shalo_o[...] = jnp.where(lax.axis_index("seq") == 0, 0.0, first)
        sext[Q:, :] = shalo_o[...]

    sext[:HALO, :] = sext[Q:, :]
    spre = dg(normed[...], full[...], NN)
    spre_o[...] = spre
    sext[HALO:, :] = spre
    step_pre = dg(normed[...], step_w[...], NN)
    spre_step_o[...] = step_pre
    act = conv_act(pre, pre_prev, pre_halo, params, 0, ext)
    sact = params[12:13, :two] + params[8 + TAPS - 1 : 8 + TAPS, :two] * spre
    for k in range(TAPS - 1):
        start = HALO - TAPS + 1 + k
        sact = sact + params[8 + k : 9 + k, :two] * sext[start : start + Q, :]
    act_o[...] = act
    sact_o[...] = sact
    bmat = silu(sact[:, :state_size])
    step = jax.nn.softplus(step_pre + params[7:8, LANES : 2 * LANES])
    cum = tri_sum(True, step * params[7:8, :LANES])
    step_o[...] = step
    cum_o[...] = cum
    cumt_o[...] = cum.T
    last = cum[Q - 1 :, :]
    weight = spread(step * jnp.exp(last - cum), hot)
    xw = silu(act) * weight
    sin_o[...] = state[...]
    before_o[...] = total[...]
    decay = spread(jnp.broadcast_to(jnp.exp(last), (HALO, LANES)), hot)[:1]
    state[...] = state[...] * decay + dot3(bmat, xw, TN)
    total[...] = total[...] + last
    dev_o[:state_size, :] = state[...]
    dev_o[state_size:, :] = spread(jnp.broadcast_to(jnp.exp(total[...]), (HALO, LANES)), hot)
    total_o[...] = total[...]


def bmat_width(ref):
    return ref.shape[1] // 2


def pair_stack(value):
    high, low = split(value)
    return jnp.concatenate(
        [
            jnp.concatenate([high, low], axis=1),
            jnp.concatenate([high, jnp.zeros_like(high)], axis=1),
        ],
        axis=0,
    )


def intra_kernel(
    ns, act, sact, step, cum, cumt, params, onehot, packed, out, incoming,
    xs_ref, entered, got_s, got_d, prefix, sems,
):
    c = pl.program_id(0)
    count = pl.num_programs(0)
    seq = lax.axis_index("seq")
    begin, turn, end = swap_states(ns, packed, entered, got_s, got_d, prefix, sems, False)
    barrier = pltpu.get_barrier_semaphore()

    @pl.when(c == 0)
    def _():
        for k in range(1, ns):
            pl.semaphore_signal(
                barrier, inc=1, device_id={"seq": (seq + k) % ns}, device_id_type=MESH_ID
            )
        pl.semaphore_wait(barrier, ns - 1)
        begin()

    state_size = bmat_width(sact)
    sconv = silu(sact[...])
    bmat, cmat = sconv[:, :state_size], sconv[:, state_size:]
    scores = dot3(cmat, bmat, NT)
    x = silu(act[...])
    xs_ref[...] = x * spread(step[...], onehot[...])
    out[...] = x * params[6:7, :]
    causal = triangle(True)
    lane = lax.broadcasted_iota(jnp.int32, (Q, LANES), 1)
    for p in range(act.shape[1] // LANES):
        cols = slice(p * LANES, (p + 1) * LANES)
        right = pair_stack(xs_ref[:, cols])
        got = []
        for j in range(2):
            h = p * 2 + j
            gap = cum[:, h : h + 1] - cumt[h : h + 1, :]
            mixing = scores * jnp.exp(jnp.where(causal, gap, -1e30))
            wide = dg(jnp.concatenate(split(mixing), axis=1), right, NN)
            got.append(wide[:, :LANES] + wide[:, LANES:])
        out[:, cols] = out[:, cols] + jnp.where(lane < LANES // 2, got[0], got[1])

    @pl.when(c == count // 2)
    def _():
        turn()

    @pl.when(c == count - 1)
    def _():
        end()
        incoming[...] = entered[...]


STREAMS = 4
GAP = 2
SPAN = 83.0


def encode(value):
    top = jnp.max(jnp.abs(value), axis=1, keepdims=True)
    scale = (top * 1.004 + 1e-30).astype(BF16)
    code = jnp.exp(value * (SPAN / scale.astype(F32))).astype(BF16)
    return code, jnp.broadcast_to(scale, (value.shape[0], LANES))


def decode(block, width):
    scale = block[:, width : width + 1].astype(F32) * (1.0 / SPAN)
    return jnp.log(block[:, :width].astype(F32)) * scale


def swap_states(ns, packed, out, got_s, got_d, prefix, sems, reverse):
    seq = lax.axis_index("seq")
    own = out.shape[0] // ns
    total = out.shape[0]

    def rows_of(j):
        return pl.ds(pl.multiple_of(j * own, own), own)

    def remote(src, dst, send, recv, to):
        return pltpu.make_async_remote_copy(
            src_ref=src,
            dst_ref=dst,
            send_sem=send,
            recv_sem=recv,
            device_id={"seq": to},
            device_id_type=MESH_ID,
        )

    def copies(k, arriving):
        other = (seq + k) % ns
        slot = other if arriving else seq
        part = packed.at[rows_of(other)]
        decay = packed.at[pl.ds(total, HALO)]
        return (
            remote(part, got_s.at[slot], sems.at[0, k], sems.at[1, slot], other),
            remote(decay, got_d.at[slot], sems.at[2, k], sems.at[3, slot], other),
        )

    def answer(k, arriving):
        other = (seq + k) % ns
        slot = other if arriving else seq
        return remote(
            prefix.at[other], out.at[rows_of(slot)], sems.at[4, k], sems.at[5, slot], other
        )

    def begin():
        for k in range(1, ns):
            for copy in copies(k, False):
                copy.start()

    def turn():
        got_s[seq] = packed[rows_of(seq), :]
        got_d[seq] = packed[total:, :]
        for k in range(1, ns):
            for copy in copies(k, True):
                copy.wait_recv()
        carry = jnp.zeros((own, out.shape[1]), F32)
        for i in reversed(range(ns)) if reverse else range(ns):
            prefix[i] = carry
            carry = carry * got_d[i, 0:1, :] + got_s[i]
        for k in range(1, ns):
            answer(k, False).start()
        out[rows_of(seq), :] = prefix[seq]

    def end():
        for k in range(1, ns):
            answer(k, True).wait_recv()
        for k in range(1, ns):
            answer(k, False).wait_send()
            for copy in copies(k, False):
                copy.wait_send()

    return begin, turn, end


def swap_scratch(ns, shape):
    own = shape[0] // ns
    return [
        pltpu.VMEM((ns, own, shape[1]), F32),
        pltpu.VMEM((ns, HALO, shape[1]), F32),
        pltpu.VMEM((ns, own, shape[1]), F32),
        pltpu.SemaphoreType.DMA((6, ns)),
    ]


def reduce_kernel(n, ns, dims, cols, with_sums, *refs):
    terms = len(dims)
    lefts, rights = refs[:terms], refs[terms : 2 * terms]
    refs = refs[2 * terms :]
    if with_sums:
        hidden_ref, inv_ref, small_a, small_b, states_ref, out_ref, sum_a, sum_b, sum_s = refs[:9]
        refs = refs[9:]
    else:
        packed, out_ref, later = refs[:3]
        refs = refs[3:]
    part, code_r, code_l, got_r, got_l, sr_sem, sl_sem, rr_sem, rl_sem, ar_sem, al_sem, ag_sem = refs[:12]
    me = lax.axis_index("head")
    tokens = part.shape[0]
    width = part.shape[1]
    span = tokens // STREAMS
    rows_own = span // n
    has_right, has_left = me < n - 1, me > 0

    barrier = pltpu.get_barrier_semaphore()
    for k in range(1, n):
        pl.semaphore_signal(
            barrier, inc=1, device_id={"head": (me + k) % n}, device_id_type=MESH_ID
        )
    seq = lax.axis_index("seq")
    for k in range(1, ns):
        pl.semaphore_signal(
            barrier, inc=1, device_id={"seq": (seq + k) % ns}, device_id_type=MESH_ID
        )
    expected = n + ns - 2
    if with_sums:
        got_a, got_b, got_s, got_c, mine_b = refs[12:17]
        sa_sem, ra_sem, sb_sem, rb_sem, ss_sem, rs_sem, sc_sem, rc_sem = refs[17:]
    else:
        begin, turn, end = swap_states(ns, packed, later, *refs[12:], True)

    def to_seq(src, dst, ssem, rsem, k):
        return pltpu.make_async_remote_copy(
            src_ref=src,
            dst_ref=dst.at[seq],
            send_sem=ssem.at[k],
            recv_sem=rsem.at[seq],
            device_id={"seq": (seq + k) % ns},
            device_id_type=MESH_ID,
        )

    def from_seq(src, dst, ssem, rsem, k):
        other = (seq + k) % ns
        return pltpu.make_async_remote_copy(
            src_ref=src,
            dst_ref=dst.at[other],
            send_sem=ssem.at[k],
            recv_sem=rsem.at[other],
            device_id={"seq": other},
            device_id_type=MESH_ID,
        )

    def states_at(j):
        own = sum_s.shape[0]
        return states_ref.at[pl.ds(pl.multiple_of(j * own, own), own)]

    def at(d, h):
        return pl.ds(pl.multiple_of(h * span + d * rows_own, rows_own), rows_own)

    def step(d, h, right):
        code, got, ssem, rsem = (
            (code_r, got_r, sr_sem, rr_sem) if right else (code_l, got_l, sl_sem, rl_sem)
        )
        return pltpu.make_async_remote_copy(
            src_ref=code.at[at(d, h)],
            dst_ref=got.at[at(d, h)],
            send_sem=ssem.at[h, d],
            recv_sem=rsem.at[h, d],
            device_id={"head": me + 1 if right else me - 1},
            device_id_type=MESH_ID,
        )

    def hand_on(b, h, right):
        return pltpu.make_async_remote_copy(
            src_ref=out_ref.at[at(b, h)],
            dst_ref=out_ref.at[at(b, h)],
            send_sem=(ar_sem if right else al_sem).at[h, b],
            recv_sem=ag_sem.at[h, b],
            device_id={"head": me + 1 if right else me - 1},
            device_id_type=MESH_ID,
        )

    def put(ref, where, value):
        code, scale = encode(value)
        ref[where, :width] = code
        ref[where, width:] = scale

    def compute(h):
        where = pl.ds(h * span, span)
        total = None
        for left, right, dim, col in zip(lefts, rights, dims, cols):
            value = left[where, :] if col is None else left[where, col[0] : col[1]]
            term = dg(value, right[...], dim)
            total = term if total is None else total + term
        part[where, :] = total
        if with_sums:
            seen = total * (hidden_ref[where, :].astype(F32) * inv_ref[where, :])
            row = jnp.sum(seen, axis=0, keepdims=True)
            mine_b[0:1, :] = row if h == 0 else mine_b[0:1, :] + row

    def chain(h, u):
        for right in (True, False):
            d = me + (n - 1 - u) if right else me - (n - 1 - u)
            code, got = (code_r, got_r) if right else (code_l, got_l)
            inside = d <= n - 1 if right else d >= 0
            fed = has_left if right else has_right

            @pl.when(inside & fed)
            def _():
                step(d, h, right).wait_recv()
                put(code, at(d, h), part[at(d, h), :] + decode(got[at(d, h), :], width))
                step(d, h, right).start()

            @pl.when(inside & jnp.logical_not(fed))
            def _():
                put(code, at(d, h), part[at(d, h), :])
                step(d, h, right).start()

    def finish(h):
        own = at(me, h)

        @pl.when(has_left)
        def _():
            step(me, h, True).wait_recv()
            part[own, :] = part[own, :] + decode(got_r[own, :], width)

        @pl.when(has_right)
        def _():
            step(me, h, False).wait_recv()
            part[own, :] = part[own, :] + decode(got_l[own, :], width)

        if not with_sums:
            put(out_ref, pl.ds(h * rows_own, rows_own), part[own, :])
            return

        put(out_ref, own, part[own, :])

        @pl.when(has_right)
        def _():
            hand_on(me, h, True).start()

        @pl.when(has_left)
        def _():
            hand_on(me, h, False).start()

    def relay(h, s):
        @pl.when(me - s >= 0)
        def _():
            hand_on(me - s, h, True).wait_recv()

            @pl.when(has_right)
            def _():
                hand_on(me - s, h, True).start()

        @pl.when(me + s < n)
        def _():
            hand_on(me + s, h, False).wait_recv()

            @pl.when(has_left)
            def _():
                hand_on(me + s, h, False).start()

    for t in range(GAP * (STREAMS - 1) + 2 * n - 1):
        for h in range(STREAMS):
            u = t - GAP * h
            if u == 0:
                compute(h)
                if h == 0:
                    pl.semaphore_wait(barrier, expected)
                    if with_sums:
                        for k in range(1, ns):
                            to_seq(small_a, got_a, sa_sem, ra_sem, k).start()
                            to_seq(states_at((seq + k) % ns), got_s, ss_sem, rs_sem, k).start()
                    else:
                        begin()
                if h == STREAMS - 1 and with_sums:
                    mine_b[8:16, :] = jnp.zeros((8, width), F32)
                    mine_b[8:16, : small_b.shape[1]] = small_b[...]
                    for k in range(1, ns):
                        to_seq(mine_b, got_b, sb_sem, rb_sem, k).start()
            if 0 <= u < n - 1:
                chain(h, u)
            if u == n - 1:
                finish(h)
            if with_sums and n - 1 < u < 2 * n - 1:
                relay(h, u - n + 1)
        if not with_sums and t == n - 1:
            turn()
    if not with_sums:
        end()
    if with_sums:
        total = small_a[...]
        for k in range(1, ns):
            from_seq(small_a, got_a, sa_sem, ra_sem, k).wait_recv()
            total = total + got_a[(seq + k) % ns]
        sum_a[...] = total
        total = states_at(seq)[...]
        for k in range(1, ns):
            from_seq(states_at(seq), got_s, ss_sem, rs_sem, k).wait_recv()
            total = total + got_s[(seq + k) % ns]
        sum_s[...] = total
        total = mine_b[...]
        for k in range(1, ns):
            from_seq(mine_b, got_b, sb_sem, rb_sem, k).wait_recv()
            total = total + got_b[(seq + k) % ns]
        sum_b[...] = total

        def to_head(k):
            return pltpu.make_async_remote_copy(
                src_ref=sum_b,
                dst_ref=got_c.at[me],
                send_sem=sc_sem.at[k],
                recv_sem=rc_sem.at[me],
                device_id={"head": (me + k) % n},
                device_id_type=MESH_ID,
            )

        def from_head(k):
            other = (me + k) % n
            return pltpu.make_async_remote_copy(
                src_ref=sum_b,
                dst_ref=got_c.at[other],
                send_sem=sc_sem.at[k],
                recv_sem=rc_sem.at[other],
                device_id={"head": other},
                device_id_type=MESH_ID,
            )

        for k in range(1, n):
            to_head(k).start()
        total = sum_b[...]
        for k in range(1, n):
            from_head(k).wait_recv()
        for k in range(1, n):
            to_head(k).wait_send()
            total = total + got_c[(me + k) % n]
        sum_b[...] = total
        for k in range(1, ns):
            to_seq(small_a, got_a, sa_sem, ra_sem, k).wait_send()
            to_seq(states_at((seq + k) % ns), got_s, ss_sem, rs_sem, k).wait_send()
            to_seq(mine_b, got_b, sb_sem, rb_sem, k).wait_send()
    for h in range(STREAMS):
        for i in range(n):

            @pl.when(i > me)
            def _():
                step(i, h, True).wait_send()

            @pl.when(i < me)
            def _():
                step(i, h, False).wait_send()

            if with_sums:

                @pl.when(has_right & (i <= me))
                def _():
                    hand_on(i, h, True).wait_send()

                @pl.when(has_left & (i >= me))
                def _():
                    hand_on(i, h, False).wait_send()


def reduce_over_heads(products, dims, collective, sums=None, packed=None, cols=None):
    n, ns = lax.axis_size("head"), lax.axis_size("seq")
    tokens, width = products[0][0].shape[0], products[0][1].shape[dims[0][0][1][0] ^ 1]
    lefts, rights = [a for a, _ in products], [b for _, b in products]
    dma = pltpu.SemaphoreType.DMA
    coded = pltpu.VMEM((tokens, width + LANES), BF16)
    scratch = [pltpu.VMEM((tokens, width), F32), coded, coded, coded, coded]
    scratch += [dma((STREAMS, n))] * 7
    if sums is not None:
        extra = list(sums)
        small_a = sums[2].shape
        states = (sums[4].shape[0] // ns, sums[4].shape[1])
        out_shape = [sds((tokens, width + LANES), BF16), sds(small_a), sds((16, width)), sds(states)]
        scratch += [
            pltpu.VMEM((ns, *small_a), F32),
            pltpu.VMEM((ns, 16, width), F32),
            pltpu.VMEM((ns, *states), F32),
            pltpu.VMEM((n, 16, width), F32),
            pltpu.VMEM((16, width), F32),
        ]
        scratch += [dma((ns,))] * 6 + [dma((n,))] * 2
    else:
        extra = [packed]
        states = (packed.shape[0] - HALO, packed.shape[1])
        out_shape = [sds((tokens // n, width + LANES), BF16), sds(states)]
        scratch += swap_scratch(ns, states)
    vmem = pl.BlockSpec(memory_space=pltpu.VMEM)
    return pl.pallas_call(
        functools.partial(reduce_kernel, n, ns, dims, cols or [None] * len(dims), sums is not None),
        in_specs=[vmem] * (len(lefts) + len(rights) + len(extra)),
        out_specs=[vmem] * len(out_shape),
        out_shape=out_shape,
        scratch_shapes=scratch,
        compiler_params=pltpu.CompilerParams(
            collective_id=collective, has_side_effects=True, vmem_limit_bytes=VMEM_LIMIT
        ),
        cost_estimate=pl.CostEstimate(
            flops=2 * tokens * width * sum(a.shape[1] for a in lefts),
            bytes_accessed=100 * tokens * width,
            transcendentals=0,
        ),
        name="reduce_heads" if sums is not None else "scatter_heads",
    )(*lefts, *rights, *extra)


def result_kernel(n, *refs):
    pieces, hidden, out = refs[:n], refs[n], refs[n + 1]
    me = lax.axis_index("head")
    width = out.shape[1]
    size = out.shape[0] // n
    for k in range(n):
        where = pl.ds(pl.multiple_of(((me + n - k) % n) * size, size), size)
        out[where, :] = hidden[where, :].astype(F32) + decode(pieces[k][...], width)


def turn_kernel(value, out):
    high = value.shape[0]
    more = jnp.zeros((-high % LANES, value.shape[1]), F32)
    out[...] = jnp.concatenate([value[...], more], axis=0).T[:, :high]


def hidden_kernel(code, hidden, cotangent, inv, gain, out):
    width = out.shape[1]
    grad = decode(code[...], width) * gain[...]
    resid = hidden[...].astype(F32)
    scale = inv[...]
    dots = jnp.sum(grad * resid, axis=1, keepdims=True) * (1.0 / width)
    out[...] = (
        cotangent[...].astype(F32) + scale * grad - resid * (scale * scale * scale * dots)
    )


def rows_of_sums(square, cross):
    ones = jnp.ones((HALO, square.shape[1]), BF16)
    (sh, sl), (ch, cl) = split(square), split(cross)
    first = dg(ones, sh, NT) + dg(ones, sl, NT)
    second = dg(ones, ch, NT) + dg(ones, cl, NT)
    row = lax.broadcasted_iota(jnp.int32, first.shape, 0)
    return jnp.where(row == 0, first, second)


def middle_kernel(
    n, yloc, act, sact, cum, sin, before_log, total_log, incoming, gate, gyn, params, onehot,
    y_o, ynorm_o, gpre_o, gssd_o, dout_o, dev_o, rows_o,
    keep, mine, got, adj, ssem, rsem,
):
    i = pl.program_id(0)
    count = pl.num_programs(0) // 2
    c = jnp.where(i < count, i, 2 * count - 1 - i)
    me = lax.axis_index("head")
    state_size = bmat_width(sact)
    hot = onehot[...]
    gain = params[5:6, :]
    where = pl.ds(pl.multiple_of(c * Q, Q), Q)
    barrier = pltpu.get_barrier_semaphore()

    def copy(k, arriving):
        other = (me + k) % n
        return pltpu.make_async_remote_copy(
            src_ref=mine,
            dst_ref=got.at[other if arriving else me],
            send_sem=ssem.at[k],
            recv_sem=rsem.at[other if arriving else me],
            device_id={"head": other},
            device_id_type=MESH_ID,
        )

    @pl.when(i == 0)
    def _():
        for k in range(1, n):
            pl.semaphore_signal(
                barrier, inc=1, device_id={"head": (me + k) % n}, device_id_type=MESH_ID
            )

    cmat = silu(sact[:, state_size:])
    gv = gate[...]
    sg = sigmoid(gv)
    gsilu = gv * sg
    growth = spread(jnp.exp(cum[...]), hot)

    @pl.when(i < count)
    def _():
        carry = spread(jnp.broadcast_to(jnp.exp(before_log[...]), (HALO, LANES)), hot)[:1]
        state = sin[...] + carry * incoming[...]
        y = yloc[...] + growth * dot3(cmat, state, NN)
        y_o[...] = y
        keep[where, :] = y
        gated = y * gsilu
        mine[:, where] = rows_of_sums(gated * gated, gyn[...] * gain * gated)

    @pl.when(i == count - 1)
    def _():
        pl.semaphore_wait(barrier, n - 1)
        for k in range(1, n):
            copy(k, False).start()

    @pl.when(i == count)
    def _():
        adj[...] = jnp.zeros_like(adj)
        rows_o[...] = jnp.zeros_like(rows_o)
        total = mine[...]
        for k in range(1, n):
            copy(k, True).wait_recv()
        for k in range(1, n):
            copy(k, False).wait_send()
            total = total + got[(me + k) % n]
        mine[...] = total

    @pl.when(i >= count)
    def _():
        total = mine[:, where]
        columns = jnp.concatenate([total, jnp.zeros((Q - HALO, Q), F32)], axis=0).T
        inv = lax.rsqrt(columns[:, 0:1] / DI + EPS)
        cross = columns[:, 1:2] / DI
        yv = keep[where, :]
        gated = yv * gsilu
        normed = gated * inv
        ynorm_o[...] = (normed * gain).astype(BF16)
        rows_o[0:1, :] = rows_o[0:1, :] + jnp.sum(gyn[...] * normed, axis=0, keepdims=True)
        ggated = inv * (gyn[...] * gain) - normed * (inv * inv * cross)
        gpre_o[...] = (ggated * yv * sg * (1.0 + gv * (1.0 - sg))).astype(BF16)
        gssd = ggated * gsilu
        gssd_o[...] = gssd
        rows_o[1:2, :] = rows_o[1:2, :] + jnp.sum(gssd * silu(act[...]), axis=0, keepdims=True)
        dout_o[...] = adj[...]
        decay = spread(jnp.broadcast_to(jnp.exp(cum[Q - 1 :, :]), (HALO, LANES)), hot)[:1]
        adj[...] = adj[...] * decay + dot3(cmat, gssd * growth, TN)

    @pl.when(i == 2 * count - 1)
    def _():
        dev_o[:state_size, :] = adj[...]
        whole_log = jnp.broadcast_to(jnp.exp(total_log[...]), (HALO, LANES))
        dev_o[state_size:, :] = spread(whole_log, hot)


def back_kernel(
    n, ns, act, sact, y, gssd, step, step_pre, cum, cumt, sin, dout, before_log, total_log, incoming,
    later, params, onehot, rows_in, pre, pre_prev, pre_halo, spre, spre_prev, spre_halo,
    gin_o, gsb_out, small_a, small_b,
    gsb_o, gstep, xs_ref, u_ref, st_ref, gext, sext, pext, spext, halo_send, halo_got, shalo_send, shalo_got,
    psend, pgot, h_sem, p_send, p_recv, g_send, g_recv,
):
    c = pl.program_id(0)
    count = pl.num_programs(0) - 1
    total_chunks = psend.shape[0] // Q
    groups = total_chunks // n
    taps = TAPS
    me, seq = lax.axis_index("head"), lax.axis_index("seq")
    state_size = bmat_width(sact)
    two = 2 * state_size
    barrier = pltpu.get_barrier_semaphore()

    def halo(src, dst, k):
        return pltpu.make_async_remote_copy(
            src_ref=src,
            dst_ref=dst,
            send_sem=h_sem.at[k],
            recv_sem=h_sem.at[k + 1],
            device_id={"seq": (seq + ns - 1) % ns},
            device_id_type=MESH_ID,
        )

    def chunk_rows(k):
        return pl.ds(pl.multiple_of(k * Q, Q), Q)

    def to_owner(k):
        return pltpu.make_async_remote_copy(
            src_ref=psend.at[chunk_rows(k)],
            dst_ref=pgot.at[me, chunk_rows(k // n)],
            send_sem=p_send.at[k],
            recv_sem=p_recv.at[me, k // n],
            device_id={"head": k % n},
            device_id_type=MESH_ID,
        )

    def from_other(j, g):
        return pltpu.make_async_remote_copy(
            src_ref=psend.at[chunk_rows(g)],
            dst_ref=pgot.at[j, chunk_rows(g)],
            send_sem=p_send.at[g],
            recv_sem=p_recv.at[j, g],
            device_id={"head": j},
            device_id_type=MESH_ID,
        )

    def give(k, g, arriving):
        other = (me + k) % n
        owner = other if arriving else me
        where = chunk_rows(g * n + owner)
        return pltpu.make_async_remote_copy(
            src_ref=gsb_o.at[where],
            dst_ref=gsb_o.at[where],
            send_sem=g_send.at[k, g],
            recv_sem=g_recv.at[owner, g],
            device_id={"head": other},
            device_id_type=MESH_ID,
        )

    @pl.when(c == 0)
    def _():
        for k in range(1, n):
            pl.semaphore_signal(
                barrier, inc=1, device_id={"head": (me + k) % n}, device_id_type=MESH_ID
            )

        @pl.when(seq < ns - 1)
        def _():
            pl.semaphore_signal(
                barrier, inc=1, device_id={"seq": (seq + 1) % ns}, device_id_type=MESH_ID
            )

        small_a[...] = jnp.zeros_like(small_a)
        small_b[...] = jnp.zeros_like(small_b)
        small_a[5:7, :] = rows_in[0:2, :]

    @pl.when(c < count)
    def _():
        hot = onehot[...]
        skip = params[6:7, :]
        rate = params[7:8, :LANES]
        sactv = sact[...]
        ssg = sigmoid(sactv)
        sconv = sactv * ssg
        bmat, cmat = sconv[:, :state_size], sconv[:, state_size:]
        actv = act[...]
        sg = sigmoid(actv)
        x = actv * sg
        cumv, stepv = cum[...], step[...]
        last = cumv[Q - 1 :, :]
        step_wide = spread(stepv, hot)
        xs = x * step_wide
        xs_ref[...] = xs
        g = gssd[...]

        def row(value):
            return spread(jnp.broadcast_to(jnp.exp(value), (HALO, LANES)), hot)[:1]

        state = sin[...] + row(before_log[...]) * incoming[...]
        adj = dout[...] + row(total_log[...] - before_log[...] - last) * later[...]
        to_end = spread(jnp.exp(last - cumv), hot)
        u_state = to_end * dot3(bmat, adj, NN)
        ends = row(last) * jnp.sum(adj * state, axis=0, keepdims=True) + jnp.sum(
            xs * u_state, axis=0, keepdims=True
        )
        scores_t = dot3(bmat, cmat, NT)
        later_mask = triangle(False)
        lane = lax.broadcasted_iota(jnp.int32, (Q, LANES), 1)
        st_ref[...] = jnp.zeros_like(st_ref)
        for p in range(act.shape[1] // LANES):
            cols = slice(p * LANES, (p + 1) * LANES)
            right = pair_stack(gssd[:, cols])
            g_high, g_low = right[:Q, :LANES], right[:Q, LANES:]
            twice = jnp.concatenate([g_high, g_high], axis=1)
            pair = xs_ref[:, cols]
            got = []
            for j in range(2):
                h = p * 2 + j
                gap = cumt[h : h + 1, :] - cum[:, h : h + 1]
                decay = jnp.exp(jnp.where(later_mask, gap, -1e30))
                wide = dg(jnp.concatenate(split(scores_t * decay), axis=1), right, NN)
                got.append(wide[:, :LANES] + wide[:, LANES:])
                mine = (lane < LANES // 2) if j == 0 else (lane >= LANES // 2)
                xh, xl = split(jnp.where(mine, pair, 0.0))
                inner = dg(jnp.concatenate([xh, xl], axis=1), twice, NT) + dg(xh, g_low, NT)
                st_ref[...] = st_ref[...] + decay * inner
            u_ref[:, cols] = jnp.where(lane < LANES // 2, got[0], got[1])
        u = u_ref[...] + u_state
        sc = st_ref[...]
        g_scaled = g * spread(jnp.exp(cumv), hot)
        gstates = jnp.concatenate(
            [
                dot3(sc, cmat, NN) + dot3(xs * to_end, adj, NT),
                dot3(sc.T, bmat, NN) + dot3(g_scaled, state, NT),
            ],
            axis=1,
        )
        gsact = gstates * (ssg * (1.0 + sactv * (1.0 - ssg)))
        gact = (step_wide * u + skip * g) * (sg * (1.0 + actv * (1.0 - sg)))
        u_ref[...] = gact
        sext[Q + HALO :, :] = gsact
        small_a[4:5, :] = small_a[4:5, :] + jnp.sum(gact, axis=0, keepdims=True)
        small_b[4:5, :] = small_b[4:5, :] + jnp.sum(gsact, axis=0, keepdims=True)
        direct = gather(x * u, hot)
        flow = gather(g * (y[...] - skip * x), hot) - stepv * direct
        ends_heads = gather(jnp.broadcast_to(ends, (HALO, ends.shape[1])), hot)[:1]
        da = tri_sum(False, flow) + ends_heads
        slope = (direct + rate * da) * sigmoid(step_pre[...] + params[7:8, LANES : 2 * LANES])
        gstep[Q:, :] = slope.astype(BF16)
        small_a[7:8, :LANES] = small_a[7:8, :LANES] + jnp.sum(
            stepv * rate * da, axis=0, keepdims=True
        )
        small_a[7:8, LANES : 2 * LANES] = small_a[7:8, LANES : 2 * LANES] + jnp.sum(
            slope, axis=0, keepdims=True
        )

    @pl.when(c == 0)
    def _():
        halo_send[...] = u_ref[:HALO, :]
        shalo_send[...] = sext[Q + HALO : Q + 2 * HALO, :]
        pl.semaphore_wait(barrier, n - 1 + jnp.where(seq > 0, 1, 0))

        @pl.when(seq > 0)
        def _():
            halo(halo_send, halo_got, 0).start()
            halo(shalo_send, shalo_got, 2).start()

    @pl.when(c == count)
    def _():
        @pl.when(seq < ns - 1)
        def _():
            halo(halo_send, halo_got, 0).wait_recv()
            halo(shalo_send, shalo_got, 2).wait_recv()
            u_ref[:HALO, :] = halo_got[...]
            sext[Q + HALO : Q + 2 * HALO, :] = shalo_got[...]

        @pl.when(seq == ns - 1)
        def _():
            u_ref[:HALO, :] = jnp.zeros((HALO, u_ref.shape[1]), F32)
            sext[Q + HALO : Q + 2 * HALO, :] = jnp.zeros((HALO, two), F32)

        @pl.when(seq > 0)
        def _():
            halo(halo_send, halo_got, 0).wait_send()
            halo(shalo_send, shalo_got, 2).wait_send()

    @pl.when(c >= 1)
    def _():
        gext[Q:, :] = u_ref[:HALO, :]
        sext[Q : Q + HALO, :] = sext[Q + HALO : Q + 2 * HALO, :]
        pext[:HALO, :] = jnp.where(c == 1, pre_halo[...], pre_prev[...])
        pext[HALO:, :] = pre[...]
        spext[:HALO, :] = jnp.where(c == 1, spre_halo[...], spre_prev[...])
        spext[HALO:, :] = spre[...]

        def conv_back(ext, ext_pre, taps_at, size, sums):
            g = ext[:Q, :]
            total = params[taps_at + taps - 1 : taps_at + taps, :size] * g
            for k in range(taps - 1):
                start = taps - 1 - k
                total = total + params[taps_at + k : taps_at + k + 1, :size] * ext[start : start + Q, :]
            for k in range(taps):
                start = HALO - taps + 1 + k
                sums[k : k + 1, :] = sums[k : k + 1, :] + jnp.sum(
                    g * ext_pre[start : start + Q, :], axis=0, keepdims=True
                )
            return total

        inner = gext.shape[1]
        gin_o[:, :inner] = conv_back(gext, pext, 0, inner, small_a).astype(BF16)
        gin_o[:, inner:] = gstep[:Q, :]
        psend[chunk_rows(c - 1), :] = conv_back(sext, spext, 8, two, small_b)

        @pl.when((c - 1) % n != me)
        def _():
            to_owner(c - 1).start()

    @pl.when(c < count)
    def _():
        gext[:Q, :] = u_ref[...]
        gstep[:Q, :] = gstep[Q:, :]
        sext[:Q, :] = sext[Q + HALO :, :]

    for g in range(groups):

        @pl.when(c == min((g + 1) * n + 2, total_chunks))
        def _():
            own = chunk_rows(g * n + me)
            total = psend[own, :]
            for k in range(1, n):
                j = (me + k) % n
                from_other(j, g).wait_recv()
                total = total + pgot[j, g * Q : (g + 1) * Q, :]
            gsb_o[own, :] = total.astype(BF16)
            for k in range(1, n):
                give(k, g, False).start()

    @pl.when(c == count)
    def _():
        for g in range(groups):
            for k in range(1, n):
                give(k, g, True).wait_recv()
        gsb_out[...] = gsb_o[...]
        for g in range(groups):
            for k in range(1, n):
                give(k, g, False).wait_send()
        for k in range(total_chunks):

            @pl.when(k % n != me)
            def _():
                to_owner(k).wait_send()


def matmul_low(left, right):
    return jnp.dot(left, right, preferred_element_type=F32)


def times_transposed(left, right):
    return dg(left, right, NT)


def transposed_times(left, right):
    return dg(left, right, TN)


def on_device(
    hidden,
    in_gain,
    proj_gate,
    proj_input,
    proj_states,
    proj_step,
    conv_input,
    conv_input_bias,
    conv_states,
    conv_states_bias,
    step_bias,
    decay_log,
    skip_gain,
    gate_gain,
    proj_output,
    cotangent,
):
    seg_count = lax.axis_size("seq")
    seg_index = lax.axis_index("seq")
    head_index = lax.axis_index("head")
    is_first = seg_index == 0
    tokens, width = hidden.shape
    heads = proj_step.shape[1]
    inner = proj_gate.shape[1]
    state_size = conv_states.shape[1] // 2
    head_dim = inner // heads
    row_width = proj_states.shape[0]
    count = tokens // Q
    gain_full = in_gain.astype(F32)

    def pad_heads(value):
        return jnp.pad(value, [(0, 0)] * (value.ndim - 1) + [(0, LANES - heads)])

    n, ns = lax.axis_size("head"), seg_count

    def turned(value, k):
        return lax.ppermute(value, "head", [(i, (i + k) % n) for i in range(n)])

    pieces = [proj_states] + [turned(proj_states, k) for k in range(1, n)]
    hidden_halo = shifted(hidden[tokens - HALO :], "seq", 1)

    def norm(rows_):
        value = rows_.astype(F32)
        inv = lax.rsqrt(jnp.mean(value * value, axis=-1, keepdims=True) + EPS)
        return inv, (value * inv * gain_full[None, :]).astype(BF16)

    inv_rms, normed = norm(hidden)
    normed_halo = norm(hidden_halo)[1]
    keep = jnp.where(is_first, 0.0, 1.0)
    proj_step_wide = pad_heads(proj_step)
    input_pre = matmul_low(normed, proj_input)
    input_halo = matmul_low(normed_halo, proj_input) * keep
    gate_pre = matmul_low(normed, proj_gate)
    grad_ynorm = times_transposed(cotangent, proj_output)
    two = 2 * state_size
    flat = jnp.concatenate(
        [
            pad_heads(decay_log),
            pad_heads(step_bias),
            pad_heads(skip_gain),
            conv_input_bias.astype(F32),
            gate_gain.astype(F32),
            conv_states_bias.astype(F32),
        ]
    )
    flat = jnp.pad(flat, (0, -flat.shape[0] % 1024))
    vec = flat.reshape(-1, LANES)
    onehot = jnp.asarray(
        np.arange(LANES)[:, None] == np.arange(inner)[None, :] // head_dim, dtype=BF16
    )
    hot = (onehot, whole((LANES, inner)))
    state_rows = pl.BlockSpec((state_size, inner), lambda c: (c, 0))
    packed_shape = (state_size + HALO, inner)
    (
        act, sact, states_pre, states_halo, step_pre, step, cum, cumt, sin, packed, total_log,
        before_log, params,
    ) = call(
        functools.partial(states_kernel, n),
        (count,),
        [
            (input_pre, rows(inner)),
            (input_pre, before(inner)),
            (input_halo, whole((HALO, inner))),
            (normed, rows(width)),
            (normed_halo, whole((HALO, width))),
            (proj_step_wide, whole((width, LANES))),
            (vec, whole(vec.shape)),
            (conv_input, whole(conv_input.shape)),
            (conv_states, whole(conv_states.shape)),
            hot,
        ]
        + [(piece, whole(piece.shape)) for piece in pieces],
        [
            (sds((tokens, inner)), rows(inner)),
            (sds((tokens, two)), rows(two)),
            (sds((tokens, two)), rows(two)),
            (sds((HALO, two)), whole((HALO, two))),
            (sds((tokens, LANES)), rows(LANES)),
            (sds((tokens, LANES)), rows(LANES)),
            (sds((tokens, LANES)), rows(LANES)),
            (sds((tokens, LANES)), rows(LANES)),
            (sds((count * state_size, inner)), state_rows),
            (sds(packed_shape), whole(packed_shape)),
            (sds((1, LANES)), whole((1, LANES))),
            (sds((count, 1, LANES)), pl.BlockSpec((None, 1, LANES), lambda c: (c, 0, 0))),
            (sds((16, inner)), whole((16, inner))),
        ],
        scratch=[
            pltpu.VMEM((Q + HALO, inner), F32),
            pltpu.VMEM((Q + HALO, two), F32),
            pltpu.VMEM((state_size, inner), F32),
            pltpu.VMEM((1, LANES), F32),
            pltpu.VMEM((width, two), BF16),
        ],
        flops=10 * tokens * inner * state_size,
    )
    par = (params, whole((16, inner)))
    packed, gate_pre, grad_ynorm = lax.optimization_barrier((packed, gate_pre, grad_ynorm))
    yloc, incoming = call(
        functools.partial(intra_kernel, ns),
        (count,),
        [
            (act, rows(inner)),
            (sact, rows(two)),
            (step, rows(LANES)),
            (cum, rows(LANES)),
            (cumt, rows(LANES)),
            par,
            hot,
            (packed, whole(packed_shape)),
        ],
        [
            (sds((tokens, inner)), rows(inner)),
            (sds((state_size, inner)), whole((state_size, inner))),
        ],
        scratch=[pltpu.VMEM((Q, inner), F32), pltpu.VMEM((state_size, inner), F32)]
        + swap_scratch(ns, (state_size, inner)),
        flops=12 * tokens * inner * Q,
        collective=5,
    )

    def both(i):
        return jnp.where(i < count, i, 2 * count - 1 - i)

    def fore(i):
        return jnp.minimum(i, count - 1)

    def aft(i):
        return jnp.minimum(2 * count - 1 - i, count - 1)

    def at(size, which, height=Q):
        return pl.BlockSpec((height, size), lambda i: (which(i), 0))

    y, ynorm, grad_gate_pre, grad_ssd, dout, packed_back, grad_rows = call(
        functools.partial(middle_kernel, n),
        (2 * count,),
        [
            (yloc, at(inner, fore)),
            (act, at(inner, aft)),
            (sact, at(two, both)),
            (cum, at(LANES, both)),
            (sin, at(inner, fore, state_size)),
            (before_log, pl.BlockSpec((None, 1, LANES), lambda i: (fore(i), 0, 0))),
            (total_log, whole((1, LANES))),
            (incoming, whole((state_size, inner))),
            (gate_pre, at(inner, both)),
            (grad_ynorm, at(inner, both)),
            par,
            hot,
        ],
        [
            (sds((tokens, inner)), at(inner, fore)),
            (sds((tokens, inner), BF16), at(inner, aft)),
            (sds((tokens, inner), BF16), at(inner, aft)),
            (sds((tokens, inner)), at(inner, aft)),
            (sds((count * state_size, inner)), at(inner, aft, state_size)),
            (sds(packed_shape), whole(packed_shape)),
            (sds((HALO, inner)), whole((HALO, inner))),
        ],
        scratch=[
            pltpu.VMEM((tokens, inner), F32),
            pltpu.VMEM((HALO, tokens), F32),
            pltpu.VMEM((n, HALO, tokens), F32),
            pltpu.VMEM((state_size, inner), F32),
            pltpu.SemaphoreType.DMA((n,)),
            pltpu.SemaphoreType.DMA((n,)),
        ],
        flops=12 * tokens * inner * state_size,
        collective=3,
    )
    local_proj_output = transposed_times(cotangent, ynorm)
    local_proj_gate = transposed_times(normed, grad_gate_pre)
    own_code, later = reduce_over_heads(
        [(ynorm, proj_output)], [NN], 1, packed=packed_back
    )
    codes = [own_code]
    for k in range(1, n):
        codes.append(turned(own_code, k))
    summed_out = lax.psum_scatter(
        local_proj_output, "seq", scatter_dimension=0, tiled=True
    )
    grad_proj_output = pl.pallas_call(
        turn_kernel, out_shape=sds(summed_out.shape[::-1]), name="turn"
    )(summed_out)
    grad_proj_gate = lax.psum_scatter(
        local_proj_gate, "seq", scatter_dimension=0, tiled=True
    )

    def held(size, height=Q):
        return pl.BlockSpec((height, size), lambda c: (jnp.minimum(c, count - 1), 0))

    def prior(size):
        return pl.BlockSpec((Q, size), lambda c: (jnp.maximum(c - 1, 0), 0))

    def prior_edge(size):
        return pl.BlockSpec(
            (HALO, size), lambda c: (jnp.maximum((c - 1) * (Q // HALO) - 1, 0), 0)
        )

    dma = pltpu.SemaphoreType.DMA
    groups = count // n
    grad_in_b, grad_states_b, small_a, small_b = call(
        functools.partial(back_kernel, n, ns),
        (count + 1,),
        [
            (act, held(inner)),
            (sact, held(two)),
            (y, held(inner)),
            (grad_ssd, held(inner)),
            (step, held(LANES)),
            (step_pre, held(LANES)),
            (cum, held(LANES)),
            (cumt, held(LANES)),
            (sin, held(inner, state_size)),
            (dout, held(inner, state_size)),
            (
                before_log,
                pl.BlockSpec((None, 1, LANES), lambda c: (jnp.minimum(c, count - 1), 0, 0)),
            ),
            (total_log, whole((1, LANES))),
            (incoming, whole((state_size, inner))),
            (later, whole((state_size, inner))),
            par,
            hot,
            (grad_rows, whole((HALO, inner))),
            (input_pre, prior(inner)),
            (input_pre, prior_edge(inner)),
            (input_halo, whole((HALO, inner))),
            (states_pre, prior(two)),
            (states_pre, prior_edge(two)),
            (states_halo, whole((HALO, two))),
        ],
        [
            (sds((tokens, inner + LANES), BF16), prior(inner + LANES)),
            (sds((tokens, two), BF16), whole((tokens, two))),
            (sds((16, inner)), whole((16, inner))),
            (sds((HALO, two)), whole((HALO, two))),
        ],
        scratch=[
            pltpu.VMEM((tokens, two), BF16),
            pltpu.VMEM((2 * Q, LANES), BF16),
            pltpu.VMEM((Q, inner), F32),
            pltpu.VMEM((Q, inner), F32),
            pltpu.VMEM((Q, Q), F32),
            pltpu.VMEM((Q + HALO, inner), F32),
            pltpu.VMEM((2 * Q + HALO, two), F32),
            pltpu.VMEM((Q + HALO, inner), F32),
            pltpu.VMEM((Q + HALO, two), F32),
            pltpu.VMEM((HALO, inner), F32),
            pltpu.VMEM((HALO, inner), F32),
            pltpu.VMEM((HALO, two), F32),
            pltpu.VMEM((HALO, two), F32),
            pltpu.VMEM((tokens, two), F32),
            pltpu.VMEM((n, groups * Q, two), F32),
            dma((4,)),
            dma((count,)),
            dma((n, groups)),
            dma((n, groups)),
            dma((n, groups)),
        ],
        flops=40 * tokens * inner * Q,
        collective=4,
    )
    stream = tokens // STREAMS
    result = call(
        functools.partial(result_kernel, n),
        (STREAMS,),
        [
            (code, pl.BlockSpec((stream // n, width + LANES), lambda c: (c, 0)))
            for code in codes
        ]
        + [(hidden, pl.BlockSpec((stream, width), lambda c: (c, 0)))],
        [(sds((tokens, width)), pl.BlockSpec((stream, width), lambda c: (c, 0)))],
        flops=20 * tokens * width,
    )[0]
    row_start = head_index * row_width
    own_states = lax.dynamic_update_slice_in_dim(
        jnp.zeros((width, two), BF16), proj_states, row_start, 0
    )
    normed_rows = lax.dynamic_slice_in_dim(normed, row_start, row_width, 1)
    local_proj_in = transposed_times(normed, grad_in_b)
    local_proj_states = transposed_times(grad_states_b, normed_rows)
    summed_in = lax.psum_scatter(local_proj_in, "seq", scatter_dimension=0, tiled=True)
    grad_code, sum_a, sum_b, grad_proj_states = reduce_over_heads(
        [
            (grad_gate_pre, proj_gate),
            (grad_in_b, proj_input),
            (grad_in_b, proj_step_wide),
            (grad_states_b, own_states),
        ],
        [NT] * 4,
        2,
        (hidden, inv_rms, small_a, small_b, local_proj_states),
        cols=(None, (0, inner), (inner, inner + LANES), None),
    )
    grad_hidden = call(
        hidden_kernel,
        (count,),
        [
            (grad_code, rows(width + LANES)),
            (hidden, rows(width)),
            (cotangent, rows(width)),
            (inv_rms, rows(1)),
            (gain_full[None, :], whole((1, width))),
        ],
        [(sds((tokens, width)), rows(width))],
        flops=20 * tokens * width,
    )[0]
    return (
        result,
        grad_hidden,
        sum_b[0],
        grad_proj_gate,
        summed_in[:, :inner],
        grad_proj_states.T,
        summed_in[:, inner : inner + heads],
        sum_a[:TAPS],
        sum_a[4],
        sum_b[8 : 8 + TAPS, :two],
        sum_b[12, :two],
        sum_a[7, LANES : LANES + heads],
        sum_a[7, :heads],
        jnp.sum(sum_a[6].reshape(heads, head_dim), axis=1),
        sum_a[5],
        grad_proj_output,
    )


def solution(mesh):
    in_specs = (
        P("seq", None),
        P(),
        P(None, "head"),
        P(None, "head"),
        P("head", None),
        P(None, "head"),
        P(None, "head"),
        P("head"),
        P(),
        P(),
        P("head"),
        P("head"),
        P("head"),
        P("head"),
        P("head", None),
        P("seq", None),
    )
    out_specs = (
        P("seq", None),
        P("seq", None),
        P(),
        P("seq", "head"),
        P("seq", "head"),
        P("head", "seq"),
        P("seq", "head"),
        P(None, "head"),
        P("head"),
        P(),
        P(),
        P("head"),
        P("head"),
        P("head"),
        P("head"),
        P("head", "seq"),
    )

    return jax.shard_map(
        on_device, mesh=mesh, in_specs=in_specs, out_specs=out_specs, check_vma=False
    )
```

time: 1450 us -> 467 us (0.32)
  waiting for transfers between devices: 654 us -> 0.07 us
  Pallas kernels: 0 us -> 368 us
  local copies, waits for them, and re-layouts: 315 us -> 20.9 us
  matrix products: 205 us -> 36.3 us
  other arithmetic: 173 us -> 5.69 us
  blocking collectives: 59.6 us -> 0 us
    psum x3 -> x0, waiting for transfers between devices: 479 us -> none  [the longest x1 428 us: on_device(): branch = lax.psum(matmul_low(ynorm, proj_output), 'head')]
    pallas_call x0 -> x9, Pallas kernels: none -> 368 us  [the longest x2 230 us: reduce_over_heads(): pl.pallas_call(functools.partial(reduce_kernel, n, ns, dims, cols or [Non...]
    dynamic_update_slice x44 -> x1, local copies, waits for them, and re-layouts: 172 us -> 0.02 us  [on_device(): lax.dynamic_update_slice_in_dim(jnp.zeros((width, two), BF16), proj_state...]
    reduce_scatter x4 -> x3, waiting for transfers between devices: 168 us -> 0.01 us  [the longest x1 0.01 us: on_device(): lax.psum_scatter(local_proj_output, 'seq', scatter_dimension=0, tiled=True)]
    dot_general x77 -> x8, matrix products: 203 us -> 36.3 us  [the longest x5 25 us: dg(): return lax.dot_general(left, right, dims, preferred_element_type=F32)]
    psum x3 -> x0, blocking collectives: 45.5 us -> none  [the longest x1 24.9 us: on_device(): lax.psum((local_in_gain, grad_conv_input, grad_conv_input_bias, grad_conv...]
    another operation x62 -> x0, other arithmetic: 36.9 us -> none
    reduce_sum x17 -> x3, other arithmetic: 35.7 us -> 4.06 us  [the longest x2 3.43 us: norm(): inv = lax.rsqrt(jnp.mean(value * value, axis=-1, keepdims=True) + EPS)]
  transfers between devices with their start and end apart: 14 -> 10, of which waited for: 10 -> 0; matrix products, arithmetic and copies ran while one was open for 14% -> 12% of each run, Pallas kernels for 0% -> 66%
where the time goes in v1:
time: 467 us; the launch traced here: 459 us
  Pallas kernels  368 us (79%)
  matrix products  36.3 us (8%)
  local copies, waits for them, and re-layouts  20.9 us (4%)
  starting transfers between devices  14.4 us (3%)
  between operations  14.3 us (3%)
  other arithmetic  5.69 us (1%)
    pallas_call x2, Pallas kernels, reduce_over_heads(): pl.pallas_call(functools.partial(reduce_kernel, n, ns, dims, cols or [Non...  230 us
    pallas_call x6, Pallas kernels, call(): pl.pallas_call(kernel, grid=grid, in_specs=in_specs, out_specs=[spec for...  135 us
    dot_general x5, matrix products, dg(): return lax.dot_general(left, right, dims, preferred_element_type=F32)  25 us
    ppermute x6, starting transfers between devices, turned(): return lax.ppermute(value, 'head', [(i, (i + k) % n) for i in range(n)])  12 us
    dot_general x3, matrix products, matmul_low(): return jnp.dot(left, right, preferred_element_type=F32)  11.2 us
  transfers between devices with their start and end apart: 10, of which 0 were waited for; matrix products, arithmetic and copies ran while one was open for 12% of the time, Pallas kernels for 66%

profile of v1, /device:TPU:0, one launch (start us, length us, event | category | flops | bytes accessed | tf_op | source)
XLA Modules:
  0.0 459.4 jit_solution(9451864967858200939)
XLA Ops:
  7.2 0.0 copy-start
  7.2 0.0 reduce-scatter.8.cloned.1.call-start
  7.2 3.1 collective-permute-start.1
  10.4 2.6 collective-permute-start.2
  12.9 1.3 collective-permute-start.3
  14.3 1.3 slice.36
  15.6 1.9 collective-permute-start
  17.5 2.6 fusion
  20.2 0.0 copy-start.4
  20.2 0.8 fusion.2.normed
  21.0 0.9 copy-done.4
  21.8 4.3 fusion.9.pre.pre_prev
  26.1 0.0 copy-start.16
  26.1 0.0 copy-start.10
  26.1 0.0 copy-start.11
  26.1 0.0 copy-start.17
  26.2 0.0 copy-start.3
  26.2 0.0 copy-start.12
  26.2 4.3 fusion.10.gate
  30.6 4.3 fusion.11.gyn
  34.9 0.6 pad_bitcast_fusion.vec
  35.5 1.0 copy.37
  36.6 0.8 pad.18.step_w.refs_6_
  37.5 0.9 fusion.5
  38.3 0.8 fusion.7.normed_halo
  39.1 2.7 convolution_multiply_fusion.pre_halo
  41.9 14.5 %shard_map.288 = (f32[1024,768]{1,0:T(8,128)}, f32[1024,256]{1,0:T(8,128)}, f32[1024,256]{1,0:T(8,128)}, f32[8,256]{1,0:T(8,128)}, f32[1024,128]{1,0:T(8,128)}, ...) custom-call(f32[1024,768]{1,0:T(8,128)} %fusion.9.pre.pre_prev, ...), custom_call_target="tpu_custom_call" | custom-call | flops 1006632960 | bytes 21848576 | tf_op jit(solution)/shard_map/pallas_call | solution.py:71
  56.3 19.7 %shard_map.289 = (f32[1024,768]{1,0:T(8,128)}, f32[128,768]{1,0:T(8,128)}) custom-call(f32[1024,768]{1,0:T(8,128)} %get-tuple-element.51.act, f32[1024,256]{1,0:T(8,128)} %get-tuple-element.52.sact, f32[1024,128]{1,0:T(8,128)} %get-tuple-element.53.step, f32[1024,128]{1,0:T(8,128)} %get-tuple-element.54.cum, f32[1024,128]{1,0:T(8,128)} %get-tuple-element.55.cumt, ...), custom_call_target="tpu_custom_call" | custom-call | flops 1207959552 | bytes 9969664 | tf_op jit(solution)/shard_map/pallas_call | solution.py:71
  76.1 29.7 %shard_map.290 = (f32[1024,768]{1,0:T(8,128)}, bf16[1024,768]{1,0:T(8,128)(2,1)}, bf16[1024,768]{1,0:T(8,128)(2,1)}, f32[1024,768]{1,0:T(8,128)}, f32[1024,768]{...) custom-call(f32[1024,768]{1,0:T(8,128)} %get-tuple-element.59.yloc, f32[1024,768]{1,0:T(8,128)} %get-tuple-element.51.act, ...), custom_call_target="tpu_custom_call" | custom-call | flops 1207959552 | bytes 30970368 | tf_op jit(solution)/shard_map/pallas_call | solution.py:71
  105.7 5.8 %convolution_bitcast_fusion = f32[1536,768]{1,0:T(8,128)} fusion(bf16[1024,768]{1,0:T(8,128)(2,1)} %get-tuple-element.66.refs_0_, bf16[1024,1536]{1,0:T(8,128)(2,1)S(1)} %copy-done.3), kind=kOutput, calls=%fused_computation.5 | convolution fusion | flops 2415919104 | bytes 9437184 | tf_op jit(solution)/shard_map/dot_general | solution.py:29
  111.6 0.0 reduce-scatter.8.cloned.1.call-update
  111.6 0.0 reduce-scatter.6.cloned.1.call-start
  111.6 67.5 %scatter_heads.1 = (bf16[256,1664]{1,0:T(8,128)(2,1)}, f32[128,768]{1,0:T(8,128)}) custom-call(bf16[1024,768]{1,0:T(8,128)(2,1)} %get-tuple-element.66.refs_0_, bf16[768,1536]{1,0:T(8,128)(2,1)} %refs_1_.1, f32[136,768]{1,0:T(8,128)} %get-tuple-element.67.refs_2_), custom_call_target="tpu_custom_call" | custom-call | flops 2415919104 | bytes 157286400 | tf_op jit(solution)/shard_map/scatter_heads/pallas_call | solution.py:654
  179.1 0.0 copy-start.2
  179.1 55.2 %shard_map.292 = (bf16[1024,896]{1,0:T(8,128)(2,1)}, bf16[1024,256]{1,0:T(8,128)(2,1)}, f32[16,768]{1,0:T(8,128)}, f32[8,256]{1,0:T(8,128)}) custom-call(f32[1024,768]{1,0:T(8,128)} %get-tuple-element.51.act, f32[1024,256]{1,0:T(8,128)} %get-tuple-element.52.sact, f32[1024,768]{1,0:T(8,128)} %get-tuple-element.70.y, f32[1024,768]{1,0:T(8,128)} %get-tuple-element.71.gssd, ...), custom_call_target="tpu_custom_call" | custom-call | flops 4026531840 | bytes 30773760 | tf_op jit(solution)/shard_map/pallas_call | solution.py:71
  234.3 6.8 %fusion.13 = f32[1536,896]{1,0:T(8,128)} fusion(bf16[1024,1536]{1,0:T(8,128)(2,1)S(1)} %copy-done.2, bf16[1024,896]{1,0:T(8,128)(2,1)} %get-tuple-element.78.refs_1_.refs_2_), kind=kOutput, calls=%fused_computation.35 | convolution fusion | flops 2818572288 | bytes 10485760 | tf_op jit(solution)/shard_map/dot_general | solution.py:29
  241.2 0.0 reduce-scatter.6.cloned.1.call-update
  241.2 0.4 reduce-scatter.4.cloned.1.call-start
  241.6 5.7 %fusion.12 = f32[1536,768]{1,0:T(8,128)} fusion(bf16[1024,1536]{1,0:T(8,128)(2,1)S(1)} %copy-done.2, bf16[1024,768]{1,0:T(8,128)(2,1)} %get-tuple-element.69.refs_0_), kind=kOutput, calls=%fused_computation.34 | convolution fusion | flops 2415919104 | bytes 9437184 | tf_op jit(solution)/shard_map/dot_general | solution.py:29
  247.4 0.0 reduce-scatter.4.cloned.1.call-update
  247.4 0.6 broadcast_in_dim.5.gain
  248.0 1.0 copy.38.refs_9_.inv
  249.0 0.1 broadcast_in_dim.4
  249.1 1.3 collective-permute-start.4
  250.5 0.8 collective-permute-start.5
  251.2 2.8 collective-permute-start.6
  254.1 2.3 fusion.3.refs_12_
  256.4 162.6 %reduce_heads.1 = (bf16[1024,1664]{1,0:T(8,128)(2,1)}, f32[16,768]{1,0:T(8,128)}, f32[16,1536]{1,0:T(8,128)}, f32[32,384]{1,0:T(8,128)}) custom-call(bf16[1024,768]{1,0:T(8,128)(2,1)} %get-tuple-element.69.refs_0_, bf16[1024,896]{1,0:T(8,128)(2,1)} %get-tuple-element.78.refs_1_.refs_2_, bf16[1024,896]{1,0:T(8,128)(2,1)} %get-tuple-element.78.refs_1_.refs_2_, ...), custom_call_target="tpu_custom_call" | custom-call | flops 8858370048 | bytes 157286400 | tf_op jit(solution)/shard_map/reduce_heads/pallas_call | solution.py:654
  419.0 1.3 slice.42
  420.3 1.3 slice.43
  421.5 1.3 slice.40
  422.9 1.5 slice_reduce_fusion.1
  424.3 0.1 reshape_squeeze.3
  424.4 0.6 reduce_sum.29
  425.0 9.9 %shard_map.293 = f32[1024,1536]{1,0:T(8,128)} custom-call(bf16[1024,1664]{1,0:T(8,128)(2,1)} %get-tuple-element.82.code, bf16[1024,1536]{1,0:T(8,128)(2,1)} %hidden.1, bf16[1024,1536]{1,0:T(8,128)(2,1)} %cotangent.1, f32[1024,1]{1,0:T(8,128)} %copy.38.refs_9_.inv, f32[1,1536]{1,0:T(1,128)} %broadcast_in_dim.5.gain), custom_call_target="tpu_custom_call" | custom-call | flops 31457280 | bytes 16001024 | tf_op jit(solution)/shard_map/pallas_call | solution.py:71
  435.0 1.4 slice_reduce_fusion
  436.4 1.2 slice_bitcast_fusion
  437.6 6.5 %shard_map.291 = f32[1024,1536]{1,0:T(8,128)} custom-call(bf16[256,1664]{1,0:T(8,128)(2,1)} %get-tuple-element.68.refs_0_, bf16[256,1664]{1,0:T(8,128)(2,1)} %collective-permute-done.4.refs_1_, bf16[256,1664]{1,0:T(8,128)(2,1)} %collective-permute-done.5.refs_2_, bf16[256,1664]{1,0:T(8,128)(2,1)} %collective-permute-done.6.refs_3_, bf16[1024,1536]{1,0:T(8,128)(2,1)} %hidden.1), custom_call_target="tpu_custom_call" | custom-call | flops 31457280 | bytes 12845056 | tf_op jit(solution)/shard_map/pallas_call | solution.py:71
  444.1 2.2 turn.1
  446.3 2.2 copy.42
  448.5 0.9 slice.49
  449.4 0.7 copy.41
  450.1 1.9 slice.48
  452.0 0.6 copy.52
  (47 shorter events, 0.2 us)
Async XLA Ops:
  7.2 13.0 %copy-start = (bf16[1024,1536]{1,0:T(8,128)(2,1)S(1)}, bf16[1024,1536]{1,0:T(8,128)(2,1)}, u32[]{:S(2)}) copy-start(bf16[1024,1536]{1,0:T(8,128)(2,1)} %hidden.1) | copy-start | bytes 9437188
  7.2 12.9 %copy-start.9 = (bf16[1536]{0:T(1024)(128)(2,1)S(1)}, bf16[1536]{0:T(1024)(128)(2,1)}, u32[]{:S(2)}) copy-start(bf16[1536]{0:T(1024)(128)(2,1)} %param.18) | copy-start | bytes 9220
  7.2 436.9 %reduce-scatter.8.cloned.1.call-start = ((), (), s32[]{:S(2)}) async-start(), calls=%async_computation.5 | async-start | bytes 5308416 | tf_op jit(solution)/shard_map/reduce_scatter | solution.py:1270
  7.2 34.6 %collective-permute-start.1 = (bf16[384,256]{1,0:T(8,128)(2,1)}, bf16[384,256]{1,0:T(8,128)(2,1)}, u32[]{:S(2)}, u32[]{:S(2)}) collective-permute-start(bf16[384,256]{1,0:T(8,128)(2,1)} %refs_0_.1), channel_id=1, source_target_pairs={{0,1},{1,2},{2,3},{3,0},{4,5},{5,6},{6,7},{7,4},{8,9},{9,10},{10,1... | collective-permute-start | bytes 589832 | tf_op jit(solution)/shard_map/ppermute | solution.py:1108
  10.4 31.5 %collective-permute-start.2 = (bf16[384,256]{1,0:T(8,128)(2,1)}, bf16[384,256]{1,0:T(8,128)(2,1)}, u32[]{:S(2)}, u32[]{:S(2)}) collective-permute-start(bf16[384,256]{1,0:T(8,128)(2,1)} %refs_0_.1), channel_id=1, source_target_pairs={{0,2},{1,3},{2,0},{3,1},{4,6},{5,7},{6,4},{7,5},{8,10},{9,11},{10,... | collective-permute-start | bytes 589832 | tf_op jit(solution)/shard_map/ppermute | solution.py:1108
  12.9 28.9 %collective-permute-start.3 = (bf16[384,256]{1,0:T(8,128)(2,1)}, bf16[384,256]{1,0:T(8,128)(2,1)}, u32[]{:S(2)}, u32[]{:S(2)}) collective-permute-start(bf16[384,256]{1,0:T(8,128)(2,1)} %refs_0_.1), channel_id=1, source_target_pairs={{0,3},{1,0},{2,1},{3,2},{4,7},{5,4},{6,5},{7,6},{8,11},{9,8},{10,9... | collective-permute-start | bytes 589832 | tf_op jit(solution)/shard_map/ppermute | solution.py:1108
  15.6 21.8 %collective-permute-start = (bf16[8,1536]{1,0:T(8,128)(2,1)}, bf16[8,1536]{1,0:T(8,128)(2,1)}, u32[]{:S(2)}, u32[]{:S(2)}) collective-permute-start(bf16[8,1536]{1,0:T(8,128)(2,1)} %slice.36), channel_id=1, source_target_pairs={{0,4},{4,8},{8,12},{12,16},{16,20},{20,24},{24,28},{1,5},{5,9},{9,... | collective-permute-start | bytes 73736 | tf_op jit(solution)/shard_map/ppermute | solution.py:63
  20.2 1.7 copy-start.4
  21.8 4.3 copy-start.1
  21.8 4.3 copy-start.13
  26.1 4.4 copy-start.14
  26.1 4.4 copy-start.15
  26.1 4.4 copy-start.16
  26.1 4.4 copy-start.10
  26.1 4.4 copy-start.11
  26.1 4.4 copy-start.17
  26.2 4.4 copy-start.3
  26.2 4.4 copy-start.12
  39.1 2.7 copy-start.7
  111.6 336.9 %reduce-scatter.6.cloned.1.call-start = ((), (), s32[]{:S(2)}) async-start(), calls=%async_computation.4 | async-start | bytes 6193152 | tf_op jit(solution)/shard_map/reduce_scatter | solution.py:1374
  179.1 55.2 %copy-start.2 = (bf16[1024,1536]{1,0:T(8,128)(2,1)S(1)}, bf16[1024,1536]{1,0:T(8,128)(2,1)}, u32[]{:S(2)}) copy-start(bf16[1024,1536]{1,0:T(8,128)(2,1)} %copy-done.1) | copy-start | bytes 9437188
  241.2 210.8 %reduce-scatter.4.cloned.1.call-start = ((), (), s32[]{:S(2)}) async-start(), calls=%async_computation.3 | async-start | bytes 5308416 | tf_op jit(solution)/shard_map/reduce_scatter | solution.py:1276
  247.4 1.7 copy-start.6
  249.1 7.2 %copy-start.5 = (bf16[1536,256]{1,0:T(8,128)(2,1)}, bf16[1536,256]{1,0:T(8,128)(2,1)S(1)}, u32[]{:S(2)}) copy-start(bf16[1536,256]{1,0:T(8,128)(2,1)S(1)} %constant_dynamic-update-slice_fusion.6.refs_7_) | copy-start | bytes 2359300
  249.1 188.5 %collective-permute-start.4 = (bf16[256,1664]{1,0:T(8,128)(2,1)}, bf16[256,1664]{1,0:T(8,128)(2,1)}, u32[]{:S(2)}, u32[]{:S(2)}) collective-permute-start(bf16[256,1664]{1,0:T(8,128)(2,1)} %get-tuple-element.68.refs_0_), channel_id=1, source_target_pairs={{0,1},{1,2},{2,3},{3,0},{4,5},{5,6},{6,7},{7,4},{8,9},{9,10},{10,1... | collective-permute-start | bytes 2555912 | tf_op jit(solution)/shard_map/ppermute | solution.py:1108
  250.5 187.1 %collective-permute-start.5 = (bf16[256,1664]{1,0:T(8,128)(2,1)}, bf16[256,1664]{1,0:T(8,128)(2,1)}, u32[]{:S(2)}, u32[]{:S(2)}) collective-permute-start(bf16[256,1664]{1,0:T(8,128)(2,1)} %get-tuple-element.68.refs_0_), channel_id=1, source_target_pairs={{0,2},{1,3},{2,0},{3,1},{4,6},{5,7},{6,4},{7,5},{8,10},{9,11},{10,... | collective-permute-start | bytes 2555912 | tf_op jit(solution)/shard_map/ppermute | solution.py:1108
  251.2 186.4 %collective-permute-start.6 = (bf16[256,1664]{1,0:T(8,128)(2,1)}, bf16[256,1664]{1,0:T(8,128)(2,1)}, u32[]{:S(2)}, u32[]{:S(2)}) collective-permute-start(bf16[256,1664]{1,0:T(8,128)(2,1)} %get-tuple-element.68.refs_0_), channel_id=1, source_target_pairs={{0,3},{1,0},{2,1},{3,2},{4,7},{5,4},{6,5},{7,6},{8,11},{9,8},{10,9... | collective-permute-start | bytes 2555912 | tf_op jit(solution)/shard_map/ppermute | solution.py:1108
  444.1 7.9 %copy-start.8 = (f32[32,384]{1,0:T(8,128)S(1)}, f32[32,384]{1,0:T(8,128)}, u32[]{:S(2)}) copy-start(f32[32,384]{1,0:T(8,128)} %get-tuple-element.84) | copy-start | bytes 147460
Sparse Core Ops, SparseCore 0:
  111.7 57.2 reduce-scatter.7
  241.3 62.3 reduce-scatter.5
  307.8 53.7 reduce-scatter.3

commit v2 on v1

--- a/solution.py
+++ b/solution.py
@@ -357,40 +357,172 @@
     ]
 
 
-def reduce_kernel(n, ns, dims, cols, with_sums, *refs):
+def put(ref, where, value):
+    code, scale = encode(value)
+    width = value.shape[1]
+    ref[where, :width] = code
+    ref[where, width:] = scale
+
+
+def chain_scratch(tokens, width, n):
+    coded = pltpu.VMEM((tokens, width + LANES), BF16)
+    return [pltpu.VMEM((tokens, width), F32), coded, coded, coded] + [
+        pltpu.SemaphoreType.DMA((STREAMS, n))
+    ] * 6
+
+
+def chains(n, all_ref, part, code, got_r, got_l, s_sem, rr_sem, rl_sem, ar_sem, al_sem, ag_sem):
+    me = lax.axis_index("head")
+    tokens, width = part.shape
+    span = tokens // STREAMS
+    rows_own = span // n
+    has_right, has_left = me < n - 1, me > 0
+
+    def at(d, h):
+        return pl.ds(pl.multiple_of(h * span + d * rows_own, rows_own), rows_own)
+
+    def step(d, h, right):
+        return pltpu.make_async_remote_copy(
+            src_ref=code.at[at(d, h)],
+            dst_ref=(got_r if right else got_l).at[at(d, h)],
+            send_sem=s_sem.at[h, d],
+            recv_sem=(rr_sem if right else rl_sem).at[h, d],
+            device_id={"head": me + 1 if right else me - 1},
+            device_id_type=MESH_ID,
+        )
+
+    def hand_on(b, h, right):
+        return pltpu.make_async_remote_copy(
+            src_ref=all_ref.at[at(b, h)],
+            dst_ref=all_ref.at[at(b, h)],
+            send_sem=(ar_sem if right else al_sem).at[h, b],
+            recv_sem=ag_sem.at[h, b],
+            device_id={"head": me + 1 if right else me - 1},
+            device_id_type=MESH_ID,
+        )
+
+    def chain(h, u):
+        for right in (True, False):
+            d = me + (n - 1 - u) if right else me - (n - 1 - u)
+            got = got_r if right else got_l
+            inside = d <= n - 1 if right else d >= 0
+            fed = has_left if right else has_right
+
+            @pl.when(inside & fed)
+            def _():
+                step(d, h, right).wait_recv()
+                put(code, at(d, h), part[at(d, h), :] + decode(got[at(d, h), :], width))
+                step(d, h, right).start()
+
+            @pl.when(inside & jnp.logical_not(fed))
+            def _():
+                put(code, at(d, h), part[at(d, h), :])
+                step(d, h, right).start()
+
+    def finish(h):
+        own = at(me, h)
+
+        @pl.when(has_left)
+        def _():
+            step(me, h, True).wait_recv()
+            part[own, :] = part[own, :] + decode(got_r[own, :], width)
+
+        @pl.when(has_right)
+        def _():
+            step(me, h, False).wait_recv()
+            part[own, :] = part[own, :] + decode(got_l[own, :], width)
+
+        put(all_ref, own, part[own, :])
+
+        @pl.when(has_right)
+        def _():
+            hand_on(me, h, True).start()
+
+        @pl.when(has_left)
+        def _():
+            hand_on(me, h, False).start()
+
+    def relay(h, s):
+        @pl.when(me - s >= 0)
+        def _():
+            hand_on(me - s, h, True).wait_recv()
+
+            @pl.when(has_right)
+            def _():
+                hand_on(me - s, h, True).start()
+
+        @pl.when(me + s < n)
+        def _():
+            hand_on(me + s, h, False).wait_recv()
+
+            @pl.when(has_left)
+            def _():
+                hand_on(me + s, h, False).start()
+
+    def slot(t):
+        for h in range(STREAMS):
+            u = t - GAP * h
+            if 0 <= u < n - 1:
+                chain(h, u)
+            if u == n - 1:
+                finish(h)
+            if n - 1 < u < 2 * n - 1:
+                relay(h, u - n + 1)
+
+    def drain():
+        for h in range(STREAMS):
+            for i in range(n):
+
+                @pl.when(i > me)
+                def _():
+                    step(i, h, True).wait_send()
+
+                @pl.when(i < me)
+                def _():
+                    step(i, h, False).wait_send()
+
+                @pl.when(has_right & (i <= me))
+                def _():
+                    hand_on(i, h, True).wait_send()
+
+                @pl.when(has_left & (i >= me))
+                def _():
+                    hand_on(i, h, False).wait_send()
+
+    return slot, drain
+
+
+def slots_of(n):
+    return GAP * (STREAMS - 1) + 2 * n - 1
+
+
+def greet(n, ns):
+    barrier = pltpu.get_barrier_semaphore()
+    me, seq = lax.axis_index("head"), lax.axis_index("seq")
+    for k in range(1, n):
+        pl.semaphore_signal(
+            barrier, inc=1, device_id={"head": (me + k) % n}, device_id_type=MESH_ID
+        )
+    for k in range(1, ns):
+        pl.semaphore_signal(
+            barrier, inc=1, device_id={"seq": (seq + k) % ns}, device_id_type=MESH_ID
+        )
+    return barrier
+
+
+def reduce_kernel(n, ns, dims, cols, *refs):
     terms = len(dims)
     lefts, rights = refs[:terms], refs[terms : 2 * terms]
     refs = refs[2 * terms :]
-    if with_sums:
-        hidden_ref, inv_ref, small_a, small_b, states_ref, out_ref, sum_a, sum_b, sum_s = refs[:9]
-        refs = refs[9:]
-    else:
-        packed, out_ref, later = refs[:3]
-        refs = refs[3:]
-    part, code_r, code_l, got_r, got_l, sr_sem, sl_sem, rr_sem, rl_sem, ar_sem, al_sem, ag_sem = refs[:12]
-    me = lax.axis_index("head")
-    tokens = part.shape[0]
-    width = part.shape[1]
+    hidden_ref, inv_ref, small_a, small_b, states_ref, out_ref, sum_a, sum_b, sum_s = refs[:9]
+    slot, drain = chains(n, out_ref, *refs[9:19])
+    part = refs[9]
+    got_a, got_b, got_s, got_c, mine_b = refs[19:24]
+    sa_sem, ra_sem, sb_sem, rb_sem, ss_sem, rs_sem, sc_sem, rc_sem = refs[24:]
+    me, seq = lax.axis_index("head"), lax.axis_index("seq")
+    tokens, width = part.shape
     span = tokens // STREAMS
-    rows_own = span // n
-    has_right, has_left = me < n - 1, me > 0
-
-    barrier = pltpu.get_barrier_semaphore()
-    for k in range(1, n):
-        pl.semaphore_signal(
-            barrier, inc=1, device_id={"head": (me + k) % n}, device_id_type=MESH_ID
-        )
-    seq = lax.axis_index("seq")
-    for k in range(1, ns):
-        pl.semaphore_signal(
-            barrier, inc=1, device_id={"seq": (seq + k) % ns}, device_id_type=MESH_ID
-        )
-    expected = n + ns - 2
-    if with_sums:
-        got_a, got_b, got_s, got_c, mine_b = refs[12:17]
-        sa_sem, ra_sem, sb_sem, rb_sem, ss_sem, rs_sem, sc_sem, rc_sem = refs[17:]
-    else:
-        begin, turn, end = swap_states(ns, packed, later, *refs[12:], True)
+    barrier = greet(n, ns)
 
     def to_seq(src, dst, ssem, rsem, k):
         return pltpu.make_async_remote_copy(
@@ -417,37 +549,6 @@
         own = sum_s.shape[0]
         return states_ref.at[pl.ds(pl.multiple_of(j * own, own), own)]
 
-    def at(d, h):
-        return pl.ds(pl.multiple_of(h * span + d * rows_own, rows_own), rows_own)
-
-    def step(d, h, right):
-        code, got, ssem, rsem = (
-            (code_r, got_r, sr_sem, rr_sem) if right else (code_l, got_l, sl_sem, rl_sem)
-        )
-        return pltpu.make_async_remote_copy(
-            src_ref=code.at[at(d, h)],
-            dst_ref=got.at[at(d, h)],
-            send_sem=ssem.at[h, d],
-            recv_sem=rsem.at[h, d],
-            device_id={"head": me + 1 if right else me - 1},
-            device_id_type=MESH_ID,
-        )
-
-    def hand_on(b, h, right):
-        return pltpu.make_async_remote_copy(
-            src_ref=out_ref.at[at(b, h)],
-            dst_ref=out_ref.at[at(b, h)],
-            send_sem=(ar_sem if right else al_sem).at[h, b],
-            recv_sem=ag_sem.at[h, b],
-            device_id={"head": me + 1 if right else me - 1},
-            device_id_type=MESH_ID,
-        )
-
-    def put(ref, where, value):
-        code, scale = encode(value)
-        ref[where, :width] = code
-        ref[where, width:] = scale
-
     def compute(h):
         where = pl.ds(h * span, span)
         total = None
@@ -456,204 +557,100 @@
             term = dg(value, right[...], dim)
             total = term if total is None else total + term
         part[where, :] = total
-        if with_sums:
-            seen = total * (hidden_ref[where, :].astype(F32) * inv_ref[where, :])
-            row = jnp.sum(seen, axis=0, keepdims=True)
-            mine_b[0:1, :] = row if h == 0 else mine_b[0:1, :] + row
-
-    def chain(h, u):
-        for right in (True, False):
-            d = me + (n - 1 - u) if right else me - (n - 1 - u)
-            code, got = (code_r, got_r) if right else (code_l, got_l)
-            inside = d <= n - 1 if right else d >= 0
-            fed = has_left if right else has_right
-
-            @pl.when(inside & fed)
-            def _():
-                step(d, h, right).wait_recv()
-                put(code, at(d, h), part[at(d, h), :] + decode(got[at(d, h), :], width))
-                step(d, h, right).start()
-
-            @pl.when(inside & jnp.logical_not(fed))
-            def _():
-                put(code, at(d, h), part[at(d, h), :])
-                step(d, h, right).start()
-
-    def finish(h):
-        own = at(me, h)
-
-        @pl.when(has_left)
-        def _():
-            step(me, h, True).wait_recv()
-            part[own, :] = part[own, :] + decode(got_r[own, :], width)
-
-        @pl.when(has_right)
-        def _():
-            step(me, h, False).wait_recv()
-            part[own, :] = part[own, :] + decode(got_l[own, :], width)
-
-        if not with_sums:
-            put(out_ref, pl.ds(h * rows_own, rows_own), part[own, :])
-            return
-
-        put(out_ref, own, part[own, :])
-
-        @pl.when(has_right)
-        def _():
-            hand_on(me, h, True).start()
-
-        @pl.when(has_left)
-        def _():
-            hand_on(me, h, False).start()
-
-    def relay(h, s):
-        @pl.when(me - s >= 0)
-        def _():
-            hand_on(me - s, h, True).wait_recv()
-
-            @pl.when(has_right)
-            def _():
-                hand_on(me - s, h, True).start()
-
-        @pl.when(me + s < n)
-        def _():
-            hand_on(me + s, h, False).wait_recv()
-
-            @pl.when(has_left)
-            def _():
-                hand_on(me + s, h, False).start()
-
-    for t in range(GAP * (STREAMS - 1) + 2 * n - 1):
+        seen = total * (hidden_ref[where, :].astype(F32) * inv_ref[where, :])
+        row = jnp.sum(seen, axis=0, keepdims=True)
+        mine_b[0:1, :] = row if h == 0 else mine_b[0:1, :] + row
+
+    for t in range(slots_of(n)):
         for h in range(STREAMS):
-            u = t - GAP * h
-            if u == 0:
+            if t == GAP * h:
                 compute(h)
-                if h == 0:
-                    pl.semaphore_wait(barrier, expected)
-                    if with_sums:
-                        for k in range(1, ns):
-                            to_seq(small_a, got_a, sa_sem, ra_sem, k).start()
-                            to_seq(states_at((seq + k) % ns), got_s, ss_sem, rs_sem, k).start()
-                    else:
-                        begin()
-                if h == STREAMS - 1 and with_sums:
-                    mine_b[8:16, :] = jnp.zeros((8, width), F32)
-                    mine_b[8:16, : small_b.shape[1]] = small_b[...]
-                    for k in range(1, ns):
-                        to_seq(mine_b, got_b, sb_sem, rb_sem, k).start()
-            if 0 <= u < n - 1:
-                chain(h, u)
-            if u == n - 1:
-                finish(h)
-            if with_sums and n - 1 < u < 2 * n - 1:
-                relay(h, u - n + 1)
-        if not with_sums and t == n - 1:
-            turn()
-    if not with_sums:
-        end()
-    if with_sums:
-        total = small_a[...]
-        for k in range(1, ns):
-            from_seq(small_a, got_a, sa_sem, ra_sem, k).wait_recv()
-            total = total + got_a[(seq + k) % ns]
-        sum_a[...] = total
-        total = states_at(seq)[...]
-        for k in range(1, ns):
-            from_seq(states_at(seq), got_s, ss_sem, rs_sem, k).wait_recv()
-            total = total + got_s[(seq + k) % ns]
-        sum_s[...] = total
-        total = mine_b[...]
-        for k in range(1, ns):
-            from_seq(mine_b, got_b, sb_sem, rb_sem, k).wait_recv()
-            total = total + got_b[(seq + k) % ns]
-        sum_b[...] = total
-
-        def to_head(k):
-            return pltpu.make_async_remote_copy(
-                src_ref=sum_b,
-                dst_ref=got_c.at[me],
-                send_sem=sc_sem.at[k],
-                recv_sem=rc_sem.at[me],
-                device_id={"head": (me + k) % n},
-                device_id_type=MESH_ID,
-            )
-
-        def from_head(k):
-            other = (me + k) % n
-            return pltpu.make_async_remote_copy(
-                src_ref=sum_b,
-                dst_ref=got_c.at[other],
-                send_sem=sc_sem.at[k],
-                recv_sem=rc_sem.at[other],
-                device_id={"head": other},
-                device_id_type=MESH_ID,
-            )
-
-        for k in range(1, n):
-            to_head(k).start()
-        total = sum_b[...]
-        for k in range(1, n):
-            from_head(k).wait_recv()
-        for k in range(1, n):
-            to_head(k).wait_send()
-            total = total + got_c[(me + k) % n]
-        sum_b[...] = total
-        for k in range(1, ns):
-            to_seq(small_a, got_a, sa_sem, ra_sem, k).wait_send()
-            to_seq(states_at((seq + k) % ns), got_s, ss_sem, rs_sem, k).wait_send()
-            to_seq(mine_b, got_b, sb_sem, rb_sem, k).wait_send()
-    for h in range(STREAMS):
-        for i in range(n):
-
-            @pl.when(i > me)
-            def _():
-                step(i, h, True).wait_send()
-
-            @pl.when(i < me)
-            def _():
-                step(i, h, False).wait_send()
-
-            if with_sums:
-
-                @pl.when(has_right & (i <= me))
-                def _():
-                    hand_on(i, h, True).wait_send()
-
-                @pl.when(has_left & (i >= me))
-                def _():
-                    hand_on(i, h, False).wait_send()
-
-
-def reduce_over_heads(products, dims, collective, sums=None, packed=None, cols=None):
+        if t == 0:
+            pl.semaphore_wait(barrier, n + ns - 2)
+        slot(t)
+        if t == 1:
+            for k in range(1, ns):
+                to_seq(small_a, got_a, sa_sem, ra_sem, k).start()
+                to_seq(states_at((seq + k) % ns), got_s, ss_sem, rs_sem, k).start()
+        if t == GAP * (STREAMS - 1):
+            mine_b[8:16, :] = jnp.zeros((8, width), F32)
+            mine_b[8:16, : small_b.shape[1]] = small_b[...]
+            for k in range(1, ns):
+                to_seq(mine_b, got_b, sb_sem, rb_sem, k).start()
+        if t == slots_of(n) - 2:
+            total = small_a[...]
+            for k in range(1, ns):
+                from_seq(small_a, got_a, sa_sem, ra_sem, k).wait_recv()
+                total = total + got_a[(seq + k) % ns]
+            sum_a[...] = total
+            total = states_at(seq)[...]
+            for k in range(1, ns):
+                from_seq(states_at(seq), got_s, ss_sem, rs_sem, k).wait_recv()
+                total = total + got_s[(seq + k) % ns]
+            sum_s[...] = total
+            total = mine_b[...]
+            for k in range(1, ns):
+                from_seq(mine_b, got_b, sb_sem, rb_sem, k).wait_recv()
+                total = total + got_b[(seq + k) % ns]
+            sum_b[...] = total
+
+            def to_head(k):
+                return pltpu.make_async_remote_copy(
+                    src_ref=sum_b,
+                    dst_ref=got_c.at[me],
+                    send_sem=sc_sem.at[k],
+                    recv_sem=rc_sem.at[me],
+                    device_id={"head": (me + k) % n},
+                    device_id_type=MESH_ID,
+                )
+
+            def from_head(k):
+                other = (me + k) % n
+                return pltpu.make_async_remote_copy(
+                    src_ref=sum_b,
+                    dst_ref=got_c.at[other],
+                    send_sem=sc_sem.at[k],
+                    recv_sem=rc_sem.at[other],
+                    device_id={"head": other},
+                    device_id_type=MESH_ID,
+                )
+
+            for k in range(1, n):
+                to_head(k).start()
+    total = sum_b[...]
+    for k in range(1, n):
+        from_head(k).wait_recv()
+    for k in range(1, n):
+        to_head(k).wait_send()
+        total = total + got_c[(me + k) % n]
+    sum_b[...] = total
+    for k in range(1, ns):
+        to_seq(small_a, got_a, sa_sem, ra_sem, k).wait_send()
+        to_seq(states_at((seq + k) % ns), got_s, ss_sem, rs_sem, k).wait_send()
+        to_seq(mine_b, got_b, sb_sem, rb_sem, k).wait_send()
+    drain()
+
+
+def reduce_over_heads(products, dims, cols, collective, sums):
     n, ns = lax.axis_size("head"), lax.axis_size("seq")
-    tokens, width = products[0][0].shape[0], products[0][1].shape[dims[0][0][1][0] ^ 1]
+    tokens, width = sums[0].shape
     lefts, rights = [a for a, _ in products], [b for _, b in products]
     dma = pltpu.SemaphoreType.DMA
-    coded = pltpu.VMEM((tokens, width + LANES), BF16)
-    scratch = [pltpu.VMEM((tokens, width), F32), coded, coded, coded, coded]
-    scratch += [dma((STREAMS, n))] * 7
-    if sums is not None:
-        extra = list(sums)
-        small_a = sums[2].shape
-        states = (sums[4].shape[0] // ns, sums[4].shape[1])
-        out_shape = [sds((tokens, width + LANES), BF16), sds(small_a), sds((16, width)), sds(states)]
-        scratch += [
-            pltpu.VMEM((ns, *small_a), F32),
-            pltpu.VMEM((ns, 16, width), F32),
-            pltpu.VMEM((ns, *states), F32),
-            pltpu.VMEM((n, 16, width), F32),
-            pltpu.VMEM((16, width), F32),
-        ]
-        scratch += [dma((ns,))] * 6 + [dma((n,))] * 2
-    else:
-        extra = [packed]
-        states = (packed.shape[0] - HALO, packed.shape[1])
-        out_shape = [sds((tokens // n, width + LANES), BF16), sds(states)]
-        scratch += swap_scratch(ns, states)
+    small_a = sums[2].shape
+    states = (sums[4].shape[0] // ns, sums[4].shape[1])
+    out_shape = [sds((tokens, width + LANES), BF16), sds(small_a), sds((16, width)), sds(states)]
+    scratch = chain_scratch(tokens, width, n) + [
+        pltpu.VMEM((ns, *small_a), F32),
+        pltpu.VMEM((ns, 16, width), F32),
+        pltpu.VMEM((ns, *states), F32),
+        pltpu.VMEM((n, 16, width), F32),
+        pltpu.VMEM((16, width), F32),
+    ]
+    scratch += [dma((ns,))] * 6 + [dma((n,))] * 2
     vmem = pl.BlockSpec(memory_space=pltpu.VMEM)
     return pl.pallas_call(
-        functools.partial(reduce_kernel, n, ns, dims, cols or [None] * len(dims), sums is not None),
-        in_specs=[vmem] * (len(lefts) + len(rights) + len(extra)),
+        functools.partial(reduce_kernel, n, ns, dims, cols),
+        in_specs=[vmem] * (len(lefts) + len(rights) + len(sums)),
         out_specs=[vmem] * len(out_shape),
         out_shape=out_shape,
         scratch_shapes=scratch,
@@ -665,18 +662,12 @@
             bytes_accessed=100 * tokens * width,
             transcendentals=0,
         ),
-        name="reduce_heads" if sums is not None else "scatter_heads",
-    )(*lefts, *rights, *extra)
-
-
-def result_kernel(n, *refs):
-    pieces, hidden, out = refs[:n], refs[n], refs[n + 1]
-    me = lax.axis_index("head")
-    width = out.shape[1]
-    size = out.shape[0] // n
-    for k in range(n):
-        where = pl.ds(pl.multiple_of(((me + n - k) % n) * size, size), size)
-        out[where, :] = hidden[where, :].astype(F32) + decode(pieces[k][...], width)
+        name="reduce_heads",
+    )(*lefts, *rights, *sums)
+
+
+def result_kernel(code, hidden, out):
+    out[...] = hidden[...].astype(F32) + decode(code[...], out.shape[1])
 
 
 def turn_kernel(value, out):
@@ -801,20 +792,27 @@
 
 def back_kernel(
     n, ns, act, sact, y, gssd, step, step_pre, cum, cumt, sin, dout, before_log, total_log, incoming,
-    later, params, onehot, rows_in, pre, pre_prev, pre_halo, spre, spre_prev, spre_halo,
-    gin_o, gsb_out, small_a, small_b,
+    ynorm, proj_output, packed,
+    params, onehot, rows_in, pre, pre_prev, pre_halo, spre, spre_prev, spre_halo,
+    gin_o, gsb_out, small_a, small_b, code_out,
     gsb_o, gstep, xs_ref, u_ref, st_ref, gext, sext, pext, spext, halo_send, halo_got, shalo_send, shalo_got,
-    psend, pgot, h_sem, p_send, p_recv, g_send, g_recv,
+    psum, pgot, h_sem, p_send, p_recv, g_send, g_recv,
+    later, got_states, got_decays, prefix, swap_sems, all_ref, part, *chain_refs,
 ):
-    c = pl.program_id(0)
-    count = pl.num_programs(0) - 1
-    total_chunks = psend.shape[0] // Q
+    i = pl.program_id(0)
+    c = i - 1
+    count = pl.num_programs(0) - 2
+    total_chunks = psum.shape[0] // Q
+    begin, turn, end = swap_states(
+        ns, packed, later, got_states, got_decays, prefix, swap_sems, True
+    )
+    slot, drain = chains(n, all_ref, part, *chain_refs)
+    span = part.shape[0] // STREAMS
     groups = total_chunks // n
     taps = TAPS
     me, seq = lax.axis_index("head"), lax.axis_index("seq")
     state_size = bmat_width(sact)
     two = 2 * state_size
-    barrier = pltpu.get_barrier_semaphore()
 
     def halo(src, dst, k):
         return pltpu.make_async_remote_copy(
@@ -831,7 +829,7 @@
 
     def to_owner(k):
         return pltpu.make_async_remote_copy(
-            src_ref=psend.at[chunk_rows(k)],
+            src_ref=psum.at[chunk_rows(k)],
             dst_ref=pgot.at[me, chunk_rows(k // n)],
             send_sem=p_send.at[k],
             recv_sem=p_recv.at[me, k // n],
@@ -841,7 +839,7 @@
 
     def from_other(j, g):
         return pltpu.make_async_remote_copy(
-            src_ref=psend.at[chunk_rows(g)],
+            src_ref=psum.at[chunk_rows(g)],
             dst_ref=pgot.at[j, chunk_rows(g)],
             send_sem=p_send.at[g],
             recv_sem=p_recv.at[j, g],
@@ -862,24 +860,30 @@
             device_id_type=MESH_ID,
         )
 
-    @pl.when(c == 0)
-    def _():
-        for k in range(1, n):
-            pl.semaphore_signal(
-                barrier, inc=1, device_id={"head": (me + k) % n}, device_id_type=MESH_ID
-            )
-
-        @pl.when(seq < ns - 1)
-        def _():
-            pl.semaphore_signal(
-                barrier, inc=1, device_id={"seq": (seq + 1) % ns}, device_id_type=MESH_ID
-            )
-
+    @pl.when(i == 0)
+    def _():
+        barrier = greet(n, ns)
         small_a[...] = jnp.zeros_like(small_a)
         small_b[...] = jnp.zeros_like(small_b)
         small_a[5:7, :] = rows_in[0:2, :]
 
-    @pl.when(c < count)
+        def compute(h):
+            where = pl.ds(h * span, span)
+            part[where, :] = dg(ynorm[where, :], proj_output[...], NN)
+
+        compute(0)
+        pl.semaphore_wait(barrier, n + ns - 2)
+        begin()
+        slot(0)
+        compute(1)
+        slot(1)
+        for h in range(2, STREAMS):
+            compute(h)
+        turn()
+        slot(2)
+        end()
+
+    @pl.when((c >= 0) & (c < count))
     def _():
         hot = onehot[...]
         skip = params[6:7, :]
@@ -963,7 +967,6 @@
     def _():
         halo_send[...] = u_ref[:HALO, :]
         shalo_send[...] = sext[Q + HALO : Q + 2 * HALO, :]
-        pl.semaphore_wait(barrier, n - 1 + jnp.where(seq > 0, 1, 0))
 
         @pl.when(seq > 0)
         def _():
@@ -1014,13 +1017,14 @@
         inner = gext.shape[1]
         gin_o[:, :inner] = conv_back(gext, pext, 0, inner, small_a).astype(BF16)
         gin_o[:, inner:] = gstep[:Q, :]
-        psend[chunk_rows(c - 1), :] = conv_back(sext, spext, 8, two, small_b)
+        mine = conv_back(sext, spext, 8, two, small_b)
+        psum[chunk_rows(c - 1), :] = mine
 
         @pl.when((c - 1) % n != me)
         def _():
             to_owner(c - 1).start()
 
-    @pl.when(c < count)
+    @pl.when((c >= 0) & (c < count))
     def _():
         gext[:Q, :] = u_ref[...]
         gstep[:Q, :] = gstep[Q:, :]
@@ -1031,7 +1035,7 @@
         @pl.when(c == min((g + 1) * n + 2, total_chunks))
         def _():
             own = chunk_rows(g * n + me)
-            total = psend[own, :]
+            total = psum[own, :]
             for k in range(1, n):
                 j = (me + k) % n
                 from_other(j, g).wait_recv()
@@ -1054,6 +1058,18 @@
             @pl.when(k % n != me)
             def _():
                 to_owner(k).wait_send()
+
+    slots, last_step = slots_of(n), count + 1
+    for t in range(3, slots):
+
+        @pl.when(i == 1 + (t - 3) * last_step // (slots - 3))
+        def _():
+            slot(t)
+
+    @pl.when(i == last_step)
+    def _():
+        drain()
+        code_out[...] = all_ref[...]
 
 
 def matmul_low(left, right):
@@ -1261,12 +1277,6 @@
     )
     local_proj_output = transposed_times(cotangent, ynorm)
     local_proj_gate = transposed_times(normed, grad_gate_pre)
-    own_code, later = reduce_over_heads(
-        [(ynorm, proj_output)], [NN], 1, packed=packed_back
-    )
-    codes = [own_code]
-    for k in range(1, n):
-        codes.append(turned(own_code, k))
     summed_out = lax.psum_scatter(
         local_proj_output, "seq", scatter_dimension=0, tiled=True
     )
@@ -1277,22 +1287,31 @@
         local_proj_gate, "seq", scatter_dimension=0, tiled=True
     )
 
+    def now(i):
+        return jnp.clip(i - 1, 0, count - 1)
+
+    def past(i):
+        return jnp.maximum(i - 2, 0)
+
     def held(size, height=Q):
-        return pl.BlockSpec((height, size), lambda c: (jnp.minimum(c, count - 1), 0))
+        return pl.BlockSpec((height, size), lambda i: (now(i), 0))
 
     def prior(size):
-        return pl.BlockSpec((Q, size), lambda c: (jnp.maximum(c - 1, 0), 0))
+        return pl.BlockSpec((Q, size), lambda i: (past(i), 0))
 
     def prior_edge(size):
         return pl.BlockSpec(
-            (HALO, size), lambda c: (jnp.maximum((c - 1) * (Q // HALO) - 1, 0), 0)
-        )
+            (HALO, size), lambda i: (jnp.maximum(past(i) * (Q // HALO) - 1, 0), 0)
+        )
+
+    def once(shape):
+        return pl.BlockSpec(shape, lambda i: (0, 0), pipeline_mode=pl.Buffered(1))
 
     dma = pltpu.SemaphoreType.DMA
     groups = count // n
-    grad_in_b, grad_states_b, small_a, small_b = call(
+    grad_in_b, grad_states_b, small_a, small_b, branch_code = call(
         functools.partial(back_kernel, n, ns),
-        (count + 1,),
+        (count + 2,),
         [
             (act, held(inner)),
             (sact, held(two)),
@@ -1306,11 +1325,13 @@
             (dout, held(inner, state_size)),
             (
                 before_log,
-                pl.BlockSpec((None, 1, LANES), lambda c: (jnp.minimum(c, count - 1), 0, 0)),
+                pl.BlockSpec((None, 1, LANES), lambda i: (now(i), 0, 0)),
             ),
             (total_log, whole((1, LANES))),
-            (incoming, whole((state_size, inner))),
-            (later, whole((state_size, inner))),
+            (incoming, once((state_size, inner))),
+            (ynorm, once((tokens, inner))),
+            (proj_output, once((inner, width))),
+            (packed_back, once(packed_shape)),
             par,
             hot,
             (grad_rows, whole((HALO, inner))),
@@ -1326,6 +1347,7 @@
             (sds((tokens, two), BF16), whole((tokens, two))),
             (sds((16, inner)), whole((16, inner))),
             (sds((HALO, two)), whole((HALO, two))),
+            (sds((tokens, width + LANES), BF16), once((tokens, width + LANES))),
         ],
         scratch=[
             pltpu.VMEM((tokens, two), BF16),
@@ -1348,20 +1370,19 @@
             dma((n, groups)),
             dma((n, groups)),
             dma((n, groups)),
+            pltpu.VMEM((state_size, inner), F32),
+            *swap_scratch(ns, (state_size, inner)),
+            pltpu.VMEM((tokens, width + LANES), BF16),
+            *chain_scratch(tokens, width, n),
         ],
         flops=40 * tokens * inner * Q,
         collective=4,
     )
-    stream = tokens // STREAMS
     result = call(
-        functools.partial(result_kernel, n),
-        (STREAMS,),
-        [
-            (code, pl.BlockSpec((stream // n, width + LANES), lambda c: (c, 0)))
-            for code in codes
-        ]
-        + [(hidden, pl.BlockSpec((stream, width), lambda c: (c, 0)))],
-        [(sds((tokens, width)), pl.BlockSpec((stream, width), lambda c: (c, 0)))],
+        result_kernel,
+        (count,),
+        [(branch_code, rows(width + LANES)), (hidden, rows(width))],
+        [(sds((tokens, width)), rows(width))],
         flops=20 * tokens * width,
     )[0]
     row_start = head_index * row_width
@@ -1380,9 +1401,9 @@
             (grad_states_b, own_states),
         ],
         [NT] * 4,
+        (None, (0, inner), (inner, inner + LANES), None),
         2,
         (hidden, inv_rms, small_a, small_b, local_proj_states),
-        cols=(None, (0, inner), (inner, inner + LANES), None),
     )
     grad_hidden = call(
         hidden_kernel,

time: 467 us -> 430 us (0.921)
  Pallas kernels: 368 us -> 336 us
  starting transfers between devices: 14.4 us -> 9.05 us
    pallas_call x2 -> x1, Pallas kernels: 230 us -> 110 us  [reduce_over_heads(): pl.pallas_call(functools.partial(reduce_kernel, n, ns, dims, cols), in_sp...]
    pallas_call x6, Pallas kernels: 135 us -> 224 us  [call(): pl.pallas_call(kernel, grid=grid, in_specs=in_specs, out_specs=[spec for...]
    ppermute x6 -> x3, starting transfers between devices: 12 us -> 7.04 us  [turned(): return lax.ppermute(value, 'head', [(i, (i + k) % n) for i in range(n)])]
  transfers between devices with their start and end apart: 10 -> 7, of which waited for: 0 -> 0; matrix products, arithmetic and copies ran while one was open for 12% -> 13% of each run, Pallas kernels for 66% -> 64%
where the time goes in v2:
time: 430 us; the launch traced here: 423 us
  Pallas kernels  336 us (78%)
  matrix products  36.5 us (8%)
  local copies, waits for them, and re-layouts  20.9 us (5%)
  between operations  14.5 us (3%)
  starting transfers between devices  9.05 us (2%)
  other arithmetic  5.69 us (1%)
    pallas_call x6, Pallas kernels, call(): pl.pallas_call(kernel, grid=grid, in_specs=in_specs, out_specs=[spec for...  224 us
    pallas_call x1, Pallas kernels, reduce_over_heads(): pl.pallas_call(functools.partial(reduce_kernel, n, ns, dims, cols), in_sp...  110 us
    dot_general x5, matrix products, dg(): return lax.dot_general(left, right, dims, preferred_element_type=F32)  25.3 us
    dot_general x3, matrix products, matmul_low(): return jnp.dot(left, right, preferred_element_type=F32)  11.2 us
  transfers between devices with their start and end apart: 7, of which 0 were waited for; matrix products, arithmetic and copies ran while one was open for 13% of the time, Pallas kernels for 64%

profile of v2, /device:TPU:0, one launch (start us, length us, event | category | flops | bytes accessed | tf_op | source)
XLA Modules:
  0.0 422.6 jit_solution(7887630483745490746)
XLA Ops:
  7.2 0.0 copy-start
  7.2 0.0 reduce-scatter.8.cloned.1.call-start
  7.2 3.1 collective-permute-start.1
  10.4 2.6 collective-permute-start.2
  12.9 1.3 collective-permute-start.3
  14.3 1.3 slice.36
  15.6 1.9 collective-permute-start
  17.5 2.6 fusion
  20.1 0.0 copy-start.5
  20.2 0.8 fusion.2.normed
  20.9 0.9 copy-done.5
  21.8 4.3 %fusion.9.pre.pre_prev = f32[1024,768]{1,0:T(8,128)} fusion(bf16[1024,1536]{1,0:T(8,128)(2,1)S(1)} %fusion.2.normed, bf16[1536,768]{1,0:T(8,128)(2,1)S(1)} %copy-done.5), kind=kOutput, calls=%fused_computation.31 | convolution fusion | flops 2415919104 | bytes 8650752 | tf_op jit(solution)/shard_map/dot_general | solution.py:1076
  26.1 0.0 copy-start.16
  26.1 0.0 copy-start.11
  26.1 0.0 copy-start.12
  26.1 0.0 copy-start.17
  26.1 0.0 copy-start.3
  26.2 0.0 copy-start.4
  26.2 4.2 %fusion.10.gate = f32[1024,768]{1,0:T(8,128)} fusion(bf16[1024,1536]{1,0:T(8,128)(2,1)S(1)} %fusion.2.normed, bf16[1536,768]{1,0:T(8,128)(2,1)S(1)} %copy-done.13), kind=kOutput, calls=%fused_computation.32 | convolution fusion | flops 2415919104 | bytes 8650752 | tf_op jit(solution)/shard_map/dot_general | solution.py:1076
  30.5 4.3 %fusion.11.gyn = f32[1024,768]{1,0:T(8,128)} fusion(bf16[1024,1536]{1,0:T(8,128)(2,1)S(1)} %copy-done.3, bf16[768,1536]{1,0:T(8,128)(2,1)S(1)} %copy-done.4), kind=kOutput, calls=%fused_computation.33 | convolution fusion | flops 2415919104 | bytes 8650752 | tf_op jit(solution)/shard_map/dot_general | solution.py:29
  34.9 0.6 pad_bitcast_fusion.vec
  35.5 1.0 copy.37
  36.5 0.8 pad.18.step_w.refs_6_
  37.4 0.0 collective-permute-done
  37.4 0.9 fusion.5
  38.2 0.8 fusion.7.normed_halo
  39.0 2.7 convolution_multiply_fusion.pre_halo
  41.8 0.0 collective-permute-done.1.refs_1_
  41.8 0.0 collective-permute-done.2.refs_2_
  41.8 14.8 %shard_map.288 = (f32[1024,768]{1,0:T(8,128)}, f32[1024,256]{1,0:T(8,128)}, f32[1024,256]{1,0:T(8,128)}, f32[8,256]{1,0:T(8,128)}, f32[1024,128]{1,0:T(8,128)}, ...) custom-call(f32[1024,768]{1,0:T(8,128)} %fusion.9.pre.pre_prev, ...), custom_call_target="tpu_custom_call" | custom-call | flops 1006632960 | bytes 21848576 | tf_op jit(solution)/shard_map/pallas_call | solution.py:71
  56.6 19.7 %shard_map.289 = (f32[1024,768]{1,0:T(8,128)}, f32[128,768]{1,0:T(8,128)}) custom-call(f32[1024,768]{1,0:T(8,128)} %get-tuple-element.50.act, f32[1024,256]{1,0:T(8,128)} %get-tuple-element.51.sact, f32[1024,128]{1,0:T(8,128)} %get-tuple-element.52.step, f32[1024,128]{1,0:T(8,128)} %get-tuple-element.53.cum, f32[1024,128]{1,0:T(8,128)} %get-tuple-element.54.cumt, ...), custom_call_target="tpu_custom_call" | custom-call | flops 1207959552 | bytes 9969664 | tf_op jit(solution)/shard_map/pallas_call | solution.py:71
  76.3 29.6 %shard_map.290 = (f32[1024,768]{1,0:T(8,128)}, bf16[1024,768]{1,0:T(8,128)(2,1)}, bf16[1024,768]{1,0:T(8,128)(2,1)}, f32[1024,768]{1,0:T(8,128)}, f32[1024,768]{...) custom-call(f32[1024,768]{1,0:T(8,128)} %get-tuple-element.58.yloc, f32[1024,768]{1,0:T(8,128)} %get-tuple-element.50.act, ...), custom_call_target="tpu_custom_call" | custom-call | flops 1207959552 | bytes 30970368 | tf_op jit(solution)/shard_map/pallas_call | solution.py:71
  105.9 5.8 %convolution_bitcast_fusion = f32[1536,768]{1,0:T(8,128)} fusion(bf16[1024,768]{1,0:T(8,128)(2,1)} %get-tuple-element.69.ynorm, bf16[1024,1536]{1,0:T(8,128)(2,1)S(1)} %copy-done.3), kind=kOutput, calls=%fused_computation.5 | convolution fusion | flops 2415919104 | bytes 9437184 | tf_op jit(solution)/shard_map/dot_general | solution.py:29
  111.7 0.0 reduce-scatter.8.cloned.1.call-update
  111.8 0.0 reduce-scatter.6.cloned.1.call-start
  111.8 0.0 copy-start.2
  111.8 141.2 %shard_map.291 = (bf16[1024,896]{1,0:T(8,128)(2,1)}, bf16[1024,256]{1,0:T(8,128)(2,1)}, f32[16,768]{1,0:T(8,128)}, f32[8,256]{1,0:T(8,128)}, bf16[1024,1664]{1,0:T(8,128)(2,1)}) custom-call(f32[1024,768]{1,0:T(8,128)} %get-tuple-element.50.act, f32[1024,256]{1,0:T(8,128)} %get-tuple-element.51.sact, f32[1024,768]{1,0:T(8,128)} %get-tuple-element.65.y, ...), custom_call_target="tpu_custom_call" | custom-call | flops 4026531840 | bytes 38138368 | tf_op jit(solution)/shard_map/pallas_call | solution.py:71
  253.1 6.8 %fusion.13 = f32[1536,896]{1,0:T(8,128)} fusion(bf16[1024,1536]{1,0:T(8,128)(2,1)S(1)} %copy-done.2, bf16[1024,896]{1,0:T(8,128)(2,1)} %get-tuple-element.76.refs_1_.refs_2_), kind=kOutput, calls=%fused_computation.35 | convolution fusion | flops 2818572288 | bytes 10485760 | tf_op jit(solution)/shard_map/dot_general | solution.py:29
  259.8 0.0 reduce-scatter.6.cloned.1.call-update
  259.9 0.0 reduce-scatter.4.cloned.1.call-start
  259.9 5.8 %fusion.12 = f32[1536,768]{1,0:T(8,128)} fusion(bf16[1024,1536]{1,0:T(8,128)(2,1)S(1)} %copy-done.2, bf16[1024,768]{1,0:T(8,128)(2,1)} %get-tuple-element.75.refs_0_), kind=kOutput, calls=%fused_computation.34 | convolution fusion | flops 2415919104 | bytes 9437184 | tf_op jit(solution)/shard_map/dot_general | solution.py:29
  265.7 0.0 reduce-scatter.4.cloned.1.call-update
  265.7 0.6 broadcast_in_dim.5.gain
  266.3 1.0 copy.38.refs_9_.inv
  267.4 0.1 broadcast_in_dim.4
  267.5 0.0 copy-start.6
  267.5 2.6 fusion.3.refs_12_
  270.1 110.0 %reduce_heads.1 = (bf16[1024,1664]{1,0:T(8,128)(2,1)}, f32[16,768]{1,0:T(8,128)}, f32[16,1536]{1,0:T(8,128)}, f32[32,384]{1,0:T(8,128)}) custom-call(bf16[1024,768]{1,0:T(8,128)(2,1)} %get-tuple-element.75.refs_0_, bf16[1024,896]{1,0:T(8,128)(2,1)} %get-tuple-element.76.refs_1_.refs_2_, bf16[1024,896]{1,0:T(8,128)(2,1)} %get-tuple-element.76.refs_1_.refs_2_, ...), custom_call_target="tpu_custom_call" | custom-call | flops 8858370048 | bytes 157286400 | tf_op jit(solution)/shard_map/reduce_heads/pallas_call | solution.py:651
  380.1 1.3 slice.42
  381.4 1.3 slice.43
  382.6 1.3 slice.40
  384.0 1.5 slice_reduce_fusion.1
  385.5 0.1 reshape_squeeze.3
  385.5 0.6 reduce_sum.29
  386.2 8.3 %shard_map.292 = f32[1024,1536]{1,0:T(8,128)} custom-call(bf16[1024,1664]{1,0:T(8,128)(2,1)} %get-tuple-element.74.code, bf16[1024,1536]{1,0:T(8,128)(2,1)} %hidden.3), custom_call_target="tpu_custom_call" | custom-call | flops 31457280 | bytes 12845056 | tf_op jit(solution)/shard_map/pallas_call | solution.py:71
  394.4 9.9 %shard_map.293 = f32[1024,1536]{1,0:T(8,128)} custom-call(bf16[1024,1664]{1,0:T(8,128)(2,1)} %get-tuple-element.80.code, bf16[1024,1536]{1,0:T(8,128)(2,1)} %hidden.3, bf16[1024,1536]{1,0:T(8,128)(2,1)} %cotangent.1, f32[1024,1]{1,0:T(8,128)} %copy.38.refs_9_.inv, f32[1,1536]{1,0:T(1,128)} %broadcast_in_dim.5.gain), custom_call_target="tpu_custom_call" | custom-call | flops 31457280 | bytes 16001024 | tf_op jit(solution)/shard_map/pallas_call | solution.py:71
  404.4 1.4 slice_reduce_fusion
  405.8 1.2 slice_bitcast_fusion
  407.0 2.3 turn.1
  409.3 2.2 copy.42
  411.5 0.9 slice.49
  412.4 0.7 copy.41
  413.0 1.9 slice.48
  415.0 0.6 copy.52
  (40 shorter events, 0.1 us)
Async XLA Ops:
  7.2 13.0 %copy-start = (bf16[1024,1536]{1,0:T(8,128)(2,1)S(1)}, bf16[1024,1536]{1,0:T(8,128)(2,1)}, u32[]{:S(2)}) copy-start(bf16[1024,1536]{1,0:T(8,128)(2,1)} %hidden.3) | copy-start | bytes 9437188
  7.2 12.9 %copy-start.10 = (bf16[1536]{0:T(1024)(128)(2,1)S(1)}, bf16[1536]{0:T(1024)(128)(2,1)}, u32[]{:S(2)}) copy-start(bf16[1536]{0:T(1024)(128)(2,1)} %param.18) | copy-start | bytes 9220
  7.2 399.8 %reduce-scatter.8.cloned.1.call-start = ((), (), s32[]{:S(2)}) async-start(), calls=%async_computation.5 | async-start | bytes 5308416 | tf_op jit(solution)/shard_map/reduce_scatter | solution.py:1280
  7.2 34.5 %collective-permute-start.1 = (bf16[384,256]{1,0:T(8,128)(2,1)}, bf16[384,256]{1,0:T(8,128)(2,1)}, u32[]{:S(2)}, u32[]{:S(2)}) collective-permute-start(bf16[384,256]{1,0:T(8,128)(2,1)} %refs_0_.1), channel_id=1, source_target_pairs={{0,1},{1,2},{2,3},{3,0},{4,5},{5,6},{6,7},{7,4},{8,9},{9,10},{10,1... | collective-permute-start | bytes 589832 | tf_op jit(solution)/shard_map/ppermute | solution.py:1124
  10.4 31.4 %collective-permute-start.2 = (bf16[384,256]{1,0:T(8,128)(2,1)}, bf16[384,256]{1,0:T(8,128)(2,1)}, u32[]{:S(2)}, u32[]{:S(2)}) collective-permute-start(bf16[384,256]{1,0:T(8,128)(2,1)} %refs_0_.1), channel_id=1, source_target_pairs={{0,2},{1,3},{2,0},{3,1},{4,6},{5,7},{6,4},{7,5},{8,10},{9,11},{10,... | collective-permute-start | bytes 589832 | tf_op jit(solution)/shard_map/ppermute | solution.py:1124
  12.9 28.8 %collective-permute-start.3 = (bf16[384,256]{1,0:T(8,128)(2,1)}, bf16[384,256]{1,0:T(8,128)(2,1)}, u32[]{:S(2)}, u32[]{:S(2)}) collective-permute-start(bf16[384,256]{1,0:T(8,128)(2,1)} %refs_0_.1), channel_id=1, source_target_pairs={{0,3},{1,0},{2,1},{3,2},{4,7},{5,4},{6,5},{7,6},{8,11},{9,8},{10,9... | collective-permute-start | bytes 589832 | tf_op jit(solution)/shard_map/ppermute | solution.py:1124
  15.6 21.7 %collective-permute-start = (bf16[8,1536]{1,0:T(8,128)(2,1)}, bf16[8,1536]{1,0:T(8,128)(2,1)}, u32[]{:S(2)}, u32[]{:S(2)}) collective-permute-start(bf16[8,1536]{1,0:T(8,128)(2,1)} %slice.36), channel_id=1, source_target_pairs={{0,4},{4,8},{8,12},{12,16},{16,20},{20,24},{24,28},{1,5},{5,9},{9,... | collective-permute-start | bytes 73736 | tf_op jit(solution)/shard_map/ppermute | solution.py:63
  20.1 1.7 copy-start.5
  21.8 4.3 %copy-start.1 = (bf16[1024,1536]{1,0:T(8,128)(2,1)}, bf16[1024,1536]{1,0:T(8,128)(2,1)S(1)}, u32[]{:S(2)}) copy-start(bf16[1024,1536]{1,0:T(8,128)(2,1)S(1)} %fusion.2.normed) | copy-start | bytes 9437188
  21.8 4.3 %copy-start.13 = (bf16[1536,768]{1,0:T(8,128)(2,1)S(1)}, bf16[1536,768]{1,0:T(8,128)(2,1)}, u32[]{:S(2)}) copy-start(bf16[1536,768]{1,0:T(8,128)(2,1)} %refs_4_.1) | copy-start | bytes 7077892
  26.1 4.3 %copy-start.14 = (f32[12]{0:T(128)S(1)}, f32[12]{0:T(128)}, u32[]{:S(2)}) copy-start(f32[12]{0:T(128)} %param.28) | copy-start | bytes 148
  26.1 4.3 %copy-start.15 = (f32[12]{0:T(128)S(1)}, f32[12]{0:T(128)}, u32[]{:S(2)}) copy-start(f32[12]{0:T(128)} %param.27) | copy-start | bytes 148
  26.1 4.3 %copy-start.16 = (f32[12]{0:T(128)S(1)}, f32[12]{0:T(128)}, u32[]{:S(2)}) copy-start(f32[12]{0:T(128)} %param.29) | copy-start | bytes 148
  26.1 4.3 %copy-start.11 = (bf16[768]{0:T(1024)(128)(2,1)S(1)}, bf16[768]{0:T(1024)(128)(2,1)}, u32[]{:S(2)}) copy-start(bf16[768]{0:T(1024)(128)(2,1)} %param.24) | copy-start | bytes 4612
  26.1 4.4 %copy-start.12 = (bf16[768]{0:T(1024)(128)(2,1)S(1)}, bf16[768]{0:T(1024)(128)(2,1)}, u32[]{:S(2)}) copy-start(bf16[768]{0:T(1024)(128)(2,1)} %param.30) | copy-start | bytes 4612
  26.1 4.4 %copy-start.17 = (bf16[256]{0:T(256)(128)(2,1)S(1)}, bf16[256]{0:T(256)(128)(2,1)}, u32[]{:S(2)}) copy-start(bf16[256]{0:T(256)(128)(2,1)} %param.26) | copy-start | bytes 1540
  26.1 4.4 %copy-start.3 = (bf16[1024,1536]{1,0:T(8,128)(2,1)S(1)}, bf16[1024,1536]{1,0:T(8,128)(2,1)}, u32[]{:S(2)}) copy-start(bf16[1024,1536]{1,0:T(8,128)(2,1)} %cotangent.1) | copy-start | bytes 9437188
  26.2 4.4 %copy-start.4 = (bf16[768,1536]{1,0:T(8,128)(2,1)S(1)}, bf16[768,1536]{1,0:T(8,128)(2,1)}, u32[]{:S(2)}) copy-start(bf16[768,1536]{1,0:T(8,128)(2,1)} %proj_output.1) | copy-start | bytes 7077892
  39.0 2.7 copy-start.8
  111.8 299.7 %reduce-scatter.6.cloned.1.call-start = ((), (), s32[]{:S(2)}) async-start(), calls=%async_computation.4 | async-start | bytes 6193152 | tf_op jit(solution)/shard_map/reduce_scatter | solution.py:1395
  111.8 141.2 %copy-start.2 = (bf16[1024,1536]{1,0:T(8,128)(2,1)S(1)}, bf16[1024,1536]{1,0:T(8,128)(2,1)}, u32[]{:S(2)}) copy-start(bf16[1024,1536]{1,0:T(8,128)(2,1)} %copy-done.1) | copy-start | bytes 9437188
  259.9 155.1 %reduce-scatter.4.cloned.1.call-start = ((), (), s32[]{:S(2)}) async-start(), calls=%async_computation.3 | async-start | bytes 5308416 | tf_op jit(solution)/shard_map/reduce_scatter | solution.py:1286
  265.7 1.7 copy-start.7
  267.5 2.6 copy-start.6
  404.4 10.6 %copy-start.9 = (f32[32,384]{1,0:T(8,128)S(1)}, f32[32,384]{1,0:T(8,128)}, u32[]{:S(2)}) copy-start(f32[32,384]{1,0:T(8,128)} %get-tuple-element.82) | copy-start | bytes 147460
Sparse Core Ops, SparseCore 0:
  111.9 54.1 reduce-scatter.7
  260.0 64.7 reduce-scatter.5
  328.8 56.5 reduce-scatter.3

commit v3 on v2

--- a/solution.py
+++ b/solution.py
@@ -15,6 +15,7 @@
 LANES = 128
 HALO = 8
 TAPS = 4
+GROUP = 2
 
 F32 = jnp.float32
 BF16 = jnp.bfloat16
@@ -50,17 +51,11 @@
 
 
 def sigmoid(value):
-    return 1.0 / (1.0 + jnp.exp(-value))
+    return 0.5 * jnp.tanh(0.5 * value) + 0.5
 
 
 def silu(value):
     return value * sigmoid(value)
-
-
-def shifted(block, axis, distance):
-    devices = range(lax.axis_size(axis))
-    route = [(i - distance, i) for i in devices if i - distance in devices]
-    return lax.ppermute(block, axis, route)
 
 
 def call(kernel, grid, ins, outs, scratch=(), flops=0, collective=None):
@@ -88,18 +83,16 @@
     return jax.ShapeDtypeStruct(shape, dtype)
 
 
-def rows(width, reverse=None):
-    if reverse is None:
-        return pl.BlockSpec((Q, width), lambda c: (c, 0))
-    return pl.BlockSpec((Q, width), lambda c: (reverse - 1 - c, 0))
+def rows(width, height=Q):
+    return pl.BlockSpec((height, width), lambda c: (c, 0))
 
 
 def whole(shape):
     return pl.BlockSpec(shape, lambda c: (0,) * len(shape))
 
 
-def before(width):
-    return pl.BlockSpec((HALO, width), lambda c: (jnp.maximum(c * (Q // HALO) - 1, 0), 0))
+def before(width, height):
+    return pl.BlockSpec((HALO, width), lambda c: (jnp.maximum(c * (height // HALO) - 1, 0), 0))
 
 
 def triangle(lower):
@@ -117,28 +110,108 @@
     return dg(mask, high, NN) + (dg(mask, mid, NN) + dg(mask, low, NN))
 
 
-def conv_act(pre_ref, prev_ref, halo_ref, params, at, ext_ref):
-    first = pl.program_id(0) == 0
+def conv_act(pre, ext_ref, params, at):
     size = ext_ref.shape[1]
-    ext_ref[:HALO, :] = jnp.where(first, halo_ref[...], prev_ref[...])
-    ext_ref[HALO:, :] = pre_ref[...]
-    taps = TAPS
-    total = params[at + taps : at + taps + 1, :size] + params[at + taps - 1 : at + taps, :size] * pre_ref[...]
-    for k in range(taps - 1):
-        start = HALO - taps + 1 + k
-        total = total + params[at + k : at + k + 1, :size] * ext_ref[start : start + Q, :]
+    height = pre.shape[0]
+    ext_ref[HALO:, :] = pre
+    total = params[at + TAPS : at + TAPS + 1, :size] + params[at + TAPS - 1 : at + TAPS, :size] * pre
+    for k in range(TAPS - 1):
+        start = HALO - TAPS + 1 + k
+        total = total + params[at + k : at + k + 1, :size] * ext_ref[start : start + height, :]
     return total
 
 
+def front_kernel(
+    n, ns, hidden, cotangent, tail, gain, proj_input, proj_gate, proj_output, piece,
+    normed_o, inv_o, pre_o, gate_o, gyn_o, full_o, nhalo_o, halo_o,
+    full, halo, s_sem, r_sem, h_sem,
+):
+    c = pl.program_id(0)
+    me, seq = lax.axis_index("head"), lax.axis_index("seq")
+    height = piece.shape[0]
+
+    def slab(j):
+        return pl.ds(pl.multiple_of(j * height, height), height)
+
+    def give(k, arriving):
+        other = (me + k) % n
+        owner = other if arriving else me
+        return pltpu.make_async_remote_copy(
+            src_ref=piece,
+            dst_ref=full.at[slab(owner)],
+            send_sem=s_sem.at[k],
+            recv_sem=r_sem.at[owner],
+            device_id={"head": other},
+            device_id_type=MESH_ID,
+        )
+
+    def edge():
+        return pltpu.make_async_remote_copy(
+            src_ref=tail,
+            dst_ref=halo,
+            send_sem=h_sem.at[0],
+            recv_sem=h_sem.at[1],
+            device_id={"seq": (seq + 1) % ns},
+            device_id_type=MESH_ID,
+        )
+
+    def norm(value):
+        value = value.astype(F32)
+        inv = lax.rsqrt(jnp.mean(value * value, axis=-1, keepdims=True) + EPS)
+        return inv, (value * inv * gain[...]).astype(BF16)
+
+    @pl.when(c == 0)
+    def _():
+        barrier = greet(n, ns)
+        pl.semaphore_wait(barrier, n + ns - 2)
+        for k in range(1, n):
+            give(k, False).start()
+
+        @pl.when(seq < ns - 1)
+        def _():
+            edge().start()
+
+        full[slab(me), :] = piece[...]
+
+    inv, normed = norm(hidden[...])
+    inv_o[...] = inv
+    normed_o[...] = normed
+    pre_o[...] = dg(normed, proj_input[...], NN)
+    gate_o[...] = dg(normed, proj_gate[...], NN)
+    gyn_o[...] = dg(cotangent[...], proj_output[...], NT)
+
+    @pl.when(c == pl.num_programs(0) - 1)
+    def _():
+        @pl.when(seq > 0)
+        def _():
+            edge().wait_recv()
+
+        @pl.when(seq == 0)
+        def _():
+            halo[...] = jnp.zeros_like(halo)
+
+        before_first = norm(halo[...])[1]
+        nhalo_o[...] = before_first
+        halo_o[...] = dg(before_first, proj_input[...], NN)[16 - HALO :, :]
+
+        @pl.when(seq < ns - 1)
+        def _():
+            edge().wait_send()
+
+        for k in range(1, n):
+            give(k, True).wait_recv()
+        full_o[...] = full[...]
+        for k in range(1, n):
+            give(k, False).wait_send()
+
+
 def states_kernel(
-    n, pre, pre_prev, pre_halo, normed, normed_halo, step_w, vec, taps_in, taps_st, onehot, *refs
+    pre, pre_prev, pre_halo, normed, normed_halo, step_w, vec, taps_in, taps_st, full, onehot, *refs
 ):
-    pieces, refs = refs[:n], refs[n:]
     act_o, sact_o, spre_o, shalo_o, spre_step_o, step_o, cum_o, cumt_o, sin_o, dev_o, total_o = refs[:11]
     before_o, params = refs[11:13]
-    ext, sext, state, total, full = refs[13:]
+    ext, sext, state, total = refs[13:]
     c = pl.program_id(0)
-    me = lax.axis_index("head")
     state_size = bmat_width(sact_o)
     inner = pre.shape[1]
     two = 2 * state_size
@@ -147,13 +220,12 @@
     def line(first, size):
         return jnp.concatenate([vec[r : r + 1, :] for r in range(first, first + size // LANES)], axis=1)
 
+    height = pre.shape[0]
+
     @pl.when(c == 0)
     def _():
         state[...] = jnp.zeros_like(state)
         total[...] = jnp.zeros_like(total)
-        height = pieces[0].shape[0]
-        for k in range(n):
-            full[pl.ds(pl.multiple_of(((me + n - k) % n) * height, height), height), :] = pieces[k][...]
         params[...] = jnp.zeros_like(params)
         per = inner // LANES
         params[0:TAPS, :] = taps_in[...].astype(F32)
@@ -164,40 +236,41 @@
         params[7:8, LANES : 2 * LANES] = vec[1:2, :]
         params[8 : 8 + TAPS, :two] = taps_st[...].astype(F32)
         params[12:13, :two] = line(3 + 2 * per, two)
-        first = dg(normed_halo[...], full[...], NN)
-        shalo_o[...] = jnp.where(lax.axis_index("seq") == 0, 0.0, first)
-        sext[Q:, :] = shalo_o[...]
-
-    sext[:HALO, :] = sext[Q:, :]
+        shalo_o[...] = dg(normed_halo[...], full[...], NN)[16 - HALO :, :]
+        sext[height:, :] = shalo_o[...]
+        ext[:HALO, :] = pre_halo[...]
+
+    @pl.when(c > 0)
+    def _():
+        ext[:HALO, :] = pre_prev[...]
+
+    sext[:HALO, :] = sext[height:, :]
     spre = dg(normed[...], full[...], NN)
     spre_o[...] = spre
-    sext[HALO:, :] = spre
     step_pre = dg(normed[...], step_w[...], NN)
     spre_step_o[...] = step_pre
-    act = conv_act(pre, pre_prev, pre_halo, params, 0, ext)
-    sact = params[12:13, :two] + params[8 + TAPS - 1 : 8 + TAPS, :two] * spre
-    for k in range(TAPS - 1):
-        start = HALO - TAPS + 1 + k
-        sact = sact + params[8 + k : 9 + k, :two] * sext[start : start + Q, :]
+    act = conv_act(pre[...], ext, params, 0)
+    sact = conv_act(spre, sext, params, 8)
     act_o[...] = act
     sact_o[...] = sact
-    bmat = silu(sact[:, :state_size])
     step = jax.nn.softplus(step_pre + params[7:8, LANES : 2 * LANES])
-    cum = tri_sum(True, step * params[7:8, :LANES])
     step_o[...] = step
-    cum_o[...] = cum
-    cumt_o[...] = cum.T
-    last = cum[Q - 1 :, :]
-    weight = spread(step * jnp.exp(last - cum), hot)
-    xw = silu(act) * weight
-    sin_o[...] = state[...]
-    before_o[...] = total[...]
-    decay = spread(jnp.broadcast_to(jnp.exp(last), (HALO, LANES)), hot)[:1]
-    state[...] = state[...] * decay + dot3(bmat, xw, TN)
-    total[...] = total[...] + last
-    dev_o[:state_size, :] = state[...]
-    dev_o[state_size:, :] = spread(jnp.broadcast_to(jnp.exp(total[...]), (HALO, LANES)), hot)
-    total_o[...] = total[...]
+    x = silu(act)
+    bmat_all = silu(sact[:, :state_size])
+    for j in range(height // Q):
+        part = slice(j * Q, (j + 1) * Q)
+        cum = tri_sum(True, step[part] * params[7:8, :LANES])
+        cum_o[part, :] = cum
+        cumt_o[part, :] = cum.T
+        last = cum[Q - 1 :, :]
+        xw = x[part] * spread(step[part] * jnp.exp(last - cum), hot)
+        sin_o[j * state_size : (j + 1) * state_size, :] = state[...]
+        before_o[j] = total[...]
+        decay = spread(jnp.broadcast_to(jnp.exp(last), (HALO, LANES)), hot)[:1]
+        state[...] = state[...] * decay + dot3(bmat_all[part], xw, TN)
+        total[...] = total[...] + last
+    dev_o[...] = state[...]
+    total_o[...] = jnp.broadcast_to(total[...], (HALO, LANES))
 
 
 def bmat_width(ref):
@@ -216,13 +289,15 @@
 
 
 def intra_kernel(
-    ns, act, sact, step, cum, cumt, params, onehot, packed, out, incoming,
+    ns, act, sact, step, cum, cumt, params, onehot, packed, logs, out, incoming,
     xs_ref, entered, got_s, got_d, prefix, sems,
 ):
     c = pl.program_id(0)
     count = pl.num_programs(0)
     seq = lax.axis_index("seq")
-    begin, turn, end = swap_states(ns, packed, entered, got_s, got_d, prefix, sems, False)
+    begin, turn, end = swap_states(
+        ns, packed, logs, onehot, entered, got_s, got_d, prefix, sems, False
+    )
     barrier = pltpu.get_barrier_semaphore()
 
     @pl.when(c == 0)
@@ -235,25 +310,30 @@
         begin()
 
     state_size = bmat_width(sact)
-    sconv = silu(sact[...])
-    bmat, cmat = sconv[:, :state_size], sconv[:, state_size:]
-    scores = dot3(cmat, bmat, NT)
     x = silu(act[...])
     xs_ref[...] = x * spread(step[...], onehot[...])
     out[...] = x * params[6:7, :]
-    causal = triangle(True)
-    lane = lax.broadcasted_iota(jnp.int32, (Q, LANES), 1)
-    for p in range(act.shape[1] // LANES):
-        cols = slice(p * LANES, (p + 1) * LANES)
-        right = pair_stack(xs_ref[:, cols])
-        got = []
-        for j in range(2):
-            h = p * 2 + j
-            gap = cum[:, h : h + 1] - cumt[h : h + 1, :]
-            mixing = scores * jnp.exp(jnp.where(causal, gap, -1e30))
-            wide = dg(jnp.concatenate(split(mixing), axis=1), right, NN)
-            got.append(wide[:, :LANES] + wide[:, LANES:])
-        out[:, cols] = out[:, cols] + jnp.where(lane < LANES // 2, got[0], got[1])
+
+    @pl.loop(0, act.shape[0] // Q)
+    def _(chunk):
+        here = pl.ds(pl.multiple_of(chunk * Q, Q), Q)
+        sconv = silu(sact[here, :])
+        bmat, cmat = sconv[:, :state_size], sconv[:, state_size:]
+        scores = dot3(cmat, bmat, NT)
+        causal = triangle(True)
+        lane = lax.broadcasted_iota(jnp.int32, (Q, LANES), 1)
+        sums, turned = cum.at[here], cumt.at[here]
+        for p in range(act.shape[1] // LANES):
+            cols = slice(p * LANES, (p + 1) * LANES)
+            right = pair_stack(xs_ref[here, cols])
+            got = []
+            for j in range(2):
+                h = p * 2 + j
+                gap = sums[:, h : h + 1] - turned[h : h + 1, :]
+                mixing = scores * jnp.exp(jnp.where(causal, gap, -1e30))
+                wide = dg(jnp.concatenate(split(mixing), axis=1), right, NN)
+                got.append(wide[:, :LANES] + wide[:, LANES:])
+            out[here, cols] = out[here, cols] + jnp.where(lane < LANES // 2, got[0], got[1])
 
     @pl.when(c == count // 2)
     def _():
@@ -265,8 +345,7 @@
         incoming[...] = entered[...]
 
 
-STREAMS = 4
-GAP = 2
+STREAMS = 8
 SPAN = 83.0
 
 
@@ -282,10 +361,9 @@
     return jnp.log(block[:, :width].astype(F32)) * scale
 
 
-def swap_states(ns, packed, out, got_s, got_d, prefix, sems, reverse):
+def swap_states(ns, packed, logs, onehot, out, got_s, got_d, prefix, sems, reverse):
     seq = lax.axis_index("seq")
     own = out.shape[0] // ns
-    total = out.shape[0]
 
     def rows_of(j):
         return pl.ds(pl.multiple_of(j * own, own), own)
@@ -304,10 +382,9 @@
         other = (seq + k) % ns
         slot = other if arriving else seq
         part = packed.at[rows_of(other)]
-        decay = packed.at[pl.ds(total, HALO)]
         return (
             remote(part, got_s.at[slot], sems.at[0, k], sems.at[1, slot], other),
-            remote(decay, got_d.at[slot], sems.at[2, k], sems.at[3, slot], other),
+            remote(logs, got_d.at[slot], sems.at[2, k], sems.at[3, slot], other),
         )
 
     def answer(k, arriving):
@@ -324,14 +401,14 @@
 
     def turn():
         got_s[seq] = packed[rows_of(seq), :]
-        got_d[seq] = packed[total:, :]
+        got_d[seq] = logs[...]
         for k in range(1, ns):
             for copy in copies(k, True):
                 copy.wait_recv()
         carry = jnp.zeros((own, out.shape[1]), F32)
         for i in reversed(range(ns)) if reverse else range(ns):
             prefix[i] = carry
-            carry = carry * got_d[i, 0:1, :] + got_s[i]
+            carry = carry * spread(jnp.exp(got_d[i]), onehot[...])[:1] + got_s[i]
         for k in range(1, ns):
             answer(k, False).start()
         out[rows_of(seq), :] = prefix[seq]
@@ -351,7 +428,7 @@
     own = shape[0] // ns
     return [
         pltpu.VMEM((ns, own, shape[1]), F32),
-        pltpu.VMEM((ns, HALO, shape[1]), F32),
+        pltpu.VMEM((ns, HALO, LANES), F32),
         pltpu.VMEM((ns, own, shape[1]), F32),
         pltpu.SemaphoreType.DMA((6, ns)),
     ]
@@ -460,17 +537,21 @@
                 hand_on(me + s, h, False).start()
 
     def slot(t):
-        for h in range(STREAMS):
-            u = t - GAP * h
-            if 0 <= u < n - 1:
-                chain(h, u)
-            if u == n - 1:
-                finish(h)
-            if n - 1 < u < 2 * n - 1:
-                relay(h, u - n + 1)
+        for u in range(2 * n - 2, -1, -1):
+            h = t - u
+
+            @pl.when((h >= 0) & (h < STREAMS))
+            def _():
+                if u < n - 1:
+                    chain(h, u)
+                elif u == n - 1:
+                    finish(h)
+                else:
+                    relay(h, u - n + 1)
 
     def drain():
-        for h in range(STREAMS):
+        @pl.loop(0, STREAMS)
+        def _(h):
             for i in range(n):
 
                 @pl.when(i > me)
@@ -493,7 +574,7 @@
 
 
 def slots_of(n):
-    return GAP * (STREAMS - 1) + 2 * n - 1
+    return STREAMS - 1 + 2 * n - 1
 
 
 def greet(n, ns):
@@ -520,7 +601,7 @@
     got_a, got_b, got_s, got_c, mine_b = refs[19:24]
     sa_sem, ra_sem, sb_sem, rb_sem, ss_sem, rs_sem, sc_sem, rc_sem = refs[24:]
     me, seq = lax.axis_index("head"), lax.axis_index("seq")
-    tokens, width = part.shape
+    tokens, _ = part.shape
     span = tokens // STREAMS
     barrier = greet(n, ns)
 
@@ -550,7 +631,7 @@
         return states_ref.at[pl.ds(pl.multiple_of(j * own, own), own)]
 
     def compute(h):
-        where = pl.ds(h * span, span)
+        where = pl.ds(pl.multiple_of(h * span, span), span)
         total = None
         for left, right, dim, col in zip(lefts, rights, dims, cols):
             value = left[where, :] if col is None else left[where, col[0] : col[1]]
@@ -558,65 +639,72 @@
             total = term if total is None else total + term
         part[where, :] = total
         seen = total * (hidden_ref[where, :].astype(F32) * inv_ref[where, :])
-        row = jnp.sum(seen, axis=0, keepdims=True)
-        mine_b[0:1, :] = row if h == 0 else mine_b[0:1, :] + row
-
-    for t in range(slots_of(n)):
-        for h in range(STREAMS):
-            if t == GAP * h:
-                compute(h)
-        if t == 0:
-            pl.semaphore_wait(barrier, n + ns - 2)
+        mine_b[0:1, :] = mine_b[0:1, :] + jnp.sum(seen, axis=0, keepdims=True)
+
+    mine_b[...] = jnp.zeros_like(mine_b)
+    mine_b[8:16, : small_b.shape[1]] = small_b[...]
+    compute(0)
+    pl.semaphore_wait(barrier, n + ns - 2)
+    for k in range(1, ns):
+        to_seq(small_a, got_a, sa_sem, ra_sem, k).start()
+        to_seq(states_at((seq + k) % ns), got_s, ss_sem, rs_sem, k).start()
+
+    @pl.loop(0, STREAMS - 1)
+    def _(t):
         slot(t)
-        if t == 1:
-            for k in range(1, ns):
-                to_seq(small_a, got_a, sa_sem, ra_sem, k).start()
-                to_seq(states_at((seq + k) % ns), got_s, ss_sem, rs_sem, k).start()
-        if t == GAP * (STREAMS - 1):
-            mine_b[8:16, :] = jnp.zeros((8, width), F32)
-            mine_b[8:16, : small_b.shape[1]] = small_b[...]
-            for k in range(1, ns):
-                to_seq(mine_b, got_b, sb_sem, rb_sem, k).start()
-        if t == slots_of(n) - 2:
-            total = small_a[...]
-            for k in range(1, ns):
-                from_seq(small_a, got_a, sa_sem, ra_sem, k).wait_recv()
-                total = total + got_a[(seq + k) % ns]
-            sum_a[...] = total
-            total = states_at(seq)[...]
-            for k in range(1, ns):
-                from_seq(states_at(seq), got_s, ss_sem, rs_sem, k).wait_recv()
-                total = total + got_s[(seq + k) % ns]
-            sum_s[...] = total
-            total = mine_b[...]
-            for k in range(1, ns):
-                from_seq(mine_b, got_b, sb_sem, rb_sem, k).wait_recv()
-                total = total + got_b[(seq + k) % ns]
-            sum_b[...] = total
-
-            def to_head(k):
-                return pltpu.make_async_remote_copy(
-                    src_ref=sum_b,
-                    dst_ref=got_c.at[me],
-                    send_sem=sc_sem.at[k],
-                    recv_sem=rc_sem.at[me],
-                    device_id={"head": (me + k) % n},
-                    device_id_type=MESH_ID,
-                )
-
-            def from_head(k):
-                other = (me + k) % n
-                return pltpu.make_async_remote_copy(
-                    src_ref=sum_b,
-                    dst_ref=got_c.at[other],
-                    send_sem=sc_sem.at[k],
-                    recv_sem=rc_sem.at[other],
-                    device_id={"head": other},
-                    device_id_type=MESH_ID,
-                )
-
-            for k in range(1, n):
-                to_head(k).start()
+        compute(t + 1)
+
+    for k in range(1, ns):
+        to_seq(mine_b, got_b, sb_sem, rb_sem, k).start()
+
+    @pl.loop(STREAMS - 1, slots_of(n) - 2)
+    def _(t):
+        slot(t)
+
+    total = small_a[...]
+    for k in range(1, ns):
+        from_seq(small_a, got_a, sa_sem, ra_sem, k).wait_recv()
+        total = total + got_a[(seq + k) % ns]
+    sum_a[...] = total
+    total = states_at(seq)[...]
+    for k in range(1, ns):
+        from_seq(states_at(seq), got_s, ss_sem, rs_sem, k).wait_recv()
+        total = total + got_s[(seq + k) % ns]
+    sum_s[...] = total
+    total = mine_b[...]
+    for k in range(1, ns):
+        from_seq(mine_b, got_b, sb_sem, rb_sem, k).wait_recv()
+        total = total + got_b[(seq + k) % ns]
+    sum_b[...] = total
+
+    def to_head(k):
+        return pltpu.make_async_remote_copy(
+            src_ref=sum_b,
+            dst_ref=got_c.at[me],
+            send_sem=sc_sem.at[k],
+            recv_sem=rc_sem.at[me],
+            device_id={"head": (me + k) % n},
+            device_id_type=MESH_ID,
+        )
+
+    def from_head(k):
+        other = (me + k) % n
+        return pltpu.make_async_remote_copy(
+            src_ref=sum_b,
+            dst_ref=got_c.at[other],
+            send_sem=sc_sem.at[k],
+            recv_sem=rc_sem.at[other],
+            device_id={"head": other},
+            device_id_type=MESH_ID,
+        )
+
+    for k in range(1, n):
+        to_head(k).start()
+
+    @pl.loop(slots_of(n) - 2, slots_of(n))
+    def _(t):
+        slot(t)
+
     total = sum_b[...]
     for k in range(1, n):
         from_head(k).wait_recv()
@@ -666,20 +754,17 @@
     )(*lefts, *rights, *sums)
 
 
-def result_kernel(code, hidden, out):
-    out[...] = hidden[...].astype(F32) + decode(code[...], out.shape[1])
-
-
 def turn_kernel(value, out):
     high = value.shape[0]
     more = jnp.zeros((-high % LANES, value.shape[1]), F32)
     out[...] = jnp.concatenate([value[...], more], axis=0).T[:, :high]
 
 
-def hidden_kernel(code, hidden, cotangent, inv, gain, out):
+def finish_kernel(branch, code, hidden, cotangent, inv, gain, result, out):
     width = out.shape[1]
+    resid = hidden[...].astype(F32)
+    result[...] = resid + decode(branch[...], width)
     grad = decode(code[...], width) * gain[...]
-    resid = hidden[...].astype(F32)
     scale = inv[...]
     dots = jnp.sum(grad * resid, axis=1, keepdims=True) * (1.0 / width)
     out[...] = (
@@ -688,16 +773,16 @@
 
 
 def rows_of_sums(square, cross):
-    ones = jnp.ones((HALO, square.shape[1]), BF16)
-    (sh, sl), (ch, cl) = split(square), split(cross)
-    first = dg(ones, sh, NT) + dg(ones, sl, NT)
-    second = dg(ones, ch, NT) + dg(ones, cl, NT)
-    row = lax.broadcasted_iota(jnp.int32, first.shape, 0)
-    return jnp.where(row == 0, first, second)
+    first = jnp.sum(square, axis=1, keepdims=True)
+    second = jnp.sum(cross, axis=1, keepdims=True)
+    lane = lax.broadcasted_iota(jnp.int32, (square.shape[0], LANES), 1)
+    columns = jnp.where(lane == 0, first, jnp.where(lane == 1, second, 0.0))
+    parts = [columns[r : r + Q].T[:HALO] for r in range(0, square.shape[0], Q)]
+    return jnp.concatenate(parts, axis=1)
 
 
 def middle_kernel(
-    n, yloc, act, sact, cum, sin, before_log, total_log, incoming, gate, gyn, params, onehot,
+    n, yloc, act, sact, cum, sin, before_log, incoming, gate, gyn, params, onehot,
     y_o, ynorm_o, gpre_o, gssd_o, dout_o, dev_o, rows_o,
     keep, mine, got, adj, ssem, rsem,
 ):
@@ -708,7 +793,8 @@
     state_size = bmat_width(sact)
     hot = onehot[...]
     gain = params[5:6, :]
-    where = pl.ds(pl.multiple_of(c * Q, Q), Q)
+    height = gate.shape[0]
+    where = pl.ds(pl.multiple_of(c * height, height), height)
     barrier = pltpu.get_barrier_semaphore()
 
     def copy(k, arriving):
@@ -737,9 +823,13 @@
 
     @pl.when(i < count)
     def _():
-        carry = spread(jnp.broadcast_to(jnp.exp(before_log[...]), (HALO, LANES)), hot)[:1]
-        state = sin[...] + carry * incoming[...]
-        y = yloc[...] + growth * dot3(cmat, state, NN)
+        ahead = []
+        for j in range(height // Q):
+            part = slice(j * Q, (j + 1) * Q)
+            carry = spread(jnp.broadcast_to(jnp.exp(before_log[j]), (HALO, LANES)), hot)[:1]
+            state = sin[j * state_size : (j + 1) * state_size, :] + carry * incoming[...]
+            ahead.append(dot3(cmat[part], state, NN))
+        y = yloc[...] + growth * jnp.concatenate(ahead, axis=0)
         y_o[...] = y
         keep[where, :] = y
         gated = y * gsilu
@@ -766,7 +856,14 @@
     @pl.when(i >= count)
     def _():
         total = mine[:, where]
-        columns = jnp.concatenate([total, jnp.zeros((Q - HALO, Q), F32)], axis=0).T
+        blank = jnp.zeros((Q - HALO, Q), F32)
+        columns = jnp.concatenate(
+            [
+                jnp.concatenate([total[:, r : r + Q], blank], axis=0).T
+                for r in range(0, height, Q)
+            ],
+            axis=0,
+        )
         inv = lax.rsqrt(columns[:, 0:1] / DI + EPS)
         cross = columns[:, 1:2] / DI
         yv = keep[where, :]
@@ -779,24 +876,26 @@
         gssd = ggated * gsilu
         gssd_o[...] = gssd
         rows_o[1:2, :] = rows_o[1:2, :] + jnp.sum(gssd * silu(act[...]), axis=0, keepdims=True)
-        dout_o[...] = adj[...]
-        decay = spread(jnp.broadcast_to(jnp.exp(cum[Q - 1 :, :]), (HALO, LANES)), hot)[:1]
-        adj[...] = adj[...] * decay + dot3(cmat, gssd * growth, TN)
+        scaled = gssd * growth
+        for j in reversed(range(height // Q)):
+            part = slice(j * Q, (j + 1) * Q)
+            dout_o[j * state_size : (j + 1) * state_size, :] = adj[...]
+            last = cum[(j + 1) * Q - 1 : (j + 1) * Q, :]
+            decay = spread(jnp.broadcast_to(jnp.exp(last), (HALO, LANES)), hot)[:1]
+            adj[...] = adj[...] * decay + dot3(cmat[part], scaled[part], TN)
 
     @pl.when(i == 2 * count - 1)
     def _():
-        dev_o[:state_size, :] = adj[...]
-        whole_log = jnp.broadcast_to(jnp.exp(total_log[...]), (HALO, LANES))
-        dev_o[state_size:, :] = spread(whole_log, hot)
+        dev_o[...] = adj[...]
 
 
 def back_kernel(
     n, ns, act, sact, y, gssd, step, step_pre, cum, cumt, sin, dout, before_log, total_log, incoming,
-    ynorm, proj_output, packed,
+    ynorm, proj_output, packed, normed,
     params, onehot, rows_in, pre, pre_prev, pre_halo, spre, spre_prev, spre_halo,
-    gin_o, gsb_out, small_a, small_b, code_out,
-    gsb_o, gstep, xs_ref, u_ref, st_ref, gext, sext, pext, spext, halo_send, halo_got, shalo_send, shalo_got,
-    psum, pgot, h_sem, p_send, p_recv, g_send, g_recv,
+    gin_o, gsb_out, small_a, small_b, code_out, win_o,
+    gin_all, gsb_o, gstep, xs_ref, u_ref, st_ref, gext, sext, pext, spext, halo_send, halo_got, shalo_send, shalo_got,
+    psum, psend, pgot, h_sem, p_send, p_recv, g_send, g_recv,
     later, got_states, got_decays, prefix, swap_sems, all_ref, part, *chain_refs,
 ):
     i = pl.program_id(0)
@@ -804,7 +903,7 @@
     count = pl.num_programs(0) - 2
     total_chunks = psum.shape[0] // Q
     begin, turn, end = swap_states(
-        ns, packed, later, got_states, got_decays, prefix, swap_sems, True
+        ns, packed, total_log, onehot, later, got_states, got_decays, prefix, swap_sems, True
     )
     slot, drain = chains(n, all_ref, part, *chain_refs)
     span = part.shape[0] // STREAMS
@@ -827,10 +926,13 @@
     def chunk_rows(k):
         return pl.ds(pl.multiple_of(k * Q, Q), Q)
 
+    def code_rows(k):
+        return pl.ds(pl.multiple_of(k * (Q + 16), 16), Q + 16)
+
     def to_owner(k):
         return pltpu.make_async_remote_copy(
-            src_ref=psum.at[chunk_rows(k)],
-            dst_ref=pgot.at[me, chunk_rows(k // n)],
+            src_ref=psend.at[code_rows(k)],
+            dst_ref=pgot.at[me, code_rows(k // n)],
             send_sem=p_send.at[k],
             recv_sem=p_recv.at[me, k // n],
             device_id={"head": k % n},
@@ -839,8 +941,8 @@
 
     def from_other(j, g):
         return pltpu.make_async_remote_copy(
-            src_ref=psum.at[chunk_rows(g)],
-            dst_ref=pgot.at[j, chunk_rows(g)],
+            src_ref=psend.at[code_rows(g)],
+            dst_ref=pgot.at[j, code_rows(g)],
             send_sem=p_send.at[g],
             recv_sem=p_recv.at[j, g],
             device_id={"head": j},
@@ -868,17 +970,22 @@
         small_a[5:7, :] = rows_in[0:2, :]
 
         def compute(h):
-            where = pl.ds(h * span, span)
+            where = pl.ds(pl.multiple_of(h * span, span), span)
             part[where, :] = dg(ynorm[where, :], proj_output[...], NN)
 
         compute(0)
         pl.semaphore_wait(barrier, n + ns - 2)
         begin()
-        slot(0)
-        compute(1)
-        slot(1)
-        for h in range(2, STREAMS):
+
+        @pl.loop(0, 2)
+        def _(t):
+            slot(t)
+            compute(t + 1)
+
+        @pl.loop(3, STREAMS)
+        def _(h):
             compute(h)
+
         turn()
         slot(2)
         end()
@@ -906,7 +1013,7 @@
             return spread(jnp.broadcast_to(jnp.exp(value), (HALO, LANES)), hot)[:1]
 
         state = sin[...] + row(before_log[...]) * incoming[...]
-        adj = dout[...] + row(total_log[...] - before_log[...] - last) * later[...]
+        adj = dout[...] + row(total_log[0:1, :] - before_log[...] - last) * later[...]
         to_end = spread(jnp.exp(last - cumv), hot)
         u_state = to_end * dot3(bmat, adj, NN)
         ends = row(last) * jnp.sum(adj * state, axis=0, keepdims=True) + jnp.sum(
@@ -1017,11 +1124,17 @@
         inner = gext.shape[1]
         gin_o[:, :inner] = conv_back(gext, pext, 0, inner, small_a).astype(BF16)
         gin_o[:, inner:] = gstep[:Q, :]
+        gin_all[chunk_rows(c - 1), :] = gin_o[...]
         mine = conv_back(sext, spext, 8, two, small_b)
         psum[chunk_rows(c - 1), :] = mine
 
         @pl.when((c - 1) % n != me)
         def _():
+            top = jnp.max(jnp.abs(mine), axis=0, keepdims=True)
+            scale = (top * 1.004 + 1e-30).astype(BF16)
+            first = pl.multiple_of((c - 1) * (Q + 16), 16)
+            psend[pl.ds(first, Q), :] = jnp.exp(mine * (SPAN / scale.astype(F32))).astype(BF16)
+            psend[pl.ds(first + Q, 16), :] = jnp.broadcast_to(scale, (16, two))
             to_owner(c - 1).start()
 
     @pl.when((c >= 0) & (c < count))
@@ -1029,6 +1142,13 @@
         gext[:Q, :] = u_ref[...]
         gstep[:Q, :] = gstep[Q:, :]
         sext[:Q, :] = sext[Q + HALO :, :]
+
+    @pl.when(c == count)
+    def _():
+        @pl.loop(0, win_o.shape[0] // 256)
+        def _(m):
+            cols = pl.ds(pl.multiple_of(m * 256, 256), 256)
+            win_o[cols, :] = dg(normed[:, cols], gin_all[...], TN)
 
     for g in range(groups):
 
@@ -1039,7 +1159,9 @@
             for k in range(1, n):
                 j = (me + k) % n
                 from_other(j, g).wait_recv()
-                total = total + pgot[j, g * Q : (g + 1) * Q, :]
+                first = g * (Q + 16)
+                scale = pgot[j, first + Q : first + Q + 16, :].astype(F32)[:1] * (1.0 / SPAN)
+                total = total + jnp.log(pgot[j, first : first + Q, :].astype(F32)) * scale
             gsb_o[own, :] = total.astype(BF16)
             for k in range(1, n):
                 give(k, g, False).start()
@@ -1059,25 +1181,19 @@
             def _():
                 to_owner(k).wait_send()
 
-    slots, last_step = slots_of(n), count + 1
-    for t in range(3, slots):
-
-        @pl.when(i == 1 + (t - 3) * last_step // (slots - 3))
-        def _():
+    last_step = count + 1
+    more = slots_of(n) - 3
+
+    @pl.when(i >= 1)
+    def _():
+        @pl.loop(3 + (i - 1) * more // last_step, 3 + i * more // last_step)
+        def _(t):
             slot(t)
 
     @pl.when(i == last_step)
     def _():
         drain()
         code_out[...] = all_ref[...]
-
-
-def matmul_low(left, right):
-    return jnp.dot(left, right, preferred_element_type=F32)
-
-
-def times_transposed(left, right):
-    return dg(left, right, NT)
 
 
 def transposed_times(left, right):
@@ -1103,9 +1219,7 @@
     cotangent,
 ):
     seg_count = lax.axis_size("seq")
-    seg_index = lax.axis_index("seq")
     head_index = lax.axis_index("head")
-    is_first = seg_index == 0
     tokens, width = hidden.shape
     heads = proj_step.shape[1]
     inner = proj_gate.shape[1]
@@ -1120,25 +1234,50 @@
 
     n, ns = lax.axis_size("head"), seg_count
 
-    def turned(value, k):
-        return lax.ppermute(value, "head", [(i, (i + k) % n) for i in range(n)])
-
-    pieces = [proj_states] + [turned(proj_states, k) for k in range(1, n)]
-    hidden_halo = shifted(hidden[tokens - HALO :], "seq", 1)
-
-    def norm(rows_):
-        value = rows_.astype(F32)
-        inv = lax.rsqrt(jnp.mean(value * value, axis=-1, keepdims=True) + EPS)
-        return inv, (value * inv * gain_full[None, :]).astype(BF16)
-
-    inv_rms, normed = norm(hidden)
-    normed_halo = norm(hidden_halo)[1]
-    keep = jnp.where(is_first, 0.0, 1.0)
+    stripe = 256
+
+    def striped(size):
+        return pl.BlockSpec((stripe, size), lambda c: (c, 0))
+
+    def fixed(shape, at=0):
+        return pl.BlockSpec(shape, lambda c: (at, 0), pipeline_mode=pl.Buffered(1))
+
+    (
+        normed, inv_rms, input_pre, gate_pre, grad_ynorm, proj_states_full, normed_halo, input_halo,
+    ) = call(
+        functools.partial(front_kernel, n, ns),
+        (tokens // stripe,),
+        [
+            (hidden, striped(width)),
+            (cotangent, striped(width)),
+            (hidden, fixed((16, width), tokens // 16 - 1)),
+            (gain_full[None, :], fixed((1, width))),
+            (proj_input, fixed((width, inner))),
+            (proj_gate, fixed((width, inner))),
+            (proj_output, fixed((inner, width))),
+            (proj_states, fixed((row_width, 2 * state_size))),
+        ],
+        [
+            (sds((tokens, width), BF16), striped(width)),
+            (sds((tokens, 1)), striped(1)),
+            (sds((tokens, inner)), striped(inner)),
+            (sds((tokens, inner)), striped(inner)),
+            (sds((tokens, inner)), striped(inner)),
+            (sds((width, 2 * state_size), BF16), whole((width, 2 * state_size))),
+            (sds((16, width), BF16), whole((16, width))),
+            (sds((HALO, inner)), whole((HALO, inner))),
+        ],
+        scratch=[
+            pltpu.VMEM((width, 2 * state_size), BF16),
+            pltpu.VMEM((16, width), BF16),
+            pltpu.SemaphoreType.DMA((n,)),
+            pltpu.SemaphoreType.DMA((n,)),
+            pltpu.SemaphoreType.DMA((2,)),
+        ],
+        flops=6 * tokens * inner * width,
+        collective=6,
+    )
     proj_step_wide = pad_heads(proj_step)
-    input_pre = matmul_low(normed, proj_input)
-    input_halo = matmul_low(normed_halo, proj_input) * keep
-    gate_pre = matmul_low(normed, proj_gate)
-    grad_ynorm = times_transposed(cotangent, proj_output)
     two = 2 * state_size
     flat = jnp.concatenate(
         [
@@ -1157,98 +1296,100 @@
     )
     hot = (onehot, whole((LANES, inner)))
     state_rows = pl.BlockSpec((state_size, inner), lambda c: (c, 0))
-    packed_shape = (state_size + HALO, inner)
+    packed_shape = (state_size, inner)
+    logs_shape = (HALO, LANES)
+    big = GROUP * Q
     (
         act, sact, states_pre, states_halo, step_pre, step, cum, cumt, sin, packed, total_log,
         before_log, params,
     ) = call(
-        functools.partial(states_kernel, n),
-        (count,),
+        states_kernel,
+        (count // GROUP,),
         [
-            (input_pre, rows(inner)),
-            (input_pre, before(inner)),
+            (input_pre, rows(inner, big)),
+            (input_pre, before(inner, big)),
             (input_halo, whole((HALO, inner))),
-            (normed, rows(width)),
-            (normed_halo, whole((HALO, width))),
+            (normed, rows(width, big)),
+            (normed_halo, whole((16, width))),
             (proj_step_wide, whole((width, LANES))),
             (vec, whole(vec.shape)),
             (conv_input, whole(conv_input.shape)),
             (conv_states, whole(conv_states.shape)),
+            (proj_states_full, whole((width, two))),
             hot,
-        ]
-        + [(piece, whole(piece.shape)) for piece in pieces],
+        ],
         [
-            (sds((tokens, inner)), rows(inner)),
-            (sds((tokens, two)), rows(two)),
-            (sds((tokens, two)), rows(two)),
+            (sds((tokens, inner)), rows(inner, big)),
+            (sds((tokens, two)), rows(two, big)),
+            (sds((tokens, two)), rows(two, big)),
             (sds((HALO, two)), whole((HALO, two))),
-            (sds((tokens, LANES)), rows(LANES)),
-            (sds((tokens, LANES)), rows(LANES)),
-            (sds((tokens, LANES)), rows(LANES)),
-            (sds((tokens, LANES)), rows(LANES)),
-            (sds((count * state_size, inner)), state_rows),
+            (sds((tokens, LANES)), rows(LANES, big)),
+            (sds((tokens, LANES)), rows(LANES, big)),
+            (sds((tokens, LANES)), rows(LANES, big)),
+            (sds((tokens, LANES)), rows(LANES, big)),
+            (sds((count * state_size, inner)), pl.BlockSpec((GROUP * state_size, inner), lambda c: (c, 0))),
             (sds(packed_shape), whole(packed_shape)),
-            (sds((1, LANES)), whole((1, LANES))),
-            (sds((count, 1, LANES)), pl.BlockSpec((None, 1, LANES), lambda c: (c, 0, 0))),
+            (sds((HALO, LANES)), whole((HALO, LANES))),
+            (sds((count, 1, LANES)), pl.BlockSpec((GROUP, 1, LANES), lambda c: (c, 0, 0))),
             (sds((16, inner)), whole((16, inner))),
         ],
         scratch=[
-            pltpu.VMEM((Q + HALO, inner), F32),
-            pltpu.VMEM((Q + HALO, two), F32),
+            pltpu.VMEM((big + HALO, inner), F32),
+            pltpu.VMEM((big + HALO, two), F32),
             pltpu.VMEM((state_size, inner), F32),
             pltpu.VMEM((1, LANES), F32),
-            pltpu.VMEM((width, two), BF16),
         ],
         flops=10 * tokens * inner * state_size,
     )
     par = (params, whole((16, inner)))
-    packed, gate_pre, grad_ynorm = lax.optimization_barrier((packed, gate_pre, grad_ynorm))
     yloc, incoming = call(
         functools.partial(intra_kernel, ns),
-        (count,),
+        (count // GROUP,),
         [
-            (act, rows(inner)),
-            (sact, rows(two)),
-            (step, rows(LANES)),
-            (cum, rows(LANES)),
-            (cumt, rows(LANES)),
+            (act, rows(inner, big)),
+            (sact, rows(two, big)),
+            (step, rows(LANES, big)),
+            (cum, rows(LANES, big)),
+            (cumt, rows(LANES, big)),
             par,
             hot,
             (packed, whole(packed_shape)),
+            (total_log, whole(logs_shape)),
         ],
         [
-            (sds((tokens, inner)), rows(inner)),
+            (sds((tokens, inner)), rows(inner, big)),
             (sds((state_size, inner)), whole((state_size, inner))),
         ],
-        scratch=[pltpu.VMEM((Q, inner), F32), pltpu.VMEM((state_size, inner), F32)]
+        scratch=[pltpu.VMEM((big, inner), F32), pltpu.VMEM((state_size, inner), F32)]
         + swap_scratch(ns, (state_size, inner)),
         flops=12 * tokens * inner * Q,
         collective=5,
     )
 
+    half = count // GROUP
+
     def both(i):
-        return jnp.where(i < count, i, 2 * count - 1 - i)
+        return jnp.where(i < half, i, 2 * half - 1 - i)
 
     def fore(i):
-        return jnp.minimum(i, count - 1)
+        return jnp.minimum(i, half - 1)
 
     def aft(i):
-        return jnp.minimum(2 * count - 1 - i, count - 1)
-
-    def at(size, which, height=Q):
+        return jnp.minimum(2 * half - 1 - i, half - 1)
+
+    def at(size, which, height=big):
         return pl.BlockSpec((height, size), lambda i: (which(i), 0))
 
     y, ynorm, grad_gate_pre, grad_ssd, dout, packed_back, grad_rows = call(
         functools.partial(middle_kernel, n),
-        (2 * count,),
+        (2 * half,),
         [
             (yloc, at(inner, fore)),
             (act, at(inner, aft)),
             (sact, at(two, both)),
             (cum, at(LANES, both)),
-            (sin, at(inner, fore, state_size)),
-            (before_log, pl.BlockSpec((None, 1, LANES), lambda i: (fore(i), 0, 0))),
-            (total_log, whole((1, LANES))),
+            (sin, at(inner, fore, GROUP * state_size)),
+            (before_log, pl.BlockSpec((GROUP, 1, LANES), lambda i: (fore(i), 0, 0))),
             (incoming, whole((state_size, inner))),
             (gate_pre, at(inner, both)),
             (grad_ynorm, at(inner, both)),
@@ -1260,7 +1401,7 @@
             (sds((tokens, inner), BF16), at(inner, aft)),
             (sds((tokens, inner), BF16), at(inner, aft)),
             (sds((tokens, inner)), at(inner, aft)),
-            (sds((count * state_size, inner)), at(inner, aft, state_size)),
+            (sds((count * state_size, inner)), at(inner, aft, GROUP * state_size)),
             (sds(packed_shape), whole(packed_shape)),
             (sds((HALO, inner)), whole((HALO, inner))),
         ],
@@ -1309,7 +1450,7 @@
 
     dma = pltpu.SemaphoreType.DMA
     groups = count // n
-    grad_in_b, grad_states_b, small_a, small_b, branch_code = call(
+    grad_in_b, grad_states_b, small_a, small_b, branch_code, local_proj_in = call(
         functools.partial(back_kernel, n, ns),
         (count + 2,),
         [
@@ -1327,11 +1468,12 @@
                 before_log,
                 pl.BlockSpec((None, 1, LANES), lambda i: (now(i), 0, 0)),
             ),
-            (total_log, whole((1, LANES))),
+            (total_log, whole(logs_shape)),
             (incoming, once((state_size, inner))),
             (ynorm, once((tokens, inner))),
             (proj_output, once((inner, width))),
             (packed_back, once(packed_shape)),
+            (normed, once((tokens, width))),
             par,
             hot,
             (grad_rows, whole((HALO, inner))),
@@ -1348,8 +1490,10 @@
             (sds((16, inner)), whole((16, inner))),
             (sds((HALO, two)), whole((HALO, two))),
             (sds((tokens, width + LANES), BF16), once((tokens, width + LANES))),
+            (sds((width, inner + LANES)), once((width, inner + LANES))),
         ],
         scratch=[
+            pltpu.VMEM((tokens, inner + LANES), BF16),
             pltpu.VMEM((tokens, two), BF16),
             pltpu.VMEM((2 * Q, LANES), BF16),
             pltpu.VMEM((Q, inner), F32),
@@ -1364,7 +1508,8 @@
             pltpu.VMEM((HALO, two), F32),
             pltpu.VMEM((HALO, two), F32),
             pltpu.VMEM((tokens, two), F32),
-            pltpu.VMEM((n, groups * Q, two), F32),
+            pltpu.VMEM((count * (Q + 16), two), BF16),
+            pltpu.VMEM((n, groups * (Q + 16), two), BF16),
             dma((4,)),
             dma((count,)),
             dma((n, groups)),
@@ -1378,19 +1523,11 @@
         flops=40 * tokens * inner * Q,
         collective=4,
     )
-    result = call(
-        result_kernel,
-        (count,),
-        [(branch_code, rows(width + LANES)), (hidden, rows(width))],
-        [(sds((tokens, width)), rows(width))],
-        flops=20 * tokens * width,
-    )[0]
     row_start = head_index * row_width
     own_states = lax.dynamic_update_slice_in_dim(
         jnp.zeros((width, two), BF16), proj_states, row_start, 0
     )
     normed_rows = lax.dynamic_slice_in_dim(normed, row_start, row_width, 1)
-    local_proj_in = transposed_times(normed, grad_in_b)
     local_proj_states = transposed_times(grad_states_b, normed_rows)
     summed_in = lax.psum_scatter(local_proj_in, "seq", scatter_dimension=0, tiled=True)
     grad_code, sum_a, sum_b, grad_proj_states = reduce_over_heads(
@@ -1405,19 +1542,20 @@
         2,
         (hidden, inv_rms, small_a, small_b, local_proj_states),
     )
-    grad_hidden = call(
-        hidden_kernel,
-        (count,),
+    result, grad_hidden = call(
+        finish_kernel,
+        (tokens // stripe,),
         [
-            (grad_code, rows(width + LANES)),
-            (hidden, rows(width)),
-            (cotangent, rows(width)),
-            (inv_rms, rows(1)),
-            (gain_full[None, :], whole((1, width))),
+            (branch_code, striped(width + LANES)),
+            (grad_code, striped(width + LANES)),
+            (hidden, striped(width)),
+            (cotangent, striped(width)),
+            (inv_rms, striped(1)),
+            (gain_full[None, :], fixed((1, width))),
         ],
-        [(sds((tokens, width)), rows(width))],
-        flops=20 * tokens * width,
-    )[0]
+        [(sds((tokens, width)), striped(width)), (sds((tokens, width)), striped(width))],
+        flops=40 * tokens * width,
+    )
     return (
         result,
         grad_hidden,

time: 430 us -> 388 us (0.902); the launches traced: 423 us -> 387 us
  matrix products: 36.5 us -> 14.1 us
  starting transfers between devices: 9.05 us -> 0.52 us
    dot_general x3 -> x0, matrix products: 11.2 us -> none  [matmul_low(): return jnp.dot(left, right, preferred_element_type=F32)]
    dot_general x5 -> x3, matrix products: 25.3 us -> 14.1 us  [dg(): return lax.dot_general(left, right, dims, preferred_element_type=F32)]
    ppermute x4 -> x0, starting transfers between devices: 8.93 us -> none  [the longest x3 7.04 us: turned(): return lax.ppermute(value, 'head', [(i, (i + k) % n) for i in range(n)])]
    unnamed x43 -> x17, local copies, waits for them, and re-layouts: 5.53 us -> 9.07 us
  transfers between devices with their start and end apart: 7 -> 3, of which waited for: 0 -> 0; matrix products, arithmetic and copies ran while one was open for 13% -> 6% of each run, Pallas kernels for 64% -> 64%
where the time goes in v3:
time: 388 us; the launch traced here: 387 us
  Pallas kernels  333 us (86%)
  local copies, waits for them, and re-layouts  22.7 us (6%)
  matrix products  14.1 us (4%)
  between operations  13.9 us (4%)
    pallas_call x6, Pallas kernels, call(): pl.pallas_call(kernel, grid=grid, in_specs=in_specs, out_specs=[spec for...  224 us
    pallas_call x1, Pallas kernels, reduce_over_heads(): pl.pallas_call(functools.partial(reduce_kernel, n, ns, dims, cols), in_sp...  107 us
    dot_general x3, matrix products, dg(): return lax.dot_general(left, right, dims, preferred_element_type=F32)  14.1 us
    unnamed x17, local copies, waits for them, and re-layouts  9.07 us
  transfers between devices with their start and end apart: 3, of which 0 were waited for; matrix products, arithmetic and copies ran while one was open for 6% of the time, Pallas kernels for 64%

profile of v3, /device:TPU:0, one launch (start us, length us, event | category | flops | bytes accessed | tf_op | source)
XLA Modules:
  0.0 387.1 jit_solution(6219128415416047092)
XLA Ops:
  7.2 0.0 reduce-scatter.8.cloned.1.call-start
  7.2 1.3 reshape.36.gain
  8.5 1.0 copy.33
  9.6 0.7 constant_dynamic-update-slice_fusion.5
  10.2 0.7 constant_dynamic-update-slice_fusion.4
  10.9 0.7 constant_dynamic-update-slice_fusion.3
  11.6 0.7 constant_dynamic-update-slice_fusion.2
  12.3 0.7 constant_dynamic-update-slice_fusion.1
  12.9 0.7 constant_dynamic-update-slice_fusion
  13.6 0.6 pad_bitcast_fusion.vec
  14.2 0.8 pad.18.step_w.refs_6_
  15.0 26.5 %shard_map.288 = (bf16[1024,1536]{1,0:T(8,128)(2,1)}, f32[1024,1]{1,0:T(8,128)}, f32[1024,768]{1,0:T(8,128)}, f32[1024,768]{1,0:T(8,128)}, f32[1024,768]{1,0:T(8...) custom-call(bf16[1024,1536]{1,0:T(8,128)(2,1)} %hidden.3, ...), custom_call_target="tpu_custom_call" | custom-call | flops 7247757312 | bytes 30164992 | tf_op jit(solution)/shard_map/pallas_call | solution.py:66
  41.6 13.1 %shard_map.289 = (f32[1024,768]{1,0:T(8,128)}, f32[1024,256]{1,0:T(8,128)}, f32[1024,256]{1,0:T(8,128)}, f32[8,256]{1,0:T(8,128)}, f32[1024,128]{1,0:T(8,128)}, ...) custom-call(f32[1024,768]{1,0:T(8,128)} %get-tuple-element.58.pre.pr, ...), custom_call_target="tpu_custom_call" | custom-call | flops 1006632960 | bytes 21852160 | tf_op jit(solution)/shard_map/pallas_call | solution.py:66
  54.7 17.0 %shard_map.290 = (f32[1024,768]{1,0:T(8,128)}, f32[128,768]{1,0:T(8,128)}) custom-call(f32[1024,768]{1,0:T(8,128)} %get-tuple-element.63.act, f32[1024,256]{1,0:T(8,128)} %get-tuple-element.64.sact, f32[1024,128]{1,0:T(8,128)} %get-tuple-element.65.step, f32[1024,128]{1,0:T(8,128)} %get-tuple-element.66.cum, f32[1024,128]{1,0:T(8,128)} %get-tuple-element.67.cumt, ...), custom_call_target="tpu_custom_call" | custom-call | flops 1207959552 | bytes 9949184 | tf_op jit(solution)/shard_map/pallas_call | solution.py:66
  71.6 0.0 copy-start.1
  71.6 27.7 %shard_map.291 = (f32[1024,768]{1,0:T(8,128)}, bf16[1024,768]{1,0:T(8,128)(2,1)}, bf16[1024,768]{1,0:T(8,128)(2,1)}, f32[1024,768]{1,0:T(8,128)}, f32[1024,768]{...) custom-call(f32[1024,768]{1,0:T(8,128)} %get-tuple-element.71.yloc, f32[1024,768]{1,0:T(8,128)} %get-tuple-element.63.act, ...), custom_call_target="tpu_custom_call" | custom-call | flops 1207959552 | bytes 30945280 | tf_op jit(solution)/shard_map/pallas_call | solution.py:66
  99.3 0.0 copy-done.1
  99.3 5.8 %convolution_bitcast_fusion = f32[1536,768]{1,0:T(8,128)} fusion(bf16[1024,768]{1,0:T(8,128)(2,1)} %get-tuple-element.81.ynorm, bf16[1024,1536]{1,0:T(8,128)(2,1)S(1)} %copy-done.1), kind=kOutput, calls=%fused_computation | convolution fusion | flops 2415919104 | bytes 9437184 | tf_op jit(solution)/shard_map/dot_general | solution.py:30
  105.1 0.0 reduce-scatter.8.cloned.1.call-update
  105.2 0.2 reduce-scatter.6.cloned.1.call-start
  105.4 129.5 %shard_map.292 = (bf16[1024,896]{1,0:T(8,128)(2,1)}, bf16[1024,256]{1,0:T(8,128)(2,1)}, f32[16,768]{1,0:T(8,128)}, f32[8,256]{1,0:T(8,128)}, bf16[1024,1664]{1,0:T(8,128)(2,1)}, /*index=5*/f32[1536,896]{1,0:T(8,128)}) custom-call(f32[1024,768]{1,0:T(8,128)} %get-tuple-element.63.act, f32[1024,256]{1,0:T(8,128)} %get-tuple-element.64.sact, ...), custom_call_target="tpu_custom_call" | custom-call | flops 4026531840 | bytes 46768128 | tf_op jit(solution)/shard_map/pallas_call | solution.py:66
  234.9 0.0 copy-start
  234.9 0.0 reduce-scatter.6.cloned.1.call-update
  235.0 0.3 reduce-scatter.4.cloned.1.call-start
  235.2 1.6 copy-done
  236.8 5.7 %fusion.3 = f32[1536,768]{1,0:T(8,128)} fusion(bf16[1024,1536]{1,0:T(8,128)(2,1)S(1)} %copy-done, bf16[1024,768]{1,0:T(8,128)(2,1)} %get-tuple-element.87.refs_0_), kind=kOutput, calls=%fused_computation.18 | convolution fusion | flops 2415919104 | bytes 9437184 | tf_op jit(solution)/shard_map/dot_general | solution.py:30
  242.5 0.0 copy-start.3
  242.5 0.0 reduce-scatter.4.cloned.1.call-update
  242.6 0.1 broadcast_in_dim.11
  242.6 0.9 copy-done.3
  243.6 0.0 copy-start.2
  243.6 2.6 fusion.refs_12_
  246.2 0.0 copy-done.2
  246.2 106.5 %reduce_heads.1 = (bf16[1024,1664]{1,0:T(8,128)(2,1)}, f32[16,768]{1,0:T(8,128)}, f32[16,1536]{1,0:T(8,128)}, f32[32,384]{1,0:T(8,128)}) custom-call(bf16[1024,768]{1,0:T(8,128)(2,1)} %get-tuple-element.87.refs_0_, bf16[1024,896]{1,0:T(8,128)(2,1)} %get-tuple-element.88.refs_1_.refs_2_, bf16[1024,896]{1,0:T(8,128)(2,1)} %get-tuple-element.88.refs_1_.refs_2_, ...), custom_call_target="tpu_custom_call" | custom-call | flops 8858370048 | bytes 157286400 | tf_op jit(solution)/shard_map/reduce_heads/pallas_call | solution.py:739
  352.7 1.3 slice.38
  354.0 1.3 slice.39
  355.3 1.3 slice.36
  356.6 1.5 slice_reduce_fusion.1
  358.1 0.1 reshape_squeeze.3
  358.2 0.6 reduce_sum.9
  358.8 10.6 %shard_map.293 = (f32[1024,1536]{1,0:T(8,128)}, f32[1024,1536]{1,0:T(8,128)}) custom-call(bf16[1024,1664]{1,0:T(8,128)(2,1)} %get-tuple-element.86.branch, bf16[1024,1664]{1,0:T(8,128)(2,1)} %get-tuple-element.93.code, bf16[1024,1536]{1,0:T(8,128)(2,1)} %hidden.3, bf16[1024,1536]{1,0:T(8,128)(2,1)} %cotangent.3, f32[1024,1]{1,0:T(8,128)} %get-tuple-element.90.refs_9_.inv, ...), custom_call_target="tpu_custom_call" | custom-call | flops 62914560 | bytes 25700352 | tf_op jit(solution)/shard_map/pallas_call | solution.py:66
  369.4 0.0 copy-start.4
  369.4 1.4 slice_reduce_fusion
  370.8 1.2 slice_bitcast_fusion
  372.0 0.0 reduce-scatter.8.cloned.1.call-done.value
  372.0 2.2 turn.1
  374.2 2.2 copy.36
  376.4 0.0 reduce-scatter.6.cloned.1.call-done
  376.4 0.9 slice.45
  377.3 0.7 copy.35
  378.0 1.9 slice.44
  380.0 0.0 reduce-scatter.4.cloned.1.call-done
  380.0 0.0 copy-done.4
  380.0 0.6 copy.46
  (2 shorter events, 0.0 us)
Async XLA Ops:
  7.2 364.9 %reduce-scatter.8.cloned.1.call-start = ((), (), s32[]{:S(2)}) async-start(), calls=%async_computation.5 | async-start | bytes 5308416 | tf_op jit(solution)/shard_map/reduce_scatter | solution.py:1421
  71.6 27.7 %copy-start.1 = (bf16[1024,1536]{1,0:T(8,128)(2,1)S(1)}, bf16[1024,1536]{1,0:T(8,128)(2,1)}, u32[]{:S(2)}) copy-start(bf16[1024,1536]{1,0:T(8,128)(2,1)} %cotangent.3) | copy-start | bytes 9437188
  105.2 271.3 %reduce-scatter.6.cloned.1.call-start = ((), (), s32[]{:S(2)}) async-start(), calls=%async_computation.4 | async-start | bytes 6193152 | tf_op jit(solution)/shard_map/reduce_scatter | solution.py:1532
  234.9 1.9 copy-start
  235.0 145.0 %reduce-scatter.4.cloned.1.call-start = ((), (), s32[]{:S(2)}) async-start(), calls=%async_computation.3 | async-start | bytes 5308416 | tf_op jit(solution)/shard_map/reduce_scatter | solution.py:1427
  242.5 1.0 copy-start.3
  243.6 2.6 copy-start.2
  369.4 10.5 %copy-start.4 = (f32[32,384]{1,0:T(8,128)S(1)}, f32[32,384]{1,0:T(8,128)}, u32[]{:S(2)}) copy-start(f32[32,384]{1,0:T(8,128)} %get-tuple-element.98) | copy-start | bytes 147460
Sparse Core Ops, SparseCore 0:
  105.3 52.3 reduce-scatter.7
  235.1 62.0 reduce-scatter.5
  301.2 59.1 reduce-scatter.3

commit v4 on v3

--- a/solution.py
+++ b/solution.py
@@ -22,7 +22,7 @@
 NN = (((1,), (0,)), ((), ()))
 NT = (((1,), (1,)), ((), ()))
 TN = (((0,), (0,)), ((), ()))
-VMEM_LIMIT = 60 * 1024 * 1024
+VMEM_LIMIT = 63 * 1024 * 1024
 MESH_ID = pl.DeviceIdType.MESH
 
 
@@ -121,27 +121,49 @@
     return total
 
 
+def line(vec, first, size):
+    return jnp.concatenate([vec[r : r + 1, :] for r in range(first, first + size // LANES)], axis=1)
+
+
 def front_kernel(
-    n, ns, hidden, cotangent, tail, gain, proj_input, proj_gate, proj_output, piece,
+    n, ns, hidden, cotangent, tail, vec, proj_input, proj_gate, proj_output, piece,
     normed_o, inv_o, pre_o, gate_o, gyn_o, full_o, nhalo_o, halo_o,
-    full, halo, s_sem, r_sem, h_sem,
+    full, halo, s_sem, r_sem, w_sem, v_sem, h_sem,
 ):
     c = pl.program_id(0)
     me, seq = lax.axis_index("head"), lax.axis_index("seq")
     height = piece.shape[0]
+    short = height // 2
+    odd = seq % 2
+    last = pl.num_programs(0) - 1
 
     def slab(j):
         return pl.ds(pl.multiple_of(j * height, height), height)
+
+    def part(j, which):
+        return pl.ds(pl.multiple_of(j * height + which * short, short), short)
 
     def give(k, arriving):
         other = (me + k) % n
         owner = other if arriving else me
         return pltpu.make_async_remote_copy(
-            src_ref=piece,
-            dst_ref=full.at[slab(owner)],
+            src_ref=piece.at[pl.ds(pl.multiple_of(odd * short, short), short)],
+            dst_ref=full.at[part(owner, odd)],
             send_sem=s_sem.at[k],
             recv_sem=r_sem.at[owner],
             device_id={"head": other},
+            device_id_type=MESH_ID,
+        )
+
+    def swap(k, arriving):
+        owner = (me + k) % n
+        where = part(owner, 1 - odd if arriving else odd)
+        return pltpu.make_async_remote_copy(
+            src_ref=full.at[where],
+            dst_ref=full.at[where],
+            send_sem=w_sem.at[k],
+            recv_sem=v_sem.at[k],
+            device_id={"seq": seq + 1 - 2 * odd},
             device_id_type=MESH_ID,
         )
 
@@ -158,29 +180,43 @@
     def norm(value):
         value = value.astype(F32)
         inv = lax.rsqrt(jnp.mean(value * value, axis=-1, keepdims=True) + EPS)
-        return inv, (value * inv * gain[...]).astype(BF16)
+        return inv, (value * inv * gain).astype(BF16)
+
+    first = 3 + (2 * pre_o.shape[1] + piece.shape[1]) // LANES
+    gain = line(vec, first, hidden.shape[1])
+    barrier = pltpu.get_barrier_semaphore()
 
     @pl.when(c == 0)
     def _():
-        barrier = greet(n, ns)
-        pl.semaphore_wait(barrier, n + ns - 2)
-        for k in range(1, n):
-            give(k, False).start()
-
-        @pl.when(seq < ns - 1)
-        def _():
-            edge().start()
-
-        full[slab(me), :] = piece[...]
+        greet(n, ns)
 
     inv, normed = norm(hidden[...])
     inv_o[...] = inv
     normed_o[...] = normed
     pre_o[...] = dg(normed, proj_input[...], NN)
+
+    @pl.when(c == 0)
+    def _():
+        pl.semaphore_wait(barrier, n + ns - 2)
+        for k in range(1, n):
+            give(k, False).start()
+
+        @pl.when(seq < ns - 1)
+        def _():
+            edge().start()
+
+        full[slab(me), :] = piece[...]
+
     gate_o[...] = dg(normed, proj_gate[...], NN)
     gyn_o[...] = dg(cotangent[...], proj_output[...], NT)
 
-    @pl.when(c == pl.num_programs(0) - 1)
+    @pl.when(c == jnp.maximum(last - 1, 0))
+    def _():
+        for k in range(1, n):
+            give(k, True).wait_recv()
+            swap(k, False).start()
+
+    @pl.when(c == last)
     def _():
         @pl.when(seq > 0)
         def _():
@@ -199,9 +235,10 @@
             edge().wait_send()
 
         for k in range(1, n):
-            give(k, True).wait_recv()
+            swap(k, True).wait_recv()
         full_o[...] = full[...]
         for k in range(1, n):
+            swap(k, False).wait_send()
             give(k, False).wait_send()
 
 
@@ -217,9 +254,6 @@
     two = 2 * state_size
     hot = onehot[...]
 
-    def line(first, size):
-        return jnp.concatenate([vec[r : r + 1, :] for r in range(first, first + size // LANES)], axis=1)
-
     height = pre.shape[0]
 
     @pl.when(c == 0)
@@ -229,13 +263,13 @@
         params[...] = jnp.zeros_like(params)
         per = inner // LANES
         params[0:TAPS, :] = taps_in[...].astype(F32)
-        params[4:5, :] = line(3, inner)
-        params[5:6, :] = line(3 + per, inner)
+        params[4:5, :] = line(vec, 3, inner)
+        params[5:6, :] = line(vec, 3 + per, inner)
         params[6:7, :] = spread(jnp.broadcast_to(vec[2:3, :], (HALO, LANES)), hot)[:1]
         params[7:8, :LANES] = -jnp.exp(vec[0:1, :])
         params[7:8, LANES : 2 * LANES] = vec[1:2, :]
         params[8 : 8 + TAPS, :two] = taps_st[...].astype(F32)
-        params[12:13, :two] = line(3 + 2 * per, two)
+        params[12:13, :two] = line(vec, 3 + 2 * per, two)
         shalo_o[...] = dg(normed_halo[...], full[...], NN)[16 - HALO :, :]
         sext[height:, :] = shalo_o[...]
         ext[:HALO, :] = pre_halo[...]
@@ -247,7 +281,7 @@
     sext[:HALO, :] = sext[height:, :]
     spre = dg(normed[...], full[...], NN)
     spre_o[...] = spre
-    step_pre = dg(normed[...], step_w[...], NN)
+    step_pre = dg(normed[...], step_w[...], NT)
     spre_step_o[...] = step_pre
     act = conv_act(pre[...], ext, params, 0)
     sact = conv_act(spre, sext, params, 8)
@@ -754,22 +788,37 @@
     )(*lefts, *rights, *sums)
 
 
-def turn_kernel(value, out):
-    high = value.shape[0]
-    more = jnp.zeros((-high % LANES, value.shape[1]), F32)
-    out[...] = jnp.concatenate([value[...], more], axis=0).T[:, :high]
-
-
-def finish_kernel(branch, code, hidden, cotangent, inv, gain, result, out):
+def transposed(value):
+    high, wide = value.shape
+    value = jnp.concatenate([value, jnp.zeros((-high % LANES, wide), F32)], axis=0)
+    return value.T[:, :high]
+
+
+def finish_kernel(
+    branch, code, hidden, cotangent, inv, vec, sum_a, sum_b, sum_s, out_grad, in_grad,
+    result, out, grad_out, grad_in, grad_step, grad_states, taps_in, taps_st,
+):
     width = out.shape[1]
+    inner = grad_in.shape[1]
+    heads = grad_step.shape[0]
+    gain = line(vec, 3 + (2 * inner + taps_st.shape[1]) // LANES, width)
     resid = hidden[...].astype(F32)
     result[...] = resid + decode(branch[...], width)
-    grad = decode(code[...], width) * gain[...]
+    grad = decode(code[...], width) * gain
     scale = inv[...]
     dots = jnp.sum(grad * resid, axis=1, keepdims=True) * (1.0 / width)
     out[...] = (
         cotangent[...].astype(F32) + scale * grad - resid * (scale * scale * scale * dots)
     )
+
+    @pl.when(pl.program_id(0) == 0)
+    def _():
+        grad_out[...] = out_grad[...]
+        grad_in[...] = in_grad[:, :inner]
+        grad_step[...] = transposed(in_grad[:, inner:])[:heads]
+        grad_states[...] = sum_s[...]
+        taps_in[...] = sum_a[:TAPS, :]
+        taps_st[...] = sum_b[8 : 8 + TAPS, : taps_st.shape[1]]
 
 
 def rows_of_sums(square, cross):
@@ -891,9 +940,9 @@
 
 def back_kernel(
     n, ns, act, sact, y, gssd, step, step_pre, cum, cumt, sin, dout, before_log, total_log, incoming,
-    ynorm, proj_output, packed, normed,
+    ynorm, proj_output, packed, normed, cotangent,
     params, onehot, rows_in, pre, pre_prev, pre_halo, spre, spre_prev, spre_halo,
-    gin_o, gsb_out, small_a, small_b, code_out, win_o,
+    gin_o, gsb_out, small_a, small_b, code_out, win_o, wout_o,
     gin_all, gsb_o, gstep, xs_ref, u_ref, st_ref, gext, sext, pext, spext, halo_send, halo_got, shalo_send, shalo_got,
     psum, psend, pgot, h_sem, p_send, p_recv, g_send, g_recv,
     later, got_states, got_decays, prefix, swap_sems, all_ref, part, *chain_refs,
@@ -982,12 +1031,27 @@
             slot(t)
             compute(t + 1)
 
+        def product(m):
+            cols = pl.ds(pl.multiple_of(m * 256, 256), 256)
+            wout_o[cols, :] = dg(cotangent[:, cols], ynorm[...], TN)
+
+        tiles = wout_o.shape[0] // 256
+
         @pl.loop(3, STREAMS)
         def _(h):
             compute(h)
 
+        @pl.loop(0, tiles // 2)
+        def _(m):
+            product(m)
+
         turn()
         slot(2)
+
+        @pl.loop(tiles // 2, tiles)
+        def _(m):
+            product(m)
+
         end()
 
     @pl.when((c >= 0) & (c < count))
@@ -1143,8 +1207,20 @@
         gstep[:Q, :] = gstep[Q:, :]
         sext[:Q, :] = sext[Q + HALO :, :]
 
-    @pl.when(c == count)
-    def _():
+    last_step = count + 1
+    tail_slot = slots_of(n) - 3
+    more = tail_slot - 3
+
+    @pl.when((i >= 1) & (i < last_step))
+    def _():
+        @pl.loop(3 + (i - 1) * more // count, 3 + i * more // count)
+        def _(t):
+            slot(t)
+
+    @pl.when(i == last_step)
+    def _():
+        slot(tail_slot)
+
         @pl.loop(0, win_o.shape[0] // 256)
         def _(m):
             cols = pl.ds(pl.multiple_of(m * 256, 256), 256)
@@ -1166,8 +1242,10 @@
             for k in range(1, n):
                 give(k, g, False).start()
 
-    @pl.when(c == count)
-    def _():
+    @pl.when(i == last_step)
+    def _():
+        slot(tail_slot + 1)
+        slot(tail_slot + 2)
         for g in range(groups):
             for k in range(1, n):
                 give(k, g, True).wait_recv()
@@ -1180,15 +1258,6 @@
             @pl.when(k % n != me)
             def _():
                 to_owner(k).wait_send()
-
-    last_step = count + 1
-    more = slots_of(n) - 3
-
-    @pl.when(i >= 1)
-    def _():
-        @pl.loop(3 + (i - 1) * more // last_step, 3 + i * more // last_step)
-        def _(t):
-            slot(t)
 
     @pl.when(i == last_step)
     def _():
@@ -1227,13 +1296,29 @@
     head_dim = inner // heads
     row_width = proj_states.shape[0]
     count = tokens // Q
-    gain_full = in_gain.astype(F32)
 
     def pad_heads(value):
         return jnp.pad(value, [(0, 0)] * (value.ndim - 1) + [(0, LANES - heads)])
 
     n, ns = lax.axis_size("head"), seg_count
 
+    two = 2 * state_size
+    fields = [
+        (decay_log, LANES),
+        (step_bias, LANES),
+        (skip_gain, LANES),
+        (conv_input_bias, inner),
+        (gate_gain, inner),
+        (conv_states_bias, two),
+        (in_gain, width),
+    ]
+    used = sum(size for _, size in fields)
+    used += -used % 1024
+    flat, place = jnp.zeros((used,), F32), 0
+    for value, size in fields:
+        flat = flat + jnp.pad(value.astype(F32), (place, used - place - value.shape[0]))
+        place += size
+    vec = flat.reshape(-1, LANES)
     stripe = 256
 
     def striped(size):
@@ -1251,7 +1336,7 @@
             (hidden, striped(width)),
             (cotangent, striped(width)),
             (hidden, fixed((16, width), tokens // 16 - 1)),
-            (gain_full[None, :], fixed((1, width))),
+            (vec, fixed(vec.shape)),
             (proj_input, fixed((width, inner))),
             (proj_gate, fixed((width, inner))),
             (proj_output, fixed((inner, width))),
@@ -1272,25 +1357,14 @@
             pltpu.VMEM((16, width), BF16),
             pltpu.SemaphoreType.DMA((n,)),
             pltpu.SemaphoreType.DMA((n,)),
+            pltpu.SemaphoreType.DMA((n,)),
+            pltpu.SemaphoreType.DMA((n,)),
             pltpu.SemaphoreType.DMA((2,)),
         ],
         flops=6 * tokens * inner * width,
         collective=6,
     )
-    proj_step_wide = pad_heads(proj_step)
-    two = 2 * state_size
-    flat = jnp.concatenate(
-        [
-            pad_heads(decay_log),
-            pad_heads(step_bias),
-            pad_heads(skip_gain),
-            conv_input_bias.astype(F32),
-            gate_gain.astype(F32),
-            conv_states_bias.astype(F32),
-        ]
-    )
-    flat = jnp.pad(flat, (0, -flat.shape[0] % 1024))
-    vec = flat.reshape(-1, LANES)
+    proj_step_tall = pad_heads(proj_step).T
     onehot = jnp.asarray(
         np.arange(LANES)[:, None] == np.arange(inner)[None, :] // head_dim, dtype=BF16
     )
@@ -1311,7 +1385,7 @@
             (input_halo, whole((HALO, inner))),
             (normed, rows(width, big)),
             (normed_halo, whole((16, width))),
-            (proj_step_wide, whole((width, LANES))),
+            (proj_step_tall, whole((LANES, width))),
             (vec, whole(vec.shape)),
             (conv_input, whole(conv_input.shape)),
             (conv_states, whole(conv_states.shape)),
@@ -1416,14 +1490,7 @@
         flops=12 * tokens * inner * state_size,
         collective=3,
     )
-    local_proj_output = transposed_times(cotangent, ynorm)
     local_proj_gate = transposed_times(normed, grad_gate_pre)
-    summed_out = lax.psum_scatter(
-        local_proj_output, "seq", scatter_dimension=0, tiled=True
-    )
-    grad_proj_output = pl.pallas_call(
-        turn_kernel, out_shape=sds(summed_out.shape[::-1]), name="turn"
-    )(summed_out)
     grad_proj_gate = lax.psum_scatter(
         local_proj_gate, "seq", scatter_dimension=0, tiled=True
     )
@@ -1450,7 +1517,7 @@
 
     dma = pltpu.SemaphoreType.DMA
     groups = count // n
-    grad_in_b, grad_states_b, small_a, small_b, branch_code, local_proj_in = call(
+    grad_in_b, grad_states_b, small_a, small_b, branch_code, local_proj_in, local_proj_output = call(
         functools.partial(back_kernel, n, ns),
         (count + 2,),
         [
@@ -1474,6 +1541,7 @@
             (proj_output, once((inner, width))),
             (packed_back, once(packed_shape)),
             (normed, once((tokens, width))),
+            (cotangent, once((tokens, width))),
             par,
             hot,
             (grad_rows, whole((HALO, inner))),
@@ -1491,6 +1559,7 @@
             (sds((HALO, two)), whole((HALO, two))),
             (sds((tokens, width + LANES), BF16), once((tokens, width + LANES))),
             (sds((width, inner + LANES)), once((width, inner + LANES))),
+            (sds((width, inner)), once((width, inner))),
         ],
         scratch=[
             pltpu.VMEM((tokens, inner + LANES), BF16),
@@ -1529,20 +1598,33 @@
     )
     normed_rows = lax.dynamic_slice_in_dim(normed, row_start, row_width, 1)
     local_proj_states = transposed_times(grad_states_b, normed_rows)
+    summed_out = lax.psum_scatter(
+        local_proj_output, "seq", scatter_dimension=0, tiled=True
+    )
     summed_in = lax.psum_scatter(local_proj_in, "seq", scatter_dimension=0, tiled=True)
-    grad_code, sum_a, sum_b, grad_proj_states = reduce_over_heads(
+    grad_code, sum_a, sum_b, sum_s = reduce_over_heads(
         [
             (grad_gate_pre, proj_gate),
             (grad_in_b, proj_input),
-            (grad_in_b, proj_step_wide),
+            (grad_in_b, proj_step_tall),
             (grad_states_b, own_states),
         ],
-        [NT] * 4,
+        [NT, NT, NN, NT],
         (None, (0, inner), (inner, inner + LANES), None),
         2,
         (hidden, inv_rms, small_a, small_b, local_proj_states),
     )
-    result, grad_hidden = call(
+
+    def ones(value):
+        return (value, fixed(value.shape))
+
+    def outs(*shape):
+        return (sds(shape), fixed(shape))
+
+    (
+        result, grad_hidden, grad_proj_output, grad_proj_input, grad_proj_step, grad_proj_states,
+        grad_conv_input, grad_conv_states,
+    ) = call(
         finish_kernel,
         (tokens // stripe,),
         [
@@ -1551,9 +1633,23 @@
             (hidden, striped(width)),
             (cotangent, striped(width)),
             (inv_rms, striped(1)),
-            (gain_full[None, :], fixed((1, width))),
+            ones(vec),
+            ones(sum_a),
+            ones(sum_b),
+            ones(sum_s),
+            ones(summed_out),
+            ones(summed_in),
         ],
-        [(sds((tokens, width)), striped(width)), (sds((tokens, width)), striped(width))],
+        [
+            (sds((tokens, width)), striped(width)),
+            (sds((tokens, width)), striped(width)),
+            outs(width // ns, inner),
+            outs(width // ns, inner),
+            outs(heads, width // ns),
+            outs(two // ns, row_width),
+            outs(TAPS, inner),
+            outs(TAPS, two),
+        ],
         flops=40 * tokens * width,
     )
     return (
@@ -1561,18 +1657,18 @@
         grad_hidden,
         sum_b[0],
         grad_proj_gate,
-        summed_in[:, :inner],
+        grad_proj_input,
         grad_proj_states.T,
-        summed_in[:, inner : inner + heads],
-        sum_a[:TAPS],
+        grad_proj_step.T,
+        grad_conv_input,
         sum_a[4],
-        sum_b[8 : 8 + TAPS, :two],
+        grad_conv_states,
         sum_b[12, :two],
         sum_a[7, LANES : LANES + heads],
         sum_a[7, :heads],
         jnp.sum(sum_a[6].reshape(heads, head_dim), axis=1),
         sum_a[5],
-        grad_proj_output,
+        grad_proj_output.T,
     )
 
 

time: 388 us -> 405 us (1.044)
  waiting for transfers between devices: 0.05 us -> 40.6 us
  local copies, waits for them, and re-layouts: 22.7 us -> 9.03 us
  matrix products: 14.1 us -> 8.36 us
    reduce_scatter x1, waiting for transfers between devices: 0.01 us -> 39.8 us  [on_device(): lax.psum_scatter(local_proj_gate, 'seq', scatter_dimension=0, tiled=True)]
    unnamed x17 -> x6, local copies, waits for them, and re-layouts: 9.07 us -> 1.95 us
    dot_general x3 -> x2, matrix products: 14.1 us -> 8.36 us  [dg(): return lax.dot_general(left, right, dims, preferred_element_type=F32)]
    slice x4 -> x0, local copies, waits for them, and re-layouts: 5.45 us -> none  [the longest x1 1.92 us: on_device(): summed_in[:, :inner]]
  transfers between devices with their start and end apart: 3 -> 3, of which waited for: 0 -> 1; matrix products, arithmetic and copies ran while one was open for 6% -> 4% of each run, Pallas kernels for 64% -> 30%
where the time goes in v4:
time: 405 us
  Pallas kernels  331 us (82%)
  waiting for transfers between devices  40.6 us (10%)
  between operations  13.9 us (3%)
  local copies, waits for them, and re-layouts  9.03 us (2%)
  matrix products  8.36 us (2%)
    pallas_call x6, Pallas kernels, call(): pl.pallas_call(kernel, grid=grid, in_specs=in_specs, out_specs=[spec for...  224 us
    pallas_call x1, Pallas kernels, reduce_over_heads(): pl.pallas_call(functools.partial(reduce_kernel, n, ns, dims, cols), in_sp...  107 us
    reduce_scatter x1, waiting for transfers between devices, on_device(): lax.psum_scatter(local_proj_gate, 'seq', scatter_dimension=0, tiled=True)  39.8 us
    dot_general x2, matrix products, dg(): return lax.dot_general(left, right, dims, preferred_element_type=F32)  8.36 us
  transfers between devices with their start and end apart: 3, of which 1 were waited for; matrix products, arithmetic and copies ran while one was open for 4% of the time, Pallas kernels for 30%

profile of v4, /device:TPU:0, one launch (start us, length us, event | category | flops | bytes accessed | tf_op | source)
XLA Modules:
  0.0 404.5 jit_solution(12137817613405159797)
XLA Ops:
  7.2 0.0 reduce-scatter.4.cloned.1.call-start
  7.2 1.6 pad_bitcast_fusion.step_w.refs_6_
  8.8 1.4 add_bitcast_fusion.vec
  10.2 23.3 %shard_map.288 = (bf16[1024,1536]{1,0:T(8,128)(2,1)}, f32[1024,1]{1,0:T(8,128)}, f32[1024,768]{1,0:T(8,128)}, f32[1024,768]{1,0:T(8,128)}, f32[1024,768]{1,0:T(8...) custom-call(bf16[1024,1536]{1,0:T(8,128)(2,1)} %hidden.3, ...), custom_call_target="tpu_custom_call" | custom-call | flops 7247757312 | bytes 30175232 | tf_op jit(solution)/shard_map/pallas_call | solution.py:66
  33.5 12.7 %shard_map.289 = (f32[1024,768]{1,0:T(8,128)}, f32[1024,256]{1,0:T(8,128)}, f32[1024,256]{1,0:T(8,128)}, f32[8,256]{1,0:T(8,128)}, f32[1024,128]{1,0:T(8,128)}, ...) custom-call(f32[1024,768]{1,0:T(8,128)} %get-tuple-element.65.pre.pr, ...), custom_call_target="tpu_custom_call" | custom-call | flops 1006632960 | bytes 21856256 | tf_op jit(solution)/shard_map/pallas_call | solution.py:66
  46.3 17.0 %shard_map.290 = (f32[1024,768]{1,0:T(8,128)}, f32[128,768]{1,0:T(8,128)}) custom-call(f32[1024,768]{1,0:T(8,128)} %get-tuple-element.70.act, f32[1024,256]{1,0:T(8,128)} %get-tuple-element.71.sact, f32[1024,128]{1,0:T(8,128)} %get-tuple-element.72.step, f32[1024,128]{1,0:T(8,128)} %get-tuple-element.73.cum, f32[1024,128]{1,0:T(8,128)} %get-tuple-element.74.cumt, ...), custom_call_target="tpu_custom_call" | custom-call | flops 1207959552 | bytes 9949184 | tf_op jit(solution)/shard_map/pallas_call | solution.py:66
  63.3 25.5 %shard_map.291 = (f32[1024,768]{1,0:T(8,128)}, bf16[1024,768]{1,0:T(8,128)(2,1)}, bf16[1024,768]{1,0:T(8,128)(2,1)}, f32[1024,768]{1,0:T(8,128)}, f32[1024,768]{...) custom-call(f32[1024,768]{1,0:T(8,128)} %get-tuple-element.78.yloc, f32[1024,768]{1,0:T(8,128)} %get-tuple-element.70.act, ...), custom_call_target="tpu_custom_call" | custom-call | flops 1207959552 | bytes 30945280 | tf_op jit(solution)/shard_map/pallas_call | solution.py:66
  88.8 132.4 %shard_map.292 = (bf16[1024,896]{1,0:T(8,128)(2,1)}, bf16[1024,256]{1,0:T(8,128)(2,1)}, f32[16,768]{1,0:T(8,128)}, f32[8,256]{1,0:T(8,128)}, bf16[1024,1664]{1,0...) custom-call(f32[1024,768]{1,0:T(8,128)} %get-tuple-element.70.act, f32[1024,256]{1,0:T(8,128)} %get-tuple-element.71.sact, ...), custom_call_target="tpu_custom_call" | custom-call | flops 4026531840 | bytes 54632448 | tf_op jit(solution)/shard_map/pallas_call | solution.py:66
  221.2 0.0 reduce-scatter.4.cloned.1.call-update
  221.2 0.0 copy-start
  221.2 0.0 reduce-scatter.6.cloned.1.call-start
  221.3 0.7 reduce-scatter.6.cloned.1.call-update
  222.0 0.0 reduce-scatter.8.cloned.1.call-start
  222.0 1.1 copy-done
  223.1 5.7 %fusion.3 = f32[1536,768]{1,0:T(8,128)} fusion(bf16[1024,1536]{1,0:T(8,128)(2,1)S(1)} %copy-done, bf16[1024,768]{1,0:T(8,128)(2,1)} %get-tuple-element.94.refs_0_), kind=kOutput, calls=%fused_computation.12 | convolution fusion | flops 2415919104 | bytes 9437184 | tf_op jit(solution)/shard_map/dot_general | solution.py:30
  228.8 0.0 copy-start.2
  228.8 0.0 reduce-scatter.8.cloned.1.call-update
  228.8 0.1 broadcast_in_dim.3
  228.9 0.9 copy-done.2
  229.8 0.0 copy-start.1
  229.8 2.6 fusion.refs_12_
  232.4 0.0 copy-done.1
  232.4 106.6 %reduce_heads.1 = (bf16[1024,1664]{1,0:T(8,128)(2,1)}, f32[16,768]{1,0:T(8,128)}, f32[16,1536]{1,0:T(8,128)}, f32[32,384]{1,0:T(8,128)}) custom-call(bf16[1024,768]{1,0:T(8,128)(2,1)} %get-tuple-element.94.refs_0_, bf16[1024,896]{1,0:T(8,128)(2,1)} %get-tuple-element.95.refs_1_.refs_2_, bf16[1024,896]{1,0:T(8,128)(2,1)} %get-tuple-element.95.refs_1_.refs_2_, ...), custom_call_target="tpu_custom_call" | custom-call | flops 8858370048 | bytes 157286400 | tf_op jit(solution)/shard_map/reduce_heads/pallas_call | solution.py:773
  339.1 1.5 slice_reduce_fusion.1
  340.6 0.1 reshape_squeeze.3
  340.6 1.3 slice.23
  341.9 0.6 reduce_sum.9
  342.5 1.4 slice_reduce_fusion
  343.9 1.2 slice_bitcast_fusion
  345.1 0.0 reduce-scatter.4.cloned.1.call-done.out_grad
  345.1 0.0 reduce-scatter.6.cloned.1.call-done.in_grad
  345.1 13.0 %shard_map.293 = (f32[1024,1536]{1,0:T(8,128)}, f32[1024,1536]{1,0:T(8,128)}, f32[192,768]{1,0:T(8,128)}, f32[192,768]{1,0:T(8,128)}, f32[12,192]{1,0:T(8,128)},...) custom-call(bf16[1024,1664]{1,0:T(8,128)(2,1)} %get-tuple-element.93.branch, ...), custom_call_target="tpu_custom_call" | custom-call | flops 62914560 | bytes 28439552 | tf_op jit(solution)/shard_map/pallas_call | solution.py:66
  358.1 39.8 %reduce-scatter.8.cloned.1.call-done = f32[192,768]{1,0:T(8,128)} async-done(((f32[1536,768]{1,0:T(8,128)}), f32[192,768]{1,0:T(8,128)}) %reduce-scatter.8.cloned.1.call-update) | async-done | bytes 589840 | tf_op jit(solution)/shard_map/reduce_scatter | solution.py:1494
  (1 shorter events, 0.0 us)
Async XLA Ops:
  7.2 338.0 %reduce-scatter.4.cloned.1.call-start = ((), (), s32[]{:S(2)}) async-start(), calls=%async_computation.3 | async-start | bytes 5308416 | tf_op jit(solution)/shard_map/reduce_scatter | solution.py:1601
  221.2 1.9 copy-start
  221.2 123.9 %reduce-scatter.6.cloned.1.call-start = ((), (), s32[]{:S(2)}) async-start(), calls=%async_computation.4 | async-start | bytes 6193152 | tf_op jit(solution)/shard_map/reduce_scatter | solution.py:1604
  222.0 176.0 %reduce-scatter.8.cloned.1.call-start = ((), (), s32[]{:S(2)}) async-start(), calls=%async_computation.5 | async-start | bytes 5308416 | tf_op jit(solution)/shard_map/reduce_scatter | solution.py:1494
  228.8 1.0 copy-start.2
  229.8 2.6 copy-start.1
Sparse Core Ops, SparseCore 0:
  221.3 57.5 reduce-scatter.3
  282.4 57.7 reduce-scatter.5
  344.2 53.7 reduce-scatter.7

commit v5 on v4

--- a/solution.py
+++ b/solution.py
@@ -322,35 +322,17 @@
     )
 
 
-def intra_kernel(
-    ns, act, sact, step, cum, cumt, params, onehot, packed, logs, out, incoming,
-    xs_ref, entered, got_s, got_d, prefix, sems,
-):
-    c = pl.program_id(0)
-    count = pl.num_programs(0)
-    seq = lax.axis_index("seq")
-    begin, turn, end = swap_states(
-        ns, packed, logs, onehot, entered, got_s, got_d, prefix, sems, False
-    )
-    barrier = pltpu.get_barrier_semaphore()
-
-    @pl.when(c == 0)
-    def _():
-        for k in range(1, ns):
-            pl.semaphore_signal(
-                barrier, inc=1, device_id={"seq": (seq + k) % ns}, device_id_type=MESH_ID
-            )
-        pl.semaphore_wait(barrier, ns - 1)
-        begin()
-
+def intra(base, act, sact, step, cum, cumt, params, onehot, out, xs_ref):
     state_size = bmat_width(sact)
     x = silu(act[...])
     xs_ref[...] = x * spread(step[...], onehot[...])
-    out[...] = x * params[6:7, :]
-
-    @pl.loop(0, act.shape[0] // Q)
+    height = act.shape[0]
+    out[pl.ds(pl.multiple_of(base, height), height), :] = x * params[6:7, :]
+
+    @pl.loop(0, height // Q)
     def _(chunk):
         here = pl.ds(pl.multiple_of(chunk * Q, Q), Q)
+        there = pl.ds(pl.multiple_of(base + chunk * Q, Q), Q)
         sconv = silu(sact[here, :])
         bmat, cmat = sconv[:, :state_size], sconv[:, state_size:]
         scores = dot3(cmat, bmat, NT)
@@ -367,19 +349,12 @@
                 mixing = scores * jnp.exp(jnp.where(causal, gap, -1e30))
                 wide = dg(jnp.concatenate(split(mixing), axis=1), right, NN)
                 got.append(wide[:, :LANES] + wide[:, LANES:])
-            out[here, cols] = out[here, cols] + jnp.where(lane < LANES // 2, got[0], got[1])
-
-    @pl.when(c == count // 2)
-    def _():
-        turn()
-
-    @pl.when(c == count - 1)
-    def _():
-        end()
-        incoming[...] = entered[...]
+            out[there, cols] = out[there, cols] + jnp.where(lane < LANES // 2, got[0], got[1])
 
 
 STREAMS = 8
+OPENING = 4
+CLOSING = 0
 SPAN = 83.0
 
 
@@ -795,12 +770,11 @@
 
 
 def finish_kernel(
-    branch, code, hidden, cotangent, inv, vec, sum_a, sum_b, sum_s, out_grad, in_grad,
-    result, out, grad_out, grad_in, grad_step, grad_states, taps_in, taps_st,
+    branch, code, hidden, cotangent, inv, vec, sum_a, sum_b, sum_s, out_grad,
+    result, out, grad_out, grad_states, taps_in, taps_st,
 ):
     width = out.shape[1]
-    inner = grad_in.shape[1]
-    heads = grad_step.shape[0]
+    inner = taps_in.shape[1]
     gain = line(vec, 3 + (2 * inner + taps_st.shape[1]) // LANES, width)
     resid = hidden[...].astype(F32)
     result[...] = resid + decode(branch[...], width)
@@ -814,11 +788,15 @@
     @pl.when(pl.program_id(0) == 0)
     def _():
         grad_out[...] = out_grad[...]
-        grad_in[...] = in_grad[:, :inner]
-        grad_step[...] = transposed(in_grad[:, inner:])[:heads]
         grad_states[...] = sum_s[...]
         taps_in[...] = sum_a[:TAPS, :]
         taps_st[...] = sum_b[8 : 8 + TAPS, : taps_st.shape[1]]
+
+
+def part_kernel(in_grad, grad_in, grad_step):
+    inner = grad_in.shape[1]
+    grad_in[...] = in_grad[:, :inner]
+    grad_step[...] = transposed(in_grad[:, inner:])[: grad_step.shape[0]]
 
 
 def rows_of_sums(square, cross):
@@ -831,20 +809,21 @@
 
 
 def middle_kernel(
-    n, yloc, act, sact, cum, sin, before_log, incoming, gate, gyn, params, onehot,
-    y_o, ynorm_o, gpre_o, gssd_o, dout_o, dev_o, rows_o,
-    keep, mine, got, adj, ssem, rsem,
+    n, ns, act, sact, step, cum, cumt, sin, before_log, gate, gyn, params, onehot, packed, logs,
+    y_o, ynorm_o, gpre_o, gssd_o, dout_o, dev_o, rows_o, incoming_o,
+    keep, mine, got, adj, xs_ref, incoming, got_s, got_d, prefix, swap_sems, ssem, rsem,
 ):
     i = pl.program_id(0)
-    count = pl.num_programs(0) // 2
-    c = jnp.where(i < count, i, 2 * count - 1 - i)
+    half = pl.num_programs(0) // 3
+    c = jnp.where(i < half, i, jnp.where(i < 2 * half, i - half, 3 * half - 1 - i))
     me = lax.axis_index("head")
     state_size = bmat_width(sact)
-    hot = onehot[...]
     gain = params[5:6, :]
     height = gate.shape[0]
     where = pl.ds(pl.multiple_of(c * height, height), height)
-    barrier = pltpu.get_barrier_semaphore()
+    begin, turn, end = swap_states(
+        ns, packed, logs, onehot, incoming, got_s, got_d, prefix, swap_sems, False
+    )
 
     def copy(k, arriving):
         other = (me + k) % n
@@ -859,38 +838,46 @@
 
     @pl.when(i == 0)
     def _():
-        for k in range(1, n):
-            pl.semaphore_signal(
-                barrier, inc=1, device_id={"head": (me + k) % n}, device_id_type=MESH_ID
-            )
-
-    cmat = silu(sact[:, state_size:])
-    gv = gate[...]
-    sg = sigmoid(gv)
-    gsilu = gv * sg
-    growth = spread(jnp.exp(cum[...]), hot)
-
-    @pl.when(i < count)
-    def _():
+        barrier = greet(n, ns)
+        pl.semaphore_wait(barrier, n + ns - 2)
+        begin()
+
+    @pl.when(i < half)
+    def _():
+        intra(c * height, act, sact, step, cum, cumt, params, onehot, keep, xs_ref)
+
+    @pl.when(i == half // 2)
+    def _():
+        turn()
+
+    @pl.when(i == half - 1)
+    def _():
+        end()
+        incoming_o[...] = incoming[...]
+
+    @pl.when((i >= half) & (i < 2 * half))
+    def _():
+        hot = onehot[...]
+        cmat = silu(sact[:, state_size:])
+        growth = spread(jnp.exp(cum[...]), hot)
         ahead = []
         for j in range(height // Q):
             part = slice(j * Q, (j + 1) * Q)
             carry = spread(jnp.broadcast_to(jnp.exp(before_log[j]), (HALO, LANES)), hot)[:1]
             state = sin[j * state_size : (j + 1) * state_size, :] + carry * incoming[...]
             ahead.append(dot3(cmat[part], state, NN))
-        y = yloc[...] + growth * jnp.concatenate(ahead, axis=0)
+        y = keep[where, :] + growth * jnp.concatenate(ahead, axis=0)
         y_o[...] = y
         keep[where, :] = y
-        gated = y * gsilu
+        gated = y * silu(gate[...])
         mine[:, where] = rows_of_sums(gated * gated, gyn[...] * gain * gated)
 
-    @pl.when(i == count - 1)
-    def _():
-        pl.semaphore_wait(barrier, n - 1)
+    @pl.when(i == 2 * half - 1)
+    def _():
         for k in range(1, n):
             copy(k, False).start()
 
-    @pl.when(i == count)
+    @pl.when(i == 2 * half)
     def _():
         adj[...] = jnp.zeros_like(adj)
         rows_o[...] = jnp.zeros_like(rows_o)
@@ -902,8 +889,14 @@
             total = total + got[(me + k) % n]
         mine[...] = total
 
-    @pl.when(i >= count)
-    def _():
+    @pl.when(i >= 2 * half)
+    def _():
+        hot = onehot[...]
+        cmat = silu(sact[:, state_size:])
+        gv = gate[...]
+        sg = sigmoid(gv)
+        gsilu = gv * sg
+        growth = spread(jnp.exp(cum[...]), hot)
         total = mine[:, where]
         blank = jnp.zeros((Q - HALO, Q), F32)
         columns = jnp.concatenate(
@@ -933,20 +926,26 @@
             decay = spread(jnp.broadcast_to(jnp.exp(last), (HALO, LANES)), hot)[:1]
             adj[...] = adj[...] * decay + dot3(cmat[part], scaled[part], TN)
 
-    @pl.when(i == 2 * count - 1)
+    @pl.when(i == 3 * half - 1)
     def _():
         dev_o[...] = adj[...]
 
 
 def back_kernel(
     n, ns, act, sact, y, gssd, step, step_pre, cum, cumt, sin, dout, before_log, total_log, incoming,
-    ynorm, proj_output, packed, normed, cotangent,
+    ynorm, proj_output, packed, normed_far, cotangent_far,
     params, onehot, rows_in, pre, pre_prev, pre_halo, spre, spre_prev, spre_halo,
-    gin_o, gsb_out, small_a, small_b, code_out, win_o, wout_o,
+    gin_o, gsb_out, small_a, small_b, code_far, win_far, wout_far,
     gin_all, gsb_o, gstep, xs_ref, u_ref, st_ref, gext, sext, pext, spext, halo_send, halo_got, shalo_send, shalo_got,
     psum, psend, pgot, h_sem, p_send, p_recv, g_send, g_recv,
-    later, got_states, got_decays, prefix, swap_sems, all_ref, part, *chain_refs,
+    later, got_states, got_decays, prefix, swap_sems, normed, cotangent, win_o, wout_o, c_sem,
+    all_ref, part, *chain_refs,
 ):
+    load_cotangent = pltpu.make_async_copy(cotangent_far, cotangent, c_sem.at[0])
+    load_normed = pltpu.make_async_copy(normed_far, normed, c_sem.at[1])
+    save_out = pltpu.make_async_copy(wout_o, wout_far, c_sem.at[2])
+    save_in = pltpu.make_async_copy(win_o, win_far, c_sem.at[3])
+    save_code = pltpu.make_async_copy(all_ref, code_far, c_sem.at[4])
     i = pl.program_id(0)
     c = i - 1
     count = pl.num_programs(0) - 2
@@ -1014,6 +1013,8 @@
     @pl.when(i == 0)
     def _():
         barrier = greet(n, ns)
+        load_cotangent.start()
+        load_normed.start()
         small_a[...] = jnp.zeros_like(small_a)
         small_b[...] = jnp.zeros_like(small_b)
         small_a[5:7, :] = rows_in[0:2, :]
@@ -1041,17 +1042,24 @@
         def _(h):
             compute(h)
 
+        load_cotangent.wait()
+
         @pl.loop(0, tiles // 2)
         def _(m):
             product(m)
 
         turn()
-        slot(2)
+
+        @pl.loop(2, OPENING - 1)
+        def _(t):
+            slot(t)
 
         @pl.loop(tiles // 2, tiles)
         def _(m):
             product(m)
 
+        save_out.start()
+        slot(OPENING - 1)
         end()
 
     @pl.when((c >= 0) & (c < count))
@@ -1208,23 +1216,29 @@
         sext[:Q, :] = sext[Q + HALO :, :]
 
     last_step = count + 1
-    tail_slot = slots_of(n) - 3
-    more = tail_slot - 3
+    tail_slot = slots_of(n) - CLOSING
+    more = tail_slot - OPENING
 
     @pl.when((i >= 1) & (i < last_step))
     def _():
-        @pl.loop(3 + (i - 1) * more // count, 3 + i * more // count)
+        @pl.loop(OPENING + (i - 1) * more // count, OPENING + i * more // count)
         def _(t):
             slot(t)
 
     @pl.when(i == last_step)
     def _():
-        slot(tail_slot)
+        @pl.loop(tail_slot, tail_slot + CLOSING // 2)
+        def _(t):
+            slot(t)
+
+        load_normed.wait()
 
         @pl.loop(0, win_o.shape[0] // 256)
         def _(m):
             cols = pl.ds(pl.multiple_of(m * 256, 256), 256)
             win_o[cols, :] = dg(normed[:, cols], gin_all[...], TN)
+
+        save_in.start()
 
     for g in range(groups):
 
@@ -1244,8 +1258,11 @@
 
     @pl.when(i == last_step)
     def _():
-        slot(tail_slot + 1)
-        slot(tail_slot + 2)
+        @pl.loop(tail_slot + CLOSING // 2, tail_slot + CLOSING)
+        def _(t):
+            slot(t)
+
+        save_code.start()
         for g in range(groups):
             for k in range(1, n):
                 give(k, g, True).wait_recv()
@@ -1262,7 +1279,9 @@
     @pl.when(i == last_step)
     def _():
         drain()
-        code_out[...] = all_ref[...]
+        save_code.wait()
+        save_out.wait()
+        save_in.wait()
 
 
 def transposed_times(left, right):
@@ -1416,78 +1435,69 @@
         flops=10 * tokens * inner * state_size,
     )
     par = (params, whole((16, inner)))
-    yloc, incoming = call(
-        functools.partial(intra_kernel, ns),
-        (count // GROUP,),
+    half = count // GROUP
+
+    def zero(i):
+        return jnp.minimum(i, half - 1)
+
+    def one(i):
+        return jnp.clip(i - half, 0, half - 1)
+
+    def two_(i):
+        return jnp.minimum(3 * half - 1 - i, half - 1)
+
+    def both(i):
+        return jnp.where(i < 2 * half, one(i), two_(i))
+
+    def ends(i):
+        return jnp.where(i < half, i, two_(i))
+
+    def every(i):
+        return jnp.where(i < half, i, both(i))
+
+    def at(size, which, height=big):
+        return pl.BlockSpec((height, size), lambda i: (which(i), 0))
+
+    y, ynorm, grad_gate_pre, grad_ssd, dout, packed_back, grad_rows, incoming = call(
+        functools.partial(middle_kernel, n, ns),
+        (3 * half,),
         [
-            (act, rows(inner, big)),
-            (sact, rows(two, big)),
-            (step, rows(LANES, big)),
-            (cum, rows(LANES, big)),
-            (cumt, rows(LANES, big)),
+            (act, at(inner, ends)),
+            (sact, at(two, every)),
+            (step, at(LANES, zero)),
+            (cum, at(LANES, every)),
+            (cumt, at(LANES, zero)),
+            (sin, at(inner, one, GROUP * state_size)),
+            (before_log, pl.BlockSpec((GROUP, 1, LANES), lambda i: (one(i), 0, 0))),
+            (gate_pre, at(inner, both)),
+            (grad_ynorm, at(inner, both)),
             par,
             hot,
             (packed, whole(packed_shape)),
             (total_log, whole(logs_shape)),
         ],
         [
-            (sds((tokens, inner)), rows(inner, big)),
-            (sds((state_size, inner)), whole((state_size, inner))),
-        ],
-        scratch=[pltpu.VMEM((big, inner), F32), pltpu.VMEM((state_size, inner), F32)]
-        + swap_scratch(ns, (state_size, inner)),
-        flops=12 * tokens * inner * Q,
-        collective=5,
-    )
-
-    half = count // GROUP
-
-    def both(i):
-        return jnp.where(i < half, i, 2 * half - 1 - i)
-
-    def fore(i):
-        return jnp.minimum(i, half - 1)
-
-    def aft(i):
-        return jnp.minimum(2 * half - 1 - i, half - 1)
-
-    def at(size, which, height=big):
-        return pl.BlockSpec((height, size), lambda i: (which(i), 0))
-
-    y, ynorm, grad_gate_pre, grad_ssd, dout, packed_back, grad_rows = call(
-        functools.partial(middle_kernel, n),
-        (2 * half,),
-        [
-            (yloc, at(inner, fore)),
-            (act, at(inner, aft)),
-            (sact, at(two, both)),
-            (cum, at(LANES, both)),
-            (sin, at(inner, fore, GROUP * state_size)),
-            (before_log, pl.BlockSpec((GROUP, 1, LANES), lambda i: (fore(i), 0, 0))),
-            (incoming, whole((state_size, inner))),
-            (gate_pre, at(inner, both)),
-            (grad_ynorm, at(inner, both)),
-            par,
-            hot,
-        ],
-        [
-            (sds((tokens, inner)), at(inner, fore)),
-            (sds((tokens, inner), BF16), at(inner, aft)),
-            (sds((tokens, inner), BF16), at(inner, aft)),
-            (sds((tokens, inner)), at(inner, aft)),
-            (sds((count * state_size, inner)), at(inner, aft, GROUP * state_size)),
+            (sds((tokens, inner)), at(inner, one)),
+            (sds((tokens, inner), BF16), at(inner, two_)),
+            (sds((tokens, inner), BF16), at(inner, two_)),
+            (sds((tokens, inner)), at(inner, two_)),
+            (sds((count * state_size, inner)), at(inner, two_, GROUP * state_size)),
             (sds(packed_shape), whole(packed_shape)),
             (sds((HALO, inner)), whole((HALO, inner))),
+            (sds((state_size, inner)), whole((state_size, inner))),
         ],
         scratch=[
             pltpu.VMEM((tokens, inner), F32),
             pltpu.VMEM((HALO, tokens), F32),
             pltpu.VMEM((n, HALO, tokens), F32),
             pltpu.VMEM((state_size, inner), F32),
+            pltpu.VMEM((big, inner), F32),
+            pltpu.VMEM((state_size, inner), F32),
+            *swap_scratch(ns, (state_size, inner)),
             pltpu.SemaphoreType.DMA((n,)),
             pltpu.SemaphoreType.DMA((n,)),
         ],
-        flops=12 * tokens * inner * state_size,
+        flops=24 * tokens * inner * state_size,
         collective=3,
     )
     local_proj_gate = transposed_times(normed, grad_gate_pre)
@@ -1511,6 +1521,8 @@
         return pl.BlockSpec(
             (HALO, size), lambda i: (jnp.maximum(past(i) * (Q // HALO) - 1, 0), 0)
         )
+
+    far = pl.BlockSpec(memory_space=pl.ANY)
 
     def once(shape):
         return pl.BlockSpec(shape, lambda i: (0, 0), pipeline_mode=pl.Buffered(1))
@@ -1540,8 +1552,8 @@
             (ynorm, once((tokens, inner))),
             (proj_output, once((inner, width))),
             (packed_back, once(packed_shape)),
-            (normed, once((tokens, width))),
-            (cotangent, once((tokens, width))),
+            (normed, far),
+            (cotangent, far),
             par,
             hot,
             (grad_rows, whole((HALO, inner))),
@@ -1557,9 +1569,9 @@
             (sds((tokens, two), BF16), whole((tokens, two))),
             (sds((16, inner)), whole((16, inner))),
             (sds((HALO, two)), whole((HALO, two))),
-            (sds((tokens, width + LANES), BF16), once((tokens, width + LANES))),
-            (sds((width, inner + LANES)), once((width, inner + LANES))),
-            (sds((width, inner)), once((width, inner))),
+            (sds((tokens, width + LANES), BF16), far),
+            (sds((width, inner + LANES)), far),
+            (sds((width, inner)), far),
         ],
         scratch=[
             pltpu.VMEM((tokens, inner + LANES), BF16),
@@ -1586,6 +1598,11 @@
             dma((n, groups)),
             pltpu.VMEM((state_size, inner), F32),
             *swap_scratch(ns, (state_size, inner)),
+            pltpu.VMEM((tokens, width), BF16),
+            pltpu.VMEM((tokens, width), BF16),
+            pltpu.VMEM((width, inner + LANES), F32),
+            pltpu.VMEM((width, inner), F32),
+            dma((5,)),
             pltpu.VMEM((tokens, width + LANES), BF16),
             *chain_scratch(tokens, width, n),
         ],
@@ -1622,8 +1639,7 @@
         return (sds(shape), fixed(shape))
 
     (
-        result, grad_hidden, grad_proj_output, grad_proj_input, grad_proj_step, grad_proj_states,
-        grad_conv_input, grad_conv_states,
+        result, grad_hidden, grad_proj_output, grad_proj_states, grad_conv_input, grad_conv_states,
     ) = call(
         finish_kernel,
         (tokens // stripe,),
@@ -1638,19 +1654,19 @@
             ones(sum_b),
             ones(sum_s),
             ones(summed_out),
-            ones(summed_in),
         ],
         [
             (sds((tokens, width)), striped(width)),
             (sds((tokens, width)), striped(width)),
             outs(width // ns, inner),
-            outs(width // ns, inner),
-            outs(heads, width // ns),
             outs(two // ns, row_width),
             outs(TAPS, inner),
             outs(TAPS, two),
         ],
         flops=40 * tokens * width,
+    )
+    grad_proj_input, grad_proj_step = call(
+        part_kernel, (1,), [ones(summed_in)], [outs(width // ns, inner), outs(heads, width // ns)]
     )
     return (
         result,

time: 405 us -> 396 us (0.978)
  Pallas kernels: 331 us -> 322 us
    pallas_call x6, Pallas kernels: 224 us -> 215 us  [call(): pl.pallas_call(kernel, grid=grid, in_specs=in_specs, out_specs=[spec for...]
  transfers between devices with their start and end apart: 3 -> 3, of which waited for: 1 -> 1; matrix products, arithmetic and copies ran while one was open for 4% -> 4% of each run, Pallas kernels for 30% -> 31%
where the time goes in v5:
time: 396 us; the launch traced here: 395 us
  Pallas kernels  322 us (81%)
  waiting for transfers between devices  39.7 us (10%)
  between operations  13.8 us (3%)
  local copies, waits for them, and re-layouts  9.01 us (2%)
  matrix products  8.42 us (2%)
    pallas_call x6, Pallas kernels, call(): pl.pallas_call(kernel, grid=grid, in_specs=in_specs, out_specs=[spec for...  215 us
    pallas_call x1, Pallas kernels, reduce_over_heads(): pl.pallas_call(functools.partial(reduce_kernel, n, ns, dims, cols), in_sp...  106 us
    reduce_scatter x1, waiting for transfers between devices, on_device(): lax.psum_scatter(local_proj_gate, 'seq', scatter_dimension=0, tiled=True)  38.9 us
    dot_general x2, matrix products, dg(): return lax.dot_general(left, right, dims, preferred_element_type=F32)  8.42 us
  transfers between devices with their start and end apart: 3, of which 1 were waited for; matrix products, arithmetic and copies ran while one was open for 4% of the time, Pallas kernels for 31%

profile of v5, /device:TPU:0, one launch (start us, length us, event | category | flops | bytes accessed | tf_op | source)
XLA Modules:
  0.0 394.8 jit_solution(17586622305155331087)
XLA Ops:
  7.2 0.0 reduce-scatter.4.cloned.1.call-start
  7.2 1.6 pad_bitcast_fusion.step_w.refs_6_
  8.8 1.4 add_bitcast_fusion.vec
  10.2 23.2 %shard_map.288 = (bf16[1024,1536]{1,0:T(8,128)(2,1)}, f32[1024,1]{1,0:T(8,128)}, f32[1024,768]{1,0:T(8,128)}, f32[1024,768]{1,0:T(8,128)}, f32[1024,768]{1,0:T(8...) custom-call(bf16[1024,1536]{1,0:T(8,128)(2,1)} %hidden.3, ...), custom_call_target="tpu_custom_call" | custom-call | flops 7247757312 | bytes 30175232 | tf_op jit(solution)/shard_map/pallas_call | solution.py:66
  33.4 12.7 %shard_map.289 = (f32[1024,768]{1,0:T(8,128)}, f32[1024,256]{1,0:T(8,128)}, f32[1024,256]{1,0:T(8,128)}, f32[8,256]{1,0:T(8,128)}, f32[1024,128]{1,0:T(8,128)}, ...) custom-call(f32[1024,768]{1,0:T(8,128)} %get-tuple-element.64.pre.pr, ...), custom_call_target="tpu_custom_call" | custom-call | flops 1006632960 | bytes 21856256 | tf_op jit(solution)/shard_map/pallas_call | solution.py:66
  46.2 38.3 %shard_map.290 = (f32[1024,768]{1,0:T(8,128)}, bf16[1024,768]{1,0:T(8,128)(2,1)}, bf16[1024,768]{1,0:T(8,128)(2,1)}, f32[1024,768]{1,0:T(8,128)}, f32[1024,768]{...) custom-call(f32[1024,768]{1,0:T(8,128)} %get-tuple-element.69.act, ...), custom_call_target="tpu_custom_call" | custom-call | flops 2415919104 | bytes 29245440 | tf_op jit(solution)/shard_map/pallas_call | solution.py:66
  84.5 126.4 %shard_map.291 = (bf16[1024,896]{1,0:T(8,128)(2,1)}, bf16[1024,256]{1,0:T(8,128)(2,1)}, f32[16,768]{1,0:T(8,128)}, f32[8,256]{1,0:T(8,128)}, bf16[1024,1664]{1,0...) custom-call(f32[1024,768]{1,0:T(8,128)} %get-tuple-element.69.act, f32[1024,256]{1,0:T(8,128)} %get-tuple-element.70.sact, ...), custom_call_target="tpu_custom_call" | custom-call | flops 4026531840 | bytes 54632448 | tf_op jit(solution)/shard_map/pallas_call | solution.py:66
  210.9 0.0 reduce-scatter.4.cloned.1.call-update
  210.9 0.0 copy-start
  210.9 0.0 reduce-scatter.8.cloned.1.call-start
  211.0 0.7 reduce-scatter.8.cloned.1.call-update
  211.7 0.0 reduce-scatter.6.cloned.1.call-start
  211.7 1.1 copy-done
  212.8 5.8 %fusion.3 = f32[1536,768]{1,0:T(8,128)} fusion(bf16[1024,1536]{1,0:T(8,128)(2,1)S(1)} %copy-done, bf16[1024,768]{1,0:T(8,128)(2,1)} %get-tuple-element.92.refs_0_), kind=kOutput, calls=%fused_computation.12 | convolution fusion | flops 2415919104 | bytes 9437184 | tf_op jit(solution)/shard_map/dot_general | solution.py:30
  218.6 0.0 copy-start.2
  218.6 0.0 reduce-scatter.6.cloned.1.call-update
  218.6 0.1 broadcast_in_dim.3
  218.7 0.9 copy-done.2
  219.6 0.0 copy-start.1
  219.6 2.6 fusion.refs_12_
  222.2 0.0 copy-done.1
  222.2 106.4 %reduce_heads.1 = (bf16[1024,1664]{1,0:T(8,128)(2,1)}, f32[16,768]{1,0:T(8,128)}, f32[16,1536]{1,0:T(8,128)}, f32[32,384]{1,0:T(8,128)}) custom-call(bf16[1024,768]{1,0:T(8,128)(2,1)} %get-tuple-element.92.refs_0_, bf16[1024,896]{1,0:T(8,128)(2,1)} %get-tuple-element.93.refs_1_.refs_2_, bf16[1024,896]{1,0:T(8,128)(2,1)} %get-tuple-element.93.refs_1_.refs_2_, ...), custom_call_target="tpu_custom_call" | custom-call | flops 8858370048 | bytes 157286400 | tf_op jit(solution)/shard_map/reduce_heads/pallas_call | solution.py:748
  328.6 1.5 slice_reduce_fusion.1
  330.1 0.1 reshape_squeeze.3
  330.2 1.3 slice.23
  331.5 0.6 reduce_sum.9
  332.1 1.4 slice_reduce_fusion
  333.5 1.2 slice_bitcast_fusion
  334.7 0.0 reduce-scatter.4.cloned.1.call-done.out_grad
  334.7 12.6 %shard_map.292 = (f32[1024,1536]{1,0:T(8,128)}, f32[1024,1536]{1,0:T(8,128)}, f32[192,768]{1,0:T(8,128)}, f32[32,384]{1,0:T(8,128)}, f32[4,768]{1,0:T(4,128)}, /*index=5*/f32[4,256]{1,0:T(4,128)}) custom-call(bf16[1024,1664]{1,0:T(8,128)(2,1)} %get-tuple-element.91.branch, bf16[1024,1664]{1,0:T(8,128)(2,1)} %get-tuple-element.98.code, ...), custom_call_target="tpu_custom_call" | custom-call | flops 62914560 | bytes 27152384 | tf_op jit(solution)/shard_map/pallas_call | solution.py:66
  347.3 0.0 reduce-scatter.8.cloned.1.call-done.in_grad
  347.3 2.0 shard_map.293
  349.3 38.9 %reduce-scatter.6.cloned.1.call-done = f32[192,768]{1,0:T(8,128)} async-done(((f32[1536,768]{1,0:T(8,128)}), f32[192,768]{1,0:T(8,128)}) %reduce-scatter.6.cloned.1.call-update) | async-done | bytes 589840 | tf_op jit(solution)/shard_map/reduce_scatter | solution.py:1504
  (1 shorter events, 0.0 us)
Async XLA Ops:
  7.2 327.5 %reduce-scatter.4.cloned.1.call-start = ((), (), s32[]{:S(2)}) async-start(), calls=%async_computation.3 | async-start | bytes 5308416 | tf_op jit(solution)/shard_map/reduce_scatter | solution.py:1618
  210.9 1.9 copy-start
  210.9 136.4 %reduce-scatter.8.cloned.1.call-start = ((), (), s32[]{:S(2)}) async-start(), calls=%async_computation.5 | async-start | bytes 6193152 | tf_op jit(solution)/shard_map/reduce_scatter | solution.py:1621
  211.7 176.5 %reduce-scatter.6.cloned.1.call-start = ((), (), s32[]{:S(2)}) async-start(), calls=%async_computation.4 | async-start | bytes 5308416 | tf_op jit(solution)/shard_map/reduce_scatter | solution.py:1504
  218.6 1.0 copy-start.2
  219.6 2.6 copy-start.1
Sparse Core Ops, SparseCore 0:
  211.0 57.2 reduce-scatter.3
  271.8 58.5 reduce-scatter.7
  334.4 53.7 reduce-scatter.5
